TPU v7x, 128 devices: a whole 4x4x4 slice. The times are simulated.
128 devices in a mesh: visit: 4 (over x), patch: 32 (over z, y, core).
Axes of the slice: x: 4, y: 4, z: 4, core: 2. Of those that a mesh axis runs over, the one named last changes fastest.
Arguments:
- image: float32 [4096, 128, 128], P(('visit', 'patch')), may hold values from -6 to 6
- variance: float32 [4096, 128, 128], P(('visit', 'patch')), may hold values from 0.25 to 4
- intersections: int32 [4096, 2], P(('visit', 'patch')), may hold values from 0 to 31, all different within a row; in each aligned block of 32 rows (0 to 31, 32 to 63, ...) at most 3 rows name the same one
- boxes: int32 [4096, 2, 2], P(('visit', 'patch')), may hold values from -64 to 191
- shifts: float32 [4096, 2, 2], P(('visit', 'patch')), may hold values from 0 to 1
- basis_ids: int32 [4096, 3], P(('visit', 'patch')), may hold values from 0 to 7
- coefs: float32 [4096, 3], P(('visit', 'patch')), may hold values from 0.3 to 1.5
- taps: float32 [8, 2, 41], replicated, may hold values from -1 to 1
Outputs:
- coadd: float32 [8192, 256], P('patch')
- coadd_var: float32 [8192, 256], P('patch')
Inputs may be any that keep to these rules, and one draw needn't show every extreme that they name: `intersections`: the rows of one device name every patch at most 3 times; each tile names two different patches.
All inputs are finite; a program needn't handle non-finite values.
Results may differ from a plain program's by a relative error of at most 0.0003.
Values sent between devices are 32-bit elements; how exact they have to be, the bound alone decides.
No kernel may reach another device: no remote copies, remote signals or barrier semaphores. Data moves between devices by JAX's collectives and lax.ppermute only.
A program may use at most 128 MiB of HBM per device.

v0:
```python
import jax
import jax.numpy as jnp
from jax import lax
from jax.sharding import PartitionSpec as P

PATCH = 256


HI = lax.Precision.HIGHEST
group_width = 8


def band_table(side, ntaps):
    offs = jnp.arange(side)[:, None] - jnp.arange(side)[None, :] + (ntaps - 1) // 2
    return (offs[:, :, None] == jnp.arange(ntaps)[None, None, :]).astype(jnp.float32)


def convolve(images, row_taps, col_taps, weights_b):
    band = band_table(images.shape[-1], row_taps.shape[-1])
    row_mats = jnp.einsum("ikt,gbt->gbik", band, row_taps, precision=HI)
    col_mats = jnp.einsum("jlt,gbt->gbjl", band, col_taps, precision=HI)
    partial_rows = jnp.einsum("gbik,gkl->gbil", row_mats, images, precision=HI)
    scaled = partial_rows * weights_b[:, :, None, None]
    return jnp.einsum("gbil,gbjl->gij", scaled, col_mats, precision=HI)


def interpolation(offset, shift, count, side):
    place = (
        jnp.arange(count).astype(jnp.float32)[None, :, None]
        - offset[:, None, None]
        - shift[:, None, None]
        - jnp.arange(side).astype(jnp.float32)[None, None, :]
    )
    return jnp.maximum(0.0, 1.0 - jnp.abs(place))


def warp_group(planes, meta, patch_side):
    side = planes.shape[-1]
    rows_w = interpolation(meta[:, 1], meta[:, 3], patch_side, side)
    cols_w = interpolation(meta[:, 2], meta[:, 4], patch_side, side)
    left = jnp.einsum("gpi,gcij->gcpj", rows_w, planes, precision=HI)
    both = jnp.einsum("gcpj,gqj->gcpq", left, cols_w, precision=HI)
    weight = meta[:, 0]
    num = jnp.sum(weight[:, None, None] * both[:, 0], 0)
    vsum = jnp.sum((weight * weight)[:, None, None] * both[:, 1], 0)
    cover = jnp.sum(rows_w, 2)[:, :, None] * jnp.sum(cols_w, 2)[:, None, :]
    den = jnp.sum(weight[:, None, None] * cover, 0)
    return jnp.stack([num, den, vsum], 0)


def finish(num, den, vsum):
    safe = jnp.maximum(den, 1.0)
    return (num / safe, vsum / (safe * safe))


def basis_taps(ids, taps):
    select = (ids[..., None] == jnp.arange(taps.shape[0])[None, None, :]).astype(jnp.float32)
    row_t = jnp.einsum("gbn,nk->gbk", select, taps[:, 0], precision=HI)
    col_t = jnp.einsum("gbn,nk->gbk", select, taps[:, 1], precision=HI)
    return (row_t, col_t)


def shards(image, variance, intersections, boxes, shifts, basis_ids, coefs, taps):
    tiles = image.shape[0]
    side = image.shape[1]
    nterms = coefs.shape[1]
    peers = lax.axis_size("patch")
    capacity = max(2, 3 * tiles // peers)
    slots = peers * capacity
    dest = intersections.reshape(-1)
    count = dest.shape[0]
    order = jnp.arange(count)
    earlier = (dest[:, None] == dest[None, :]) & (order[None, :] < order[:, None])
    rank = jnp.sum(earlier.astype(jnp.int32), 1)
    slot_of = dest * capacity + rank
    match = slot_of[None, :] == jnp.arange(slots)[:, None]
    live = jnp.any(match, 1)
    item = jnp.sum(jnp.where(match, order[None, :], 0), 1)
    tile_of = item // 2
    livef = live.astype(jnp.float32)
    inverse_var = 1.0 / jnp.mean(variance, axis=(1, 2))
    box_flat = boxes.reshape(count, 2).astype(jnp.float32)[item]
    shift_flat = shifts.reshape(count, 2)[item]
    geometry = jnp.concatenate([(inverse_var[tile_of] * livef)[:, None], box_flat, shift_flat], 1)
    planes = jnp.stack([image, variance], 1)[tile_of] * livef[:, None, None, None]
    meta = jnp.concatenate([geometry, coefs[tile_of], basis_ids[tile_of].astype(jnp.float32)], 1)
    width = meta.shape[1]
    sent = planes.reshape(peers, capacity, 2, side, side)
    sent_meta = meta.reshape(peers, capacity, width)
    arrived, arrived_meta = (
        lax.all_to_all(sent, "patch", split_axis=0, concat_axis=0, tiled=True),
        lax.all_to_all(sent_meta, "patch", split_axis=0, concat_axis=0, tiled=True),
    )
    groups = slots // group_width
    arrived = arrived.reshape(groups, group_width, 2, side, side)
    arrived_meta = arrived_meta.reshape(groups, group_width, width)

    def accumulate(total, parts):
        block, block_meta = parts
        ids = block_meta[:, 5 + nterms : 5 + 2 * nterms].astype(jnp.int32)
        row_t, col_t = basis_taps(ids, taps)
        matched = convolve(block[:, 0], row_t, col_t, block_meta[:, 5 : 5 + nterms])
        block = jnp.stack([matched, block[:, 1]], 1)
        return (total + warp_group(block, block_meta, PATCH), None)

    start = jnp.zeros((3, PATCH, PATCH), jnp.float32)
    partial_value = lax.scan(accumulate, start, (arrived, arrived_meta))[0]
    total = lax.psum(partial_value, "visit")
    coadd, coadd_var = finish(total[0], total[1], total[2])
    return (coadd, coadd_var)


def solution(mesh):
    in_specs = (
        P(("visit", "patch"), None, None),
        P(("visit", "patch"), None, None),
        P(("visit", "patch"), None),
        P(("visit", "patch"), None, None),
        P(("visit", "patch"), None, None),
        P(("visit", "patch"), None),
        P(("visit", "patch"), None),
        P(),
    )
    out_specs = (P("patch", None), P("patch", None))
    return jax.shard_map(shards, mesh=mesh, in_specs=in_specs, out_specs=out_specs, check_vma=False)
```

profile of v0, /device:TPU:0, one launch (start us, length us, event | category | flops | bytes accessed | tf_op | source)
XLA Modules:
  0.0 472.9 jit_solution(7930241180158183529)
XLA Ops:
  16.5 8.4 %all-to-all-start = ((f32[32,3,11]{2,1,0:T(4,128)}), f32[32,3,11]{2,1,0:T(4,128)S(1)}, u32[]{:S(2)}, u32[]{:S(2)}) async-start(f32[32,3,11]{2,1,0:T(4,128)} %copy.90), calls=%async_computation | async-start | bytes 131072 | tf_op jit(solution)/shard_map/all_to_all | solution.py:92
  24.9 3.9 pad_maximum_fusion.1
  28.9 10.9 %gather_fusion.5 = f32[96,2,128,128]{3,2,1,0:T(8,128)} fusion(f32[32,2,128,128]{3,2,0,1:T(8,128)} %pad_maximum_fusion.1, s32[1024]{0:T(1024)S(1)} %get-tuple-element.97), kind=kCustom, calls=%fused_computation.5 | custom fusion | bytes 25166208 | tf_op jit(solution)/shard_map/gather | solution.py:85
  39.9 11.8 %broadcast_multiply_fusion = f32[32,3,2,128,128]{4,3,2,1,0:T(8,128)} fusion(f32[32,3,2,128,128]{4,3,2,1,0:T(8,128)} %bitcast.135, f32[32,3]{1,0:T(8,128)S(1)} %reshape.285), kind=kLoop, calls=%fused_computation.74 | loop fusion | flops 3145728 | bytes 25166208 | tf_op jit(solution)/shard_map/mul | solution.py:85
  51.6 7.6 %all-to-all-start.1 = ((f32[32,3,2,128,128]{4,3,2,1,0:T(8,128)}), f32[32,3,2,128,128]{4,3,2,1,0:T(8,128)}, u32[]{:S(2)}, u32[]{:S(2)}) async-start(f32[32,3,2,128,128]{4,3,2,1,0:T(8,128)} %broadcast_multiply_fusion), calls=%async_computation.1 | async-start | bytes 25165824 | tf_op jit(solution)/shard_map/all_to_all | solution.py:91
  59.4 160.7 %all-to-all-done.1 = f32[32,3,2,128,128]{4,3,2,1,0:T(8,128)} async-done(((f32[32,3,2,128,128]{4,3,2,1,0:T(8,128)}), f32[32,3,2,128,128]{4,3,2,1,0:T(8,128)}, u32[]{:S(2)}, u32[]{:S(2)}) %all-to-all-start.1) | async-done | bytes 12582944 | tf_op jit(solution)/shard_map/all_to_all | solution.py:91
  220.1 202.3 %while.11 = (s32[]{:T(128)}, f32[3,256,256]{2,1,0:T(8,128)S(1)}, f32[12,8,11]{2,1,0:T(8,128)S(1)}, f32[8,2,41]{2,0,1:T(8,128)S(1)}, f32[12,8,2,128,128]{4,3,2,1,0:T(8,128)}, /*index=5*/s32[]{:T(128)}, s32[]{:T(128)}) while((s32[]{:T(128)}, f32[3,256,256]{2,1,0:T(8,128)S(1)}, f32[12,8,11]{2,1,0:T(8,128)S(1)}, ...), condition=%wide.region_10.11_spmd.clone, body=%wide.region_4.10_spmd.clone.sunk | while | flops 4022007040 | bytes 30721944 | solution.py:107
  226.2 2.3 fusion.96
  230.8 4.0 fusion.98
  243.1 2.3 fusion.96
  247.7 4.0 fusion.98
  264.5 4.0 fusion.98
  281.4 4.0 fusion.98
  293.7 2.3 fusion.96
  298.2 4.0 fusion.98
  315.1 4.0 fusion.98
  332.0 4.0 fusion.98
  348.8 4.0 fusion.98
  365.7 4.0 fusion.98
  382.5 4.0 fusion.98
  399.4 4.0 fusion.98
  411.7 2.3 fusion.96
  416.3 4.0 fusion.98
  423.3 40.8 %all-reduce.2.cloned.1.call-done = f32[3,256,256]{2,1,0:T(8,128)} async-done(((f32[3,256,256]{2,1,0:T(8,128)}), f32[3,256,256]{2,1,0:T(8,128)}) %all-reduce.2.cloned.1.call-update) | async-done | bytes 786448 | tf_op jit(solution)/shard_map/psum | solution.py:108
  (308 shorter events, 156.0 us)
Async XLA Ops:
  7.2 4.6 copy-start.6
  7.2 5.6 %copy-start.3 = (f32[32,2,2]{0,2,1:T(2,128)S(1)}, f32[32,2,2]{0,2,1:T(2,128)}, u32[]{:S(2)}) copy-start(f32[32,2,2]{0,2,1:T(2,128)} %param.14) | copy-start | bytes 1540
  7.2 6.5 %copy-start.4 = (f32[32,3]{0,1:T(4,128)S(1)}, f32[32,3]{0,1:T(4,128)}, u32[]{:S(2)}) copy-start(f32[32,3]{0,1:T(4,128)} %param.16) | copy-start | bytes 1156
  8.5 6.1 %copy-start.5 = (s32[32,3]{0,1:T(4,128)S(1)}, s32[32,3]{0,1:T(4,128)}, u32[]{:S(2)}) copy-start(s32[32,3]{0,1:T(4,128)} %param.15) | copy-start | bytes 1156
  10.4 14.5 %copy-start.1 = (f32[32,128,128]{2,1,0:T(8,128)S(1)}, f32[32,128,128]{2,1,0:T(8,128)}, u32[]{:S(2)}) copy-start(f32[32,128,128]{2,1,0:T(8,128)} %param.11) | copy-start | bytes 6291460
  16.5 35.1 %all-to-all-start = ((f32[32,3,11]{2,1,0:T(4,128)}), f32[32,3,11]{2,1,0:T(4,128)S(1)}, u32[]{:S(2)}, u32[]{:S(2)}) async-start(f32[32,3,11]{2,1,0:T(4,128)} %copy.90), calls=%async_computation | async-start | bytes 131072 | tf_op jit(solution)/shard_map/all_to_all | solution.py:92
  51.6 7.7 %copy-start.2 = (f32[8,2,41]{2,1,0:T(2,128)S(1)}, f32[8,2,41]{2,1,0:T(2,128)}, u32[]{:S(2)}) copy-start(f32[8,2,41]{2,1,0:T(2,128)} %param.17) | copy-start | bytes 7876
  51.6 168.5 %all-to-all-start.1 = ((f32[32,3,2,128,128]{4,3,2,1,0:T(8,128)}), f32[32,3,2,128,128]{4,3,2,1,0:T(8,128)}, u32[]{:S(2)}, u32[]{:S(2)}) async-start(f32[32,3,2,128,128]{4,3,2,1,0:T(8,128)} %broadcast_multiply_fusion), calls=%async_computation.1 | async-start | bytes 25165824 | tf_op jit(solution)/shard_map/all_to_all | solution.py:91
  59.3 404.8 %all-reduce.2.cloned.1.call-start = ((), (), s32[]{:S(2)}) async-start(), calls=%async_computation.2 | async-start | bytes 1572864 | tf_op jit(solution)/shard_map/psum | solution.py:108
  422.4 0.9 copy-start
Sparse Core Ops, SparseCore 0:
  423.5 40.6 all-reduce.1
where the time goes:
time: 474 us; the launch traced here: 473 us
  waiting for transfers between devices  202 us (43%)
  matrix products  153 us (32%)
  other arithmetic  47.6 us (10%)
  local copies, waits for them, and re-layouts  38.4 us (8%)
  starting transfers between devices  16.1 us (3%)
  between operations  14.3 us (3%)
    all_to_all x1, waiting for transfers between devices, shards(): lax.all_to_all(sent, 'patch', split_axis=0, concat_axis=0, tiled=True)  161 us
    dot_general x12, matrix products, warp_group(): both = jnp.einsum('gcpj,gqj->gcpq', left, cols_w, precision=HI)  47.7 us
    psum x1, waiting for transfers between devices, shards(): total = lax.psum(partial_value, 'visit')  40.8 us
    dot_general x12, matrix products, convolve(): return jnp.einsum('gbil,gbjl->gij', scaled, col_mats, precision=HI)  27.4 us
    dot_general x12, matrix products, warp_group(): left = jnp.einsum('gpi,gcij->gcpj', rows_w, planes, precision=HI)  26.9 us
    dot_general x12, matrix products, convolve(): partial_rows = jnp.einsum('gbik,gkl->gbil', row_mats, images, precision=HI)  20 us
    squeeze x24, local copies, waits for them, and re-layouts, shards(): partial_value = lax.scan(accumulate, start, (arrived, arrived_meta))[0]  15.7 us
    reduce_sum x12, other arithmetic, warp_group(): cover = jnp.sum(rows_w, 2)[:, :, None] * jnp.sum(cols_w, 2)[:, None, :]  15.5 us
  transfers between devices with their start and end apart: 3, of which 2 were waited for; matrix products, arithmetic and copies ran while one was open for 6% of the time, Pallas kernels for 0%

commit v1 on v0

v1 whole, which is shorter than its diff:
```python
import functools

import jax
import jax.numpy as jnp
from jax import lax
from jax.experimental import pallas as pl
from jax.experimental.pallas import tpu as pltpu
from jax.sharding import PartitionSpec as P

TS = 128
PATCH = 256
NB = 3
NBASIS = 8
HALF = 20
TILES = 32
ROUTES = 2 * TILES
CAP = 3
META = 24
PAD = 64
SLOTS = 256
F32 = jnp.float32
BF16 = jnp.bfloat16

BOX, SHIFT, IDS, COEF = ROUTES, 3 * ROUTES, 5 * ROUTES, 5 * ROUTES + NB * TILES


def split(x):
    high = x.astype(BF16)
    return high, (x - high.astype(F32)).astype(BF16)


def match_kernel(table, rows, cols, image, variance, out, row_mats, col_mats):
    i = lax.broadcasted_iota(jnp.int32, (TS, TS), 0)
    k = lax.broadcasted_iota(jnp.int32, (TS, TS), 1)
    near = jnp.abs(i - k) <= HALF
    for b in range(NBASIS):
        for source, target, axis in ((rows, row_mats, 0), (cols, col_mats, 1)):
            line = jnp.broadcast_to(source[b : b + 1, :], (TS, TS))
            band = jnp.where(near, pltpu.roll(line, 0, 1, stride=1, stride_axis=0), 0.0)
            target[b] = jnp.concatenate(split(band), axis)

    @pl.loop(0, TILES)
    def _(t):
        weight = float(TS * TS) / jnp.sum(variance[t], axis=(0, 1), keepdims=True)
        pixels = jnp.concatenate(split(image[t]), 1)
        total = None
        for j in range(NB):
            basis = table[IDS + NB * t + j].astype(jnp.int32)
            p = jnp.dot(row_mats[basis], pixels, preferred_element_type=F32)
            part = p[:TS, :TS] + (p[TS:, :TS] + p[:TS, TS:])
            part = jnp.concatenate(split(part * table[COEF + NB * t + j]), 0)
            p = jnp.dot(part, col_mats[basis], preferred_element_type=F32)
            p = p[:TS, :TS] + (p[TS:, :TS] + p[:TS, TS:])
            total = p if total is None else total + p
        out[t] = total * weight


def match(table, rows, cols, image, variance):
    vmem = pl.BlockSpec(memory_space=pltpu.VMEM)
    return pl.pallas_call(
        match_kernel,
        out_shape=jax.ShapeDtypeStruct((TILES, TS, TS), F32),
        in_specs=[pl.BlockSpec(memory_space=pltpu.SMEM)] + [vmem] * 4,
        out_specs=vmem,
        scratch_shapes=[pltpu.VMEM((NBASIS, 2 * TS, TS), BF16), pltpu.VMEM((NBASIS, TS, 2 * TS), BF16)],
        compiler_params=pltpu.CompilerParams(vmem_limit_bytes=40 << 20),
        cost_estimate=pl.CostEstimate(flops=8_000_000_000, bytes_accessed=6 << 20, transcendentals=0),
        name="match",
    )(table, rows, cols, image, variance)


def place(tile, row, col, frac_row, frac_col, scale, stage, acc):
    lane = lax.broadcasted_iota(jnp.int32, (1, TS), 1)
    turn = (col + TS) & (TS - 1)
    first = (col + TS) >> 7
    near, far = (1.0 - frac_col) * scale, frac_col * scale
    here = jnp.where(lane >= turn, near, 0.0)
    here_next = jnp.where(lane >= turn + 1, far, 0.0)
    over, over_next = near - here, far - here_next
    r0 = pltpu.roll(tile, turn, 1)
    r1 = pltpu.roll(r0, 1, 1)
    stage[0, 8 : 8 + TS, :] = r0 * here + r1 * here_next
    stage[1, 8 : 8 + TS, :] = r0 * over + r1 * over_next
    down = (row + PAD) & 7
    base = pl.multiple_of(((row + PAD) >> 3) * 8, 8)
    for side in range(2):
        upper = stage[side, pl.ds(8 - down, TS + 8), :]
        lower = stage[side, pl.ds(7 - down, TS + 8), :]
        acc[first + side, pl.ds(base, TS + 8), :] += upper * (1.0 - frac_row) + lower * frac_row


def geometry(table, item):
    return (
        table[BOX + 2 * item].astype(jnp.int32),
        table[BOX + 2 * item + 1].astype(jnp.int32),
        table[SHIFT + 2 * item],
        table[SHIFT + 2 * item + 1],
    )


def warp_kernel(with_meta, *refs):
    if with_meta:
        where_ref, own, other, own_tiles, other_tiles = refs[:5]
        left_keep, left_send, right_keep, right_send, slots = refs[5:10]
        stage, acc, weights, counts = refs[10:]
    else:
        slots, own, other, own_tiles, other_tiles = refs[:5]
        left_keep, left_send, right_keep, right_send = refs[5:9]
        stage, acc = refs[9:]
    lane = lax.broadcasted_iota(jnp.int32, (1, TS), 1)
    stage[:, 0:8, :] = jnp.zeros((2, 8, TS), F32)
    stage[:, 8 + TS :, :] = jnp.zeros((2, 8, TS), F32)

    if with_meta:
        mine, core, chip = where_ref[0], where_ref[1], where_ref[2]
        for side, table in ((0, own), (1, other)):
            for k in range(17):
                counts[k] = 0

            @pl.loop(0, ROUTES)
            def _(item, side=side, table=table):
                dest = table[item].astype(jnp.int32)
                z, y = dest >> 3, (dest >> 1) & 3
                z, y = z ^ (z >> 1), y ^ (y >> 1)
                code = ((z & 1) << 3) | ((z >> 1) << 2) | ((y & 1) << 1) | (y >> 1)
                k = jnp.where((dest & 1) == core, code ^ mine, 16)
                seen = counts[k]
                slots[SLOTS // 2 * side + 16 + k * CAP + seen] = item
                counts[k] = seen + 1

            for k in range(16):
                slots[SLOTS // 2 * side + k] = counts[k]

        for side, tiles in ((0, own_tiles), (1, other_tiles)):

            @pl.loop(0, TILES, step=8)
            def _(t, side=side, tiles=tiles):
                sums = jnp.concatenate([jnp.sum(tiles[t + u], axis=0, keepdims=True) for u in range(8)], 0)
                sums = jnp.sum(sums, axis=1, keepdims=True)
                at = pl.multiple_of(side * TILES + t, 8)
                weights[pl.ds(at, 8), :] = jnp.broadcast_to(float(TS * TS) / sums, (8, TS))

    @pl.loop(0, 16)
    def _(k):
        for side in (1, 2):
            acc[side, PAD : PAD + PATCH, :] = jnp.zeros((PATCH, TS), F32)
        if with_meta:
            acc[0, 384 : 384 + META, :] = jnp.zeros((META, TS), F32)
        for side, table, tiles in ((0, own, own_tiles), (1, other, other_tiles)):

            @pl.loop(0, slots[SLOTS // 2 * side + k])
            def _(n, side=side, table=table, tiles=tiles):
                item = slots[SLOTS // 2 * side + 16 + k * CAP + n]
                row, col, frac_row, frac_col = geometry(table, item)
                t = item >> 1
                if with_meta:
                    weight = weights[pl.ds(side * TILES + t, 1), :]
                    scale = weight * weight
                    field = lax.broadcasted_iota(jnp.int32, (8, TS), 0)
                    value = jnp.where(field == 1, row.astype(F32), weight)
                    value = jnp.where(field == 2, col.astype(F32), value)
                    value = jnp.where(field == 3, frac_row, value)
                    value = jnp.where(field == 4, frac_col, value)
                    value = jnp.where((field < 5) & (lane == 2 * chip + side), value, 0.0)
                    acc[0, pl.ds(pl.multiple_of(384 + 8 * n, 8), 8), :] += value
                else:
                    scale = 1.0
                place(tiles[t], row, col, frac_row, frac_col, scale, stage, acc)

        z_first, z_second, y_first, y_second = k >> 3, (k >> 2) & 1, (k >> 1) & 1, k & 1
        if not with_meta:
            z_first, z_second, y_first, y_second = z_second, z_first, y_second, y_first
        left = z_second * 4 + y_first * 2 + y_second
        right = y_second * 4 + z_first * 2 + z_second

        for gate, keep, send, index, side in (
            (z_first, left_keep, left_send, left, 1),
            (y_first, right_keep, right_send, right, 2),
        ):
            for value, target in ((0, keep), (1, send)):

                @pl.when(gate == value)
                def _(target=target, index=index, side=side):
                    target[index, 0:PATCH, :] = acc[side, PAD : PAD + PATCH, :]
                    if with_meta and side == 1:
                        target[index, PATCH : PATCH + META, :] = acc[0, 384 : 384 + META, :]


def warp(with_meta, first, own, other, own_tiles, other_tiles):
    smem, vmem = pl.BlockSpec(memory_space=pltpu.SMEM), pl.BlockSpec(memory_space=pltpu.VMEM)
    rows = PATCH + META if with_meta else PATCH
    left = jax.ShapeDtypeStruct((8, rows, TS), F32)
    right = jax.ShapeDtypeStruct((8, PATCH, TS), F32)
    outs, specs = [left, left, right, right], [vmem] * 4
    scratch = [pltpu.VMEM((2, TS + 16, TS), F32), pltpu.VMEM((4, 384 + META, TS), F32)]
    if with_meta:
        outs, specs = outs + [jax.ShapeDtypeStruct((SLOTS,), jnp.int32)], specs + [smem]
        scratch += [pltpu.VMEM((2 * TILES, TS), F32), pltpu.SMEM((17,), jnp.int32)]
    return pl.pallas_call(
        functools.partial(warp_kernel, with_meta),
        out_shape=outs,
        in_specs=[smem] * 3 + [vmem] * 2,
        out_specs=specs,
        scratch_shapes=scratch,
        compiler_params=pltpu.CompilerParams(vmem_limit_bytes=40 << 20),
        cost_estimate=pl.CostEstimate(flops=8_000_000_000, bytes_accessed=8 << 20, transcendentals=0),
        name="warp_meta" if with_meta else "warp",
    )(first, own, other, own_tiles, other_tiles)


def finish_kernel(num_left, num_right, var_left, var_right, coadd, coadd_var):
    place_of = lax.broadcasted_iota(jnp.int32, (PATCH, TS), 0).astype(F32)

    def cover(offset, shift):
        u = place_of - offset
        lower = jnp.where((u >= 0.0) & (u <= TS - 1.0), 1.0 - shift, 0.0)
        return lower + jnp.where((u >= 1.0) & (u <= float(TS)), shift, 0.0)

    den = jnp.zeros((PATCH, PATCH), F32)
    for slot in range(CAP):
        at = PATCH + 8 * slot
        weight, row, col, frac_row, frac_col = (var_left[at + f : at + f + 1, :] for f in range(5))
        down, across = cover(row, frac_row) * weight, cover(col, frac_col)
        den += lax.dot_general(
            down, across, (((1,), (1,)), ((), ())), precision=lax.Precision.HIGHEST, preferred_element_type=F32
        )
    safe = jnp.maximum(den, 1.0)
    for num, var, lo in ((num_left, var_left, 0), (num_right, var_right, TS)):
        part = safe[:, lo : lo + TS]
        coadd[:, lo : lo + TS] = num[0:PATCH, :] / part
        coadd_var[:, lo : lo + TS] = var[0:PATCH, :] / (part * part)


def finish(num_left, num_right, var_left, var_right):
    vmem = pl.BlockSpec(memory_space=pltpu.VMEM)
    return pl.pallas_call(
        finish_kernel,
        out_shape=[jax.ShapeDtypeStruct((PATCH, PATCH), F32)] * 2,
        in_specs=[vmem] * 4,
        out_specs=[vmem] * 2,
        name="finish",
    )(num_left, num_right, var_left, var_right)


EDGES = (((0, 1), (1, 0), (2, 3), (3, 2)), ((1, 2), (2, 1), (3, 0), (0, 3)))


def over_patch(axis, edge):
    pairs = []
    for a, b in EDGES[edge]:
        for other in range(4):
            for core in range(2):
                src, dst = ((a, other), (b, other)) if axis == "z" else ((other, a), (other, b))
                pairs.append((src[0] * 8 + src[1] * 2 + core, dst[0] * 8 + dst[1] * 2 + core))
    return pairs


def halve(keep, send, order):
    for step, (axis, edge) in enumerate(order):
        got = lax.ppermute(send, "patch", over_patch(axis, edge))
        n = keep.shape[0] // 2
        if step == len(order) - 1:
            return keep[0] + got[0]
        send, keep = keep[n:] + got[n:], keep[:n] + got[:n]


def double(x, first):
    for edge in (first, 1 - first):
        x = x + lax.ppermute(x, "visit", EDGES[edge])
    return x


def shards(image, variance, intersections, boxes, shifts, basis_ids, coefs, taps):
    swap = [(i, i ^ 1) for i in range(32)]
    other_variance = lax.ppermute(variance, "patch", swap)
    table = jnp.concatenate(
        [
            intersections.reshape(-1).astype(F32),
            boxes.reshape(-1).astype(F32),
            shifts.reshape(-1),
            basis_ids.reshape(-1).astype(F32),
            coefs.reshape(-1),
        ]
    )
    other_table = lax.ppermute(table, "patch", swap)
    flat = taps[:, :, ::-1]
    gap = jnp.zeros((NBASIS, TS - 2 * HALF - 1), F32)
    rows = jnp.concatenate([flat[:, 0, HALF:], gap, flat[:, 0, :HALF]], 1)
    cols = jnp.concatenate([taps[:, 1, HALF:], gap, taps[:, 1, :HALF]], 1)
    matched = match(table, rows, cols, image, variance)
    other_matched = lax.ppermute(matched, "patch", swap)

    patch = lax.axis_index("patch")
    z, y = patch >> 3, (patch >> 1) & 3
    chip = lax.axis_index("visit") * 16 + z * 4 + y
    z, y = z ^ (z >> 1), y ^ (y >> 1)
    mine = ((z & 1) << 3) | ((z >> 1) << 2) | ((y & 1) << 1) | (y >> 1)
    where = jnp.stack([mine, patch & 1, chip])

    var_left_keep, var_left_send, var_right_keep, var_right_send, slots = warp(
        True, where, table, other_table, variance, other_variance
    )
    num_left_keep, num_left_send, num_right_keep, num_right_send = warp(
        False, slots, table, other_table, matched, other_matched
    )
    z1, z2, y1, y2 = ("z", 0), ("z", 1), ("y", 0), ("y", 1)
    var_left = double(halve(var_left_keep, var_left_send, (z1, z2, y1, y2)), 0)
    var_right = double(halve(var_right_keep, var_right_send, (y1, y2, z1, z2)), 1)
    num_left = double(halve(num_left_keep, num_left_send, (z2, z1, y2, y1)), 0)
    num_right = double(halve(num_right_keep, num_right_send, (y2, y1, z2, z1)), 1)
    return tuple(finish(num_left, num_right, var_left, var_right))


def solution(mesh):
    split_spec = ("visit", "patch")
    in_specs = (
        P(split_spec, None, None),
        P(split_spec, None, None),
        P(split_spec, None),
        P(split_spec, None, None),
        P(split_spec, None, None),
        P(split_spec, None),
        P(split_spec, None),
        P(),
    )
    out_specs = (P("patch", None), P("patch", None))
    return jax.shard_map(shards, mesh=mesh, in_specs=in_specs, out_specs=out_specs, check_vma=False)
```

time: 474 us -> 158 us (0.33)
  matrix products: 153 us -> 0 us
  waiting for transfers between devices: 202 us -> 50.8 us
  Pallas kernels: 0 us -> 58.6 us
  other arithmetic: 47.6 us -> 6.08 us
  local copies, waits for them, and re-layouts: 38.4 us -> 7.62 us
  starting transfers between devices: 16.1 us -> 34.2 us
  between operations: 14.3 us -> 0.77 us
    all_to_all x2 -> x0, waiting for transfers between devices: 161 us -> none  [the longest x1 161 us: shards(): lax.all_to_all(sent, 'patch', split_axis=0, concat_axis=0, tiled=True)]
    dot_general x96 -> x0, matrix products: 153 us -> none  [the longest x12 47.7 us: warp_group(): both = jnp.einsum('gcpj,gqj->gcpq', left, cols_w, precision=HI)]
    pallas_call x0 -> x4, Pallas kernels: none -> 58.6 us  [the longest x2 37.5 us: warp(): pl.pallas_call(functools.partial(warp_kernel, with_meta), out_shape=outs,...]
    ppermute x0 -> x27, waiting for transfers between devices: none -> 50.8 us  [the longest x16 40.9 us: halve(): got = lax.ppermute(send, 'patch', over_patch(axis, edge))]
    psum x1 -> x0, waiting for transfers between devices: 40.8 us -> none  [shards(): total = lax.psum(partial_value, 'visit')]
    ppermute x0 -> x27, starting transfers between devices: none -> 34.2 us  [the longest x16 22.4 us: halve(): got = lax.ppermute(send, 'patch', over_patch(axis, edge))]
    reduce_sum x27 -> x0, other arithmetic: 24.8 us -> none  [the longest x12 15.5 us: warp_group(): cover = jnp.sum(rows_w, 2)[:, :, None] * jnp.sum(cols_w, 2)[:, None, :]]
    all_to_all x2 -> x0, starting transfers between devices: 16.1 us -> none  [the longest x1 8.42 us: shards(): lax.all_to_all(sent_meta, 'patch', split_axis=0, concat_axis=0, tiled=True)]
  transfers between devices with their start and end apart: 3 -> 27, of which waited for: 2 -> 14; matrix products, arithmetic and copies ran while one was open for 6% -> 6% of each run, Pallas kernels for 0% -> 35%
where the time goes in v1:
time: 158 us
  Pallas kernels  58.6 us (37%)
  waiting for transfers between devices  50.8 us (32%)
  starting transfers between devices  34.2 us (22%)
  local copies, waits for them, and re-layouts  7.62 us (5%)
  other arithmetic  6.08 us (4%)
    ppermute x16, waiting for transfers between devices, halve(): got = lax.ppermute(send, 'patch', over_patch(axis, edge))  40.9 us
    pallas_call x2, Pallas kernels, warp(): pl.pallas_call(functools.partial(warp_kernel, with_meta), out_shape=outs,...  37.5 us
    ppermute x16, starting transfers between devices, halve(): got = lax.ppermute(send, 'patch', over_patch(axis, edge))  22.4 us
    pallas_call x1, Pallas kernels, match(): pl.pallas_call(match_kernel, out_shape=jax.ShapeDtypeStruct((TILES, TS, T...  18.3 us
    ppermute x8, starting transfers between devices, double(): x = x + lax.ppermute(x, 'visit', EDGES[edge])  11.2 us
    ppermute x8, waiting for transfers between devices, double(): x = x + lax.ppermute(x, 'visit', EDGES[edge])  6.35 us
    unnamed x8, local copies, waits for them, and re-layouts  4.74 us
    ppermute x1, waiting for transfers between devices, shards(): other_table = lax.ppermute(table, 'patch', swap)  3.57 us
  transfers between devices with their start and end apart: 27, of which 14 were waited for; matrix products, arithmetic and copies ran while one was open for 6% of the time, Pallas kernels for 35%

profile of v1, /device:TPU:0, one launch (start us, length us, event | category | flops | bytes accessed | tf_op | source)
XLA Modules:
  0.0 158.0 jit_solution(11276121553505687742)
XLA Ops:
  10.5 18.3 %match.1.refs_3_ = f32[32,128,128]{2,1,0:T(8,128)} custom-call(f32[512]{0:T(512)S(1)} %concatenate.9.refs_1_.table, f32[8,128]{1,0:T(8,128)S(1)} %get-tuple-element.41.rows, f32[8,128]{1,0:T(8,128)S(1)} %get-tuple-element.40.cols, f32[32,128,128]{2,1,0:T(8,128)S(1)} %copy-done, f32[32,128,128]{2,1,0:T(8,128)S(1)} %copy-done.1), custom_call_target="tpu_custom_call" | custom-call | flops 8000000000 | bytes 6291456 | tf_op jit(solution)/shard_map/match/pallas_call | solution.py:60
  29.4 3.6 %collective-permute-done.refs_2_ = f32[512]{0:T(512)S(1)} collective-permute-done((f32[512]{0:T(512)S(1)}, f32[512]{0:T(512)S(1)}, u32[]{:S(2)}, u32[]{:S(2)}) %collective-permute-start) | collective-permute-done | bytes 2080 | tf_op jit(solution)/shard_map/ppermute | solution.py:285
  32.9 20.7 %warp_meta.1 = (f32[8,280,128]{2,1,0:T(8,128)S(1)}, f32[8,280,128]{2,1,0:T(8,128)S(1)}, f32[8,256,128]{2,1,0:T(8,128)S(1)}, f32[8,256,128]{2,1,0:T(8,128)S(1)}, s32[256]{0:T(256)S(1)}) custom-call(s32[3]{0:T(128)S(1)} %pad_add_fusion.refs_0_, f32[512]{0:T(512)S(1)} %concatenate.9.refs_1_.table, f32[512]{0:T(512)S(1)} %collective-permute-done.refs_2_, ...), custom_call_target="tpu_custom_call" | custom-call | flops 8000000000 | bytes 8388608 | tf_op jit(solution)/shard_map/warp_meta/pallas_call | solution.py:199
  53.6 1.7 %collective-permute-start.21 = (f32[8,256,128]{2,1,0:T(8,128)S(1)}, f32[8,256,128]{2,1,0:T(8,128)S(1)}, u32[]{:S(2)}, u32[]{:S(2)}) collective-permute-start(f32[8,256,128]{2,1,0:T(8,128)S(1)} %get-tuple-element.19), channel_id=1, source_target_pairs={{0,2},{1,3},{8,10},{9,11},{16,18},{17,19},{24,26},{25,27},{2,0},{3... | collective-permute-start | bytes 3145736 | tf_op jit(solution)/shard_map/ppermute | solution.py:260
  55.4 16.8 %warp.1 = (f32[8,256,128]{2,1,0:T(8,128)S(1)}, f32[8,256,128]{2,1,0:T(8,128)S(1)}, f32[8,256,128]{2,1,0:T(8,128)S(1)}, f32[8,256,128]{2,1,0:T(8,128)S(1)}) custom-call(s32[256]{0:T(256)S(1)} %get-tuple-element.11.refs_0_, f32[512]{0:T(512)S(1)} %concatenate.9.refs_1_.table, f32[512]{0:T(512)S(1)} %collective-permute-done.refs_2_, ...), custom_call_target="tpu_custom_call" | custom-call | flops 8000000000 | bytes 8388608 | tf_op jit(solution)/shard_map/warp/pallas_call | solution.py:199
  72.2 2.3 %collective-permute-start.9 = (f32[8,256,128]{2,1,0:T(8,128)S(1)}, f32[8,256,128]{2,1,0:T(8,128)S(1)}, u32[]{:S(2)}, u32[]{:S(2)}) collective-permute-start(f32[8,256,128]{2,1,0:T(8,128)S(1)} %get-tuple-element.15), channel_id=1, source_target_pairs={{2,4},{3,5},{10,12},{11,13},{18,20},{19,21},{26,28},{27,29},{4,2},... | collective-permute-start | bytes 3145736 | tf_op jit(solution)/shard_map/ppermute | solution.py:260
  74.4 4.0 %collective-permute-start.3 = (f32[8,256,128]{2,1,0:T(8,128)S(1)}, f32[8,256,128]{2,1,0:T(8,128)S(1)}, u32[]{:S(2)}, u32[]{:S(2)}) collective-permute-start(f32[8,256,128]{2,1,0:T(8,128)S(1)} %get-tuple-element.13), channel_id=1, source_target_pairs={{8,16},{9,17},{10,18},{11,19},{12,20},{13,21},{14,22},{15,23},{16,... | collective-permute-start | bytes 3145736 | tf_op jit(solution)/shard_map/ppermute | solution.py:260
  79.1 3.2 %collective-permute-start.22 = (f32[4,256,128]{2,1,0:T(8,128)S(1)}, f32[4,256,128]{2,1,0:T(8,128)S(1)}, u32[]{:S(2)}, u32[]{:S(2)}) collective-permute-start(f32[4,256,128]{2,1,0:T(8,128)S(1)} %get-tuple-element.23), channel_id=1, source_target_pairs={{2,4},{3,5},{10,12},{11,13},{18,20},{19,21},{26,28},{27,29},{4,2},... | collective-permute-start | bytes 1572872 | tf_op jit(solution)/shard_map/ppermute | solution.py:260
  82.2 17.3 %collective-permute-done.9 = f32[8,256,128]{2,1,0:T(8,128)S(1)} collective-permute-done((f32[8,256,128]{2,1,0:T(8,128)S(1)}, f32[8,256,128]{2,1,0:T(8,128)S(1)}, u32[]{:S(2)}, u32[]{:S(2)}) %collective-permute-start.9) | collective-permute-done | bytes 1048608 | tf_op jit(solution)/shard_map/ppermute | solution.py:260
  102.0 4.7 %collective-permute-done.15 = f32[8,280,128]{2,1,0:T(8,128)S(1)} collective-permute-done((f32[8,280,128]{2,1,0:T(8,128)S(1)}, f32[8,280,128]{2,1,0:T(8,128)S(1)}, u32[]{:S(2)}, u32[]{:S(2)}) %collective-permute-start.15) | collective-permute-done | bytes 1146912 | tf_op jit(solution)/shard_map/ppermute | solution.py:260
  107.0 2.7 %collective-permute-done.22 = f32[4,256,128]{2,1,0:T(8,128)S(1)} collective-permute-done((f32[4,256,128]{2,1,0:T(8,128)S(1)}, f32[4,256,128]{2,1,0:T(8,128)S(1)}, u32[]{:S(2)}, u32[]{:S(2)}) %collective-permute-start.22) | collective-permute-done | bytes 524320 | tf_op jit(solution)/shard_map/ppermute | solution.py:260
  109.7 2.0 %collective-permute-start.23 = (f32[2,256,128]{2,1,0:T(8,128)S(1)}, f32[2,256,128]{2,1,0:T(8,128)S(1)}, u32[]{:S(2)}, u32[]{:S(2)}) collective-permute-start(f32[2,256,128]{2,1,0:T(8,128)S(1)} %get-tuple-element.31), channel_id=1, source_target_pairs={{0,8},{1,9},{2,10},{3,11},{4,12},{5,13},{6,14},{7,15},{8,0},{9,1},... | collective-permute-start | bytes 786440 | tf_op jit(solution)/shard_map/ppermute | solution.py:260
  111.8 3.9 %collective-permute-start.11 = (f32[2,256,128]{2,1,0:T(8,128)S(1)}, f32[2,256,128]{2,1,0:T(8,128)S(1)}, u32[]{:S(2)}, u32[]{:S(2)}) collective-permute-start(f32[2,256,128]{2,1,0:T(8,128)S(1)} %get-tuple-element.33), channel_id=1, source_target_pairs={{8,16},{9,17},{10,18},{11,19},{12,20},{13,21},{14,22},{15,23},{16,... | collective-permute-start | bytes 786440 | tf_op jit(solution)/shard_map/ppermute | solution.py:260
  115.7 2.2 %collective-permute-done.4 = f32[4,256,128]{2,1,0:T(8,128)S(1)} collective-permute-done((f32[4,256,128]{2,1,0:T(8,128)S(1)}, f32[4,256,128]{2,1,0:T(8,128)S(1)}, u32[]{:S(2)}, u32[]{:S(2)}) %collective-permute-start.4) | collective-permute-done | bytes 524320 | tf_op jit(solution)/shard_map/ppermute | solution.py:260
  119.1 3.4 %collective-permute-done.16 = f32[4,280,128]{2,1,0:T(8,128)S(1)} collective-permute-done((f32[4,280,128]{2,1,0:T(8,128)S(1)}, f32[4,280,128]{2,1,0:T(8,128)S(1)}, u32[]{:S(2)}, u32[]{:S(2)}) %collective-permute-start.16) | collective-permute-done | bytes 573472 | tf_op jit(solution)/shard_map/ppermute | solution.py:260
  124.0 2.5 %collective-permute-done.11 = f32[2,256,128]{2,1,0:T(8,128)S(1)} collective-permute-done((f32[2,256,128]{2,1,0:T(8,128)S(1)}, f32[2,256,128]{2,1,0:T(8,128)S(1)}, u32[]{:S(2)}, u32[]{:S(2)}) %collective-permute-start.11) | collective-permute-done | bytes 262176 | tf_op jit(solution)/shard_map/ppermute | solution.py:260
  127.4 2.2 %collective-permute-done.24 = f32[1,256,128]{2,1,0:T(8,128)S(1)} collective-permute-done((f32[1,256,128]{2,1,0:T(8,128)S(1)}, f32[1,256,128]{2,1,0:T(8,128)S(1)}, u32[]{:S(2)}, u32[]{:S(2)}) %collective-permute-start.24) | collective-permute-done | bytes 131104 | tf_op jit(solution)/shard_map/ppermute | solution.py:260
  129.7 2.2 %collective-permute-start.25 = (f32[256,128]{1,0:T(8,128)S(1)}, f32[256,128]{1,0:T(8,128)S(1)}, u32[]{:S(2)}, u32[]{:S(2)}) collective-permute-start(f32[256,128]{1,0:T(8,128)S(1)} %fusion.3), channel_id=1, source_target_pairs={{32,64},{64,32},{96,0},{0,96},{33,65},{65,33},{97,1},{1,97},{34,66... | collective-permute-start | bytes 393224 | tf_op jit(solution)/shard_map/ppermute | solution.py:269
  134.5 3.8 %collective-permute-done.18 = f32[1,280,128]{2,1,0:T(8,128)S(1)} collective-permute-done((f32[1,280,128]{2,1,0:T(8,128)S(1)}, f32[1,280,128]{2,1,0:T(8,128)S(1)}, u32[]{:S(2)}, u32[]{:S(2)}) %collective-permute-start.18) | collective-permute-done | bytes 143392 | tf_op jit(solution)/shard_map/ppermute | solution.py:260
  138.6 1.9 %collective-permute-start.7 = (f32[256,128]{1,0:T(8,128)S(1)}, f32[256,128]{1,0:T(8,128)S(1)}, u32[]{:S(2)}, u32[]{:S(2)}) collective-permute-start(f32[256,128]{1,0:T(8,128)S(1)} %fusion.7), channel_id=1, source_target_pairs={{0,32},{32,0},{64,96},{96,64},{1,33},{33,1},{65,97},{97,65},{2,34}... | collective-permute-start | bytes 393224 | tf_op jit(solution)/shard_map/ppermute | solution.py:269
  140.5 4.5 %collective-permute-done.19 = f32[280,128]{1,0:T(8,128)S(1)} collective-permute-done((f32[280,128]{1,0:T(8,128)S(1)}, f32[280,128]{1,0:T(8,128)S(1)}, u32[]{:S(2)}, u32[]{:S(2)}) %collective-permute-start.19) | collective-permute-done | bytes 143392 | tf_op jit(solution)/shard_map/ppermute | solution.py:269
  145.4 1.8 %collective-permute-start.26 = (f32[256,128]{1,0:T(8,128)S(1)}, f32[256,128]{1,0:T(8,128)S(1)}, u32[]{:S(2)}, u32[]{:S(2)}) collective-permute-start(f32[256,128]{1,0:T(8,128)S(1)} %add.166), channel_id=1, source_target_pairs={{0,32},{32,0},{64,96},{96,64},{1,33},{33,1},{65,97},{97,65},{2,34}... | collective-permute-start | bytes 393224 | tf_op jit(solution)/shard_map/ppermute | solution.py:269
  147.6 3.1 %collective-permute-start.8 = (f32[256,128]{1,0:T(8,128)S(1)}, f32[256,128]{1,0:T(8,128)S(1)}, u32[]{:S(2)}, u32[]{:S(2)}) collective-permute-start(f32[256,128]{1,0:T(8,128)S(1)} %add.136), channel_id=1, source_target_pairs={{32,64},{64,32},{96,0},{0,96},{33,65},{65,33},{97,1},{1,97},{34,66... | collective-permute-start | bytes 393224 | tf_op jit(solution)/shard_map/ppermute | solution.py:269
  155.2 2.8 %finish.1 = (f32[256,256]{1,0:T(8,128)}, f32[256,256]{1,0:T(8,128)}) custom-call(f32[256,128]{1,0:T(8,128)} %add.137.num_left, f32[256,128]{1,0:T(8,128)} %add.147.num_right, f32[280,128]{1,0:T(8,128)} %add.157.var_left, f32[256,128]{1,0:T(8,128)} %add.167.var_right), custom_call_target="tpu_custom_call" | custom-call | tf_op jit(solution)/shard_map/finish/pallas_call | solution.py:236
  (86 shorter events, 25.7 us)
Async XLA Ops:
  0.6 32.3 %collective-permute-start.1 = (f32[32,128,128]{2,1,0:T(8,128)}, f32[32,128,128]{2,1,0:T(8,128)}, u32[]{:S(2)}, u32[]{:S(2)}) collective-permute-start(f32[32,128,128]{2,1,0:T(8,128)} %variance.1), channel_id=1, source_target_pairs={{0,1},{1,0},{2,3},{3,2},{4,5},{5,4},{6,7},{7,6},{8,9},{9,8},{10,11... | collective-permute-start | bytes 6291464 | tf_op jit(solution)/shard_map/ppermute | solution.py:275
  28.8 26.6 %collective-permute-start.2 = (f32[32,128,128]{2,1,0:T(8,128)}, f32[32,128,128]{2,1,0:T(8,128)}, u32[]{:S(2)}, u32[]{:S(2)}) collective-permute-start(f32[32,128,128]{2,1,0:T(8,128)} %match.1.refs_3_), channel_id=1, source_target_pairs={{0,1},{1,0},{2,3},{3,2},{4,5},{5,4},{6,7},{7,6},{8,9},{9,8},{10,11... | collective-permute-start | bytes 6291464 | tf_op jit(solution)/shard_map/ppermute | solution.py:291
  53.6 25.3 %collective-permute-start.21 = (f32[8,256,128]{2,1,0:T(8,128)S(1)}, f32[8,256,128]{2,1,0:T(8,128)S(1)}, u32[]{:S(2)}, u32[]{:S(2)}) collective-permute-start(f32[8,256,128]{2,1,0:T(8,128)S(1)} %get-tuple-element.19), channel_id=1, source_target_pairs={{0,2},{1,3},{8,10},{9,11},{16,18},{17,19},{24,26},{25,27},{2,0},{3... | collective-permute-start | bytes 3145736 | tf_op jit(solution)/shard_map/ppermute | solution.py:260
  72.2 27.3 %collective-permute-start.9 = (f32[8,256,128]{2,1,0:T(8,128)S(1)}, f32[8,256,128]{2,1,0:T(8,128)S(1)}, u32[]{:S(2)}, u32[]{:S(2)}) collective-permute-start(f32[8,256,128]{2,1,0:T(8,128)S(1)} %get-tuple-element.15), channel_id=1, source_target_pairs={{2,4},{3,5},{10,12},{11,13},{18,20},{19,21},{26,28},{27,29},{4,2},... | collective-permute-start | bytes 3145736 | tf_op jit(solution)/shard_map/ppermute | solution.py:260
  74.4 26.9 %collective-permute-start.3 = (f32[8,256,128]{2,1,0:T(8,128)S(1)}, f32[8,256,128]{2,1,0:T(8,128)S(1)}, u32[]{:S(2)}, u32[]{:S(2)}) collective-permute-start(f32[8,256,128]{2,1,0:T(8,128)S(1)} %get-tuple-element.13), channel_id=1, source_target_pairs={{8,16},{9,17},{10,18},{11,19},{12,20},{13,21},{14,22},{15,23},{16,... | collective-permute-start | bytes 3145736 | tf_op jit(solution)/shard_map/ppermute | solution.py:260
  78.5 28.2 %collective-permute-start.15 = (f32[8,280,128]{2,1,0:T(8,128)S(1)}, f32[8,280,128]{2,1,0:T(8,128)S(1)}, u32[]{:S(2)}, u32[]{:S(2)}) collective-permute-start(f32[8,280,128]{2,1,0:T(8,128)S(1)} %get-tuple-element.17), channel_id=1, source_target_pairs={{0,8},{1,9},{2,10},{3,11},{4,12},{5,13},{6,14},{7,15},{8,0},{9,1},... | collective-permute-start | bytes 3440648 | tf_op jit(solution)/shard_map/ppermute | solution.py:260
  79.1 30.6 %collective-permute-start.22 = (f32[4,256,128]{2,1,0:T(8,128)S(1)}, f32[4,256,128]{2,1,0:T(8,128)S(1)}, u32[]{:S(2)}, u32[]{:S(2)}) collective-permute-start(f32[4,256,128]{2,1,0:T(8,128)S(1)} %get-tuple-element.23), channel_id=1, source_target_pairs={{2,4},{3,5},{10,12},{11,13},{18,20},{19,21},{26,28},{27,29},{4,2},... | collective-permute-start | bytes 1572872 | tf_op jit(solution)/shard_map/ppermute | solution.py:260
  99.7 12.0 %collective-permute-start.10 = (f32[4,256,128]{2,1,0:T(8,128)S(1)}, f32[4,256,128]{2,1,0:T(8,128)S(1)}, u32[]{:S(2)}, u32[]{:S(2)}) collective-permute-start(f32[4,256,128]{2,1,0:T(8,128)S(1)} %get-tuple-element.25), channel_id=1, source_target_pairs={{0,2},{1,3},{8,10},{9,11},{16,18},{17,19},{24,26},{25,27},{2,0},{3... | collective-permute-start | bytes 1572872 | tf_op jit(solution)/shard_map/ppermute | solution.py:260
  101.6 16.4 %collective-permute-start.4 = (f32[4,256,128]{2,1,0:T(8,128)S(1)}, f32[4,256,128]{2,1,0:T(8,128)S(1)}, u32[]{:S(2)}, u32[]{:S(2)}) collective-permute-start(f32[4,256,128]{2,1,0:T(8,128)S(1)} %get-tuple-element.27), channel_id=1, source_target_pairs={{0,8},{1,9},{2,10},{3,11},{4,12},{5,13},{6,14},{7,15},{8,0},{9,1},... | collective-permute-start | bytes 1572872 | tf_op jit(solution)/shard_map/ppermute | solution.py:260
  106.9 15.7 %collective-permute-start.16 = (f32[4,280,128]{2,1,0:T(8,128)S(1)}, f32[4,280,128]{2,1,0:T(8,128)S(1)}, u32[]{:S(2)}, u32[]{:S(2)}) collective-permute-start(f32[4,280,128]{2,1,0:T(8,128)S(1)} %get-tuple-element.21), channel_id=1, source_target_pairs={{8,16},{9,17},{10,18},{11,19},{12,20},{13,21},{14,22},{15,23},{16,... | collective-permute-start | bytes 1720328 | tf_op jit(solution)/shard_map/ppermute | solution.py:260
  109.7 13.6 %collective-permute-start.23 = (f32[2,256,128]{2,1,0:T(8,128)S(1)}, f32[2,256,128]{2,1,0:T(8,128)S(1)}, u32[]{:S(2)}, u32[]{:S(2)}) collective-permute-start(f32[2,256,128]{2,1,0:T(8,128)S(1)} %get-tuple-element.31), channel_id=1, source_target_pairs={{0,8},{1,9},{2,10},{3,11},{4,12},{5,13},{6,14},{7,15},{8,0},{9,1},... | collective-permute-start | bytes 786440 | tf_op jit(solution)/shard_map/ppermute | solution.py:260
  111.8 14.7 %collective-permute-start.11 = (f32[2,256,128]{2,1,0:T(8,128)S(1)}, f32[2,256,128]{2,1,0:T(8,128)S(1)}, u32[]{:S(2)}, u32[]{:S(2)}) collective-permute-start(f32[2,256,128]{2,1,0:T(8,128)S(1)} %get-tuple-element.33), channel_id=1, source_target_pairs={{8,16},{9,17},{10,18},{11,19},{12,20},{13,21},{14,22},{15,23},{16,... | collective-permute-start | bytes 786440 | tf_op jit(solution)/shard_map/ppermute | solution.py:260
  118.0 8.6 %collective-permute-start.5 = (f32[2,256,128]{2,1,0:T(8,128)S(1)}, f32[2,256,128]{2,1,0:T(8,128)S(1)}, u32[]{:S(2)}, u32[]{:S(2)}) collective-permute-start(f32[2,256,128]{2,1,0:T(8,128)S(1)} %get-tuple-element.35), channel_id=1, source_target_pairs={{2,4},{3,5},{10,12},{11,13},{18,20},{19,21},{26,28},{27,29},{4,2},... | collective-permute-start | bytes 786440 | tf_op jit(solution)/shard_map/ppermute | solution.py:260
  122.6 9.3 %collective-permute-start.17 = (f32[2,280,128]{2,1,0:T(8,128)S(1)}, f32[2,280,128]{2,1,0:T(8,128)S(1)}, u32[]{:S(2)}, u32[]{:S(2)}) collective-permute-start(f32[2,280,128]{2,1,0:T(8,128)S(1)} %get-tuple-element.29), channel_id=1, source_target_pairs={{0,2},{1,3},{8,10},{9,11},{16,18},{17,19},{24,26},{25,27},{2,0},{3... | collective-permute-start | bytes 860168 | tf_op jit(solution)/shard_map/ppermute | solution.py:260
  123.4 6.3 %collective-permute-start.24 = (f32[1,256,128]{2,1,0:T(8,128)S(1)}, f32[1,256,128]{2,1,0:T(8,128)S(1)}, u32[]{:S(2)}, u32[]{:S(2)}) collective-permute-start(f32[1,256,128]{2,1,0:T(8,128)S(1)} %slice_add_fusion.18), channel_id=1, source_target_pairs={{8,16},{9,17},{10,18},{11,19},{12,20},{13,21},{14,22},{15,23},{16,... | collective-permute-start | bytes 393224 | tf_op jit(solution)/shard_map/ppermute | solution.py:260
  126.5 6.7 %collective-permute-start.12 = (f32[1,256,128]{2,1,0:T(8,128)S(1)}, f32[1,256,128]{2,1,0:T(8,128)S(1)}, u32[]{:S(2)}, u32[]{:S(2)}) collective-permute-start(f32[1,256,128]{2,1,0:T(8,128)S(1)} %slice_add_fusion.20), channel_id=1, source_target_pairs={{0,8},{1,9},{2,10},{3,11},{4,12},{5,13},{6,14},{7,15},{8,0},{9,1},... | collective-permute-start | bytes 393224 | tf_op jit(solution)/shard_map/ppermute | solution.py:260
  126.6 12.0 %collective-permute-start.6 = (f32[1,256,128]{2,1,0:T(8,128)S(1)}, f32[1,256,128]{2,1,0:T(8,128)S(1)}, u32[]{:S(2)}, u32[]{:S(2)}) collective-permute-start(f32[1,256,128]{2,1,0:T(8,128)S(1)} %slice_add_fusion.22), channel_id=1, source_target_pairs={{0,2},{1,3},{8,10},{9,11},{16,18},{17,19},{24,26},{25,27},{2,0},{3... | collective-permute-start | bytes 393224 | tf_op jit(solution)/shard_map/ppermute | solution.py:260
  129.7 15.7 %collective-permute-start.25 = (f32[256,128]{1,0:T(8,128)S(1)}, f32[256,128]{1,0:T(8,128)S(1)}, u32[]{:S(2)}, u32[]{:S(2)}) collective-permute-start(f32[256,128]{1,0:T(8,128)S(1)} %fusion.3), channel_id=1, source_target_pairs={{32,64},{64,32},{96,0},{0,96},{33,65},{65,33},{97,1},{1,97},{34,66... | collective-permute-start | bytes 393224 | tf_op jit(solution)/shard_map/ppermute | solution.py:269
  131.9 6.4 %collective-permute-start.18 = (f32[1,280,128]{2,1,0:T(8,128)S(1)}, f32[1,280,128]{2,1,0:T(8,128)S(1)}, u32[]{:S(2)}, u32[]{:S(2)}) collective-permute-start(f32[1,280,128]{2,1,0:T(8,128)S(1)} %slice_add_fusion.16), channel_id=1, source_target_pairs={{2,4},{3,5},{10,12},{11,13},{18,20},{19,21},{26,28},{27,29},{4,2},... | collective-permute-start | bytes 430088 | tf_op jit(solution)/shard_map/ppermute | solution.py:260
  133.2 13.9 %collective-permute-start.13 = (f32[256,128]{1,0:T(8,128)S(1)}, f32[256,128]{1,0:T(8,128)S(1)}, u32[]{:S(2)}, u32[]{:S(2)}) collective-permute-start(f32[256,128]{1,0:T(8,128)S(1)} %fusion.5), channel_id=1, source_target_pairs={{32,64},{64,32},{96,0},{0,96},{33,65},{65,33},{97,1},{1,97},{34,66... | collective-permute-start | bytes 393224 | tf_op jit(solution)/shard_map/ppermute | solution.py:269
  138.3 6.7 %collective-permute-start.19 = (f32[280,128]{1,0:T(8,128)S(1)}, f32[280,128]{1,0:T(8,128)S(1)}, u32[]{:S(2)}, u32[]{:S(2)}) collective-permute-start(f32[280,128]{1,0:T(8,128)S(1)} %fusion.1), channel_id=1, source_target_pairs={{0,32},{32,0},{64,96},{96,64},{1,33},{33,1},{65,97},{97,65},{2,34}... | collective-permute-start | bytes 430088 | tf_op jit(solution)/shard_map/ppermute | solution.py:269
  138.6 9.0 %collective-permute-start.7 = (f32[256,128]{1,0:T(8,128)S(1)}, f32[256,128]{1,0:T(8,128)S(1)}, u32[]{:S(2)}, u32[]{:S(2)}) collective-permute-start(f32[256,128]{1,0:T(8,128)S(1)} %fusion.7), channel_id=1, source_target_pairs={{0,32},{32,0},{64,96},{96,64},{1,33},{33,1},{65,97},{97,65},{2,34}... | collective-permute-start | bytes 393224 | tf_op jit(solution)/shard_map/ppermute | solution.py:269
  145.0 9.5 %collective-permute-start.20 = (f32[280,128]{1,0:T(8,128)S(1)}, f32[280,128]{1,0:T(8,128)S(1)}, u32[]{:S(2)}, u32[]{:S(2)}) collective-permute-start(f32[280,128]{1,0:T(8,128)S(1)} %add.156), channel_id=1, source_target_pairs={{32,64},{64,32},{96,0},{0,96},{33,65},{65,33},{97,1},{1,97},{34,66... | collective-permute-start | bytes 430088 | tf_op jit(solution)/shard_map/ppermute | solution.py:269
  147.6 6.3 %collective-permute-start.8 = (f32[256,128]{1,0:T(8,128)S(1)}, f32[256,128]{1,0:T(8,128)S(1)}, u32[]{:S(2)}, u32[]{:S(2)}) collective-permute-start(f32[256,128]{1,0:T(8,128)S(1)} %add.136), channel_id=1, source_target_pairs={{32,64},{64,32},{96,0},{0,96},{33,65},{65,33},{97,1},{1,97},{34,66... | collective-permute-start | bytes 393224 | tf_op jit(solution)/shard_map/ppermute | solution.py:269
  (6 other events, 39.6 us)

commit v2 on v1

v2 whole, which is shorter than its diff:
```python
import functools

import jax
import jax.numpy as jnp
from jax import lax
from jax.experimental import pallas as pl
from jax.experimental.pallas import tpu as pltpu
from jax.sharding import PartitionSpec as P

TS = 128
PATCH = 256
NB = 3
NBASIS = 8
HALF = 20
TILES = 32
ROUTES = 2 * TILES
CAP = 3
META = 24
PAD = 64
SLOTS = 256
F32 = jnp.float32
BF16 = jnp.bfloat16

IDS, COEF = 10, 13
EMPTY = 1 << 24
UNROLL = 4
MATCH_UNROLL = 4
MATCH_COST = WARP_COST = 10_000_000_000


def split(x):
    high = x.astype(BF16)
    return high, (x - high.astype(F32)).astype(BF16)


def pack_kernel(mine, intersections, boxes, shifts, basis_ids, coefs, out):
    out[...] = jnp.zeros_like(out)
    z, y, core = intersections[...] >> 3, (intersections[...] >> 1) & 3, intersections[...] & 1
    z, y = z ^ (z >> 1), y ^ (y >> 1)
    code = ((z & 1) << 3) | ((z >> 1) << 2) | ((y & 1) << 1) | (y >> 1)
    out[0:2, 0:TILES] = ((code ^ mine[0]) + 16 * core).astype(F32)
    for route in range(2):
        out[2 + 2 * route : 4 + 2 * route, 0:TILES] = boxes[route].astype(F32)
        out[6 + 2 * route : 8 + 2 * route, 0:TILES] = shifts[route]
    out[IDS : IDS + NB, 0:TILES] = basis_ids[...].astype(F32)
    out[COEF : COEF + NB, 0:TILES] = coefs[...]


def pack(mine, intersections, boxes, shifts, basis_ids, coefs):
    vmem = pl.BlockSpec(memory_space=pltpu.VMEM)
    return pl.pallas_call(
        pack_kernel,
        out_shape=jax.ShapeDtypeStruct((16, TS), F32),
        in_specs=[pl.BlockSpec(memory_space=pltpu.SMEM)] + [vmem] * 5,
        out_specs=vmem,
        name="pack",
    )(mine, intersections.T, boxes.transpose(1, 2, 0), shifts.transpose(1, 2, 0), basis_ids.T, coefs.T)


def match_kernel(table, taps, image, variance, out, line, row_mats, col_mats):
    i = lax.broadcasted_iota(jnp.int32, (TS, TS), 0)
    k = lax.broadcasted_iota(jnp.int32, (TS, TS), 1)
    near = jnp.abs(i - k) <= HALF
    line[...] = jnp.zeros_like(line)
    for b in range(NBASIS):
        line[2 * b : 2 * b + 2, 0 : 2 * HALF + 1] = taps[b]
    line[...] = pltpu.roll(line[...], TS - HALF, 1)
    for b in range(NBASIS):
        for side, target, axis in ((0, row_mats, 0), (1, col_mats, 1)):
            band = jnp.broadcast_to(line[2 * b + side : 2 * b + side + 1, :], (TS, TS))
            band = pltpu.roll(band, 0, 1, stride=1, stride_axis=0)
            band = jnp.where(near, band, 0.0)
            target[b] = jnp.concatenate(split(band.T if side == 0 else band), axis)

    def total(p):
        return p[:TS, :TS] + (p[TS:, :TS] + p[:TS, TS:])

    @pl.loop(0, TILES, step=MATCH_UNROLL)
    def _(first):
        for t in [first + u for u in range(MATCH_UNROLL)]:
            weight = float(TS * TS) / jnp.sum(variance[t], axis=(0, 1), keepdims=True)
            pixels = jnp.concatenate(split(image[t]), 1)
            parts, bands = [], []
            for j in range(NB):
                basis = table[IDS + j, t].astype(jnp.int32)
                p = total(jnp.dot(row_mats[basis], pixels, preferred_element_type=F32))
                parts.append(jnp.concatenate(split(p * table[COEF + j, t]), 0))
                bands.append(col_mats[basis])
            p = jnp.dot(jnp.concatenate(parts[:2], 1), jnp.concatenate(bands[:2], 0), preferred_element_type=F32)
            p = p + jnp.dot(parts[2], bands[2], preferred_element_type=F32)
            out[t] = total(p) * weight


def match(table, taps, image, variance):
    vmem = pl.BlockSpec(memory_space=pltpu.VMEM)
    return pl.pallas_call(
        match_kernel,
        out_shape=jax.ShapeDtypeStruct((TILES, TS, TS), F32),
        in_specs=[pl.BlockSpec(memory_space=pltpu.SMEM)] + [vmem] * 3,
        out_specs=vmem,
        scratch_shapes=[
            pltpu.VMEM((2 * NBASIS, TS), F32),
            pltpu.VMEM((NBASIS, 2 * TS, TS), BF16),
            pltpu.VMEM((NBASIS, TS, 2 * TS), BF16),
        ],
        compiler_params=pltpu.CompilerParams(vmem_limit_bytes=40 << 20),
        cost_estimate=pl.CostEstimate(flops=MATCH_COST, bytes_accessed=6 << 20, transcendentals=0),
        name="match",
    )(table, taps, image, variance)


def warp_kernel(with_meta, *refs):
    first, own, other, own_tiles, other_tiles = refs[:5]
    outs = refs[5:9]
    if with_meta:
        slots = refs[9]
        stage, acc, tiles, sems, both, meta, weights, counts = refs[10:]
    else:
        slots = first
        stage, acc, tiles, sems = refs[9:]
    copies = [
        pltpu.make_async_copy(source, tiles.at[pl.ds(TILES * i, TILES)], sems.at[i])
        for i, source in enumerate((own_tiles, other_tiles))
    ]
    for copy in copies:
        copy.start()
    lane = lax.broadcasted_iota(jnp.int32, (8, TS), 1)
    stage[:, :, 0:8, :] = jnp.zeros((UNROLL, 2, 8, TS), F32)
    stage[:, :, 8 + TS :, :] = jnp.zeros((UNROLL, 2, 8, TS), F32)
    for k in range(16):
        for side in (1, 2):
            acc[4 * k + side, PAD : PAD + PATCH, :] = jnp.zeros((PATCH, TS), F32)

    if with_meta:
        core, chip = first[1], first[2]
        meta[...] = jnp.zeros_like(meta)
        for side in range(2):
            for k in range(17):
                counts[side, k] = 0

        for route in range(2):

            @pl.loop(0, TILES)
            def _(t, route=route):
                for side, table in ((0, own), (1, other)):
                    k = table[route, t].astype(jnp.int32) - 16 * core
                    k = jnp.where((k >= 0) & (k < 16), k, 16)
                    seen = counts[side, k]
                    both[side, k * CAP + seen] = 2 * t + route
                    counts[side, k] = seen + 1

        n = jnp.int32(0)
        for k in range(16):
            for side in range(2):

                def add(m, n, side=side, k=k):
                    slots[1 + n] = both[side, k * CAP + m] + ((k << 16) + (side << 8)) + (m << 12)
                    return n + 1

                n = lax.fori_loop(0, counts[side, k], add, n)
        slots[0] = n
        for u in range(UNROLL):
            slots[1 + n + u] = EMPTY

    for copy in copies:
        copy.wait()

    if with_meta:

        @pl.loop(0, 2 * TILES, step=8)
        def _(t):
            sums = jnp.concatenate([jnp.sum(tiles[t + u], axis=0, keepdims=True) for u in range(8)], 0)
            sums = jnp.sum(sums, axis=1, keepdims=True)
            weights[pl.ds(pl.multiple_of(t, 8), 8), :] = jnp.broadcast_to(float(TS * TS) / sums, (8, TS))

    def place(entry, u):
        item, side, slot, k = entry & 255, (entry >> 8) & 1, (entry >> 12) & 3, (entry >> 16) & 15
        t, route = item >> 1, item & 1

        def scalar(row):
            return jnp.where(side == 0, own[row + 2 * route, t], other[row + 2 * route, t])

        row, col = scalar(2).astype(jnp.int32), scalar(3).astype(jnp.int32)
        frac_row, frac_col = scalar(6), scalar(7)
        real = jnp.where(entry >= EMPTY, 0.0, 1.0)
        at = side * TILES + t
        near, far = jnp.full((8, TS), (1.0 - frac_col) * real), jnp.full((8, TS), frac_col * real)
        if with_meta:
            weight = jnp.broadcast_to(weights[pl.ds(at, 1), :], (8, TS))
            field = lax.broadcasted_iota(jnp.int32, (8, TS), 0)
            value = jnp.where(field == 1, row.astype(F32), weight)
            value = jnp.where(field == 2, col.astype(F32), value)
            value = jnp.where(field == 3, frac_row, value)
            value = jnp.where(field == 4, frac_col, value)
            value = jnp.where((field < 5) & (lane == 2 * chip + side), value * real, 0.0)
            meta[k * CAP + slot] += value
            near, far = near * (weight * weight), far * (weight * weight)
        turn = (col + TS) & (TS - 1)
        here = jnp.where(lane >= turn, near, 0.0)
        here_next = jnp.where(lane >= turn + 1, far, 0.0)
        over, over_next = near - here, far - here_next
        tile = tiles[at]
        r0 = pltpu.roll(tile, turn, 1).reshape(TS // 8, 8, TS)
        r1 = pltpu.roll(tile, (turn + 1) & (TS - 1), 1).reshape(TS // 8, 8, TS)
        stage[u, 0, 8 : 8 + TS, :] = (r0 * here + r1 * here_next).reshape(TS, TS)
        stage[u, 1, 8 : 8 + TS, :] = (r0 * over + r1 * over_next).reshape(TS, TS)
        return 4 * k + ((col + TS) >> 7), row + PAD, frac_row

    def add_rows(u, first, row, frac_row):
        down = row & 7
        base = pl.multiple_of((row >> 3) * 8, 8)
        for side in range(2):
            upper = stage[u, side, pl.ds(8 - down, TS + 8), :]
            lower = stage[u, side, pl.ds(7 - down, TS + 8), :]
            acc[first + side, pl.ds(base, TS + 8), :] += upper * (1.0 - frac_row) + lower * frac_row

    @pl.loop(0, (slots[0] + UNROLL - 1) // UNROLL)
    def _(m):
        placed = [place(slots[1 + m * UNROLL + u], u) for u in range(UNROLL)]
        for u in range(UNROLL):
            add_rows(u, *placed[u])

    for k in range(16):
        z_first, z_second, y_first, y_second = k >> 3, (k >> 2) & 1, (k >> 1) & 1, k & 1
        if not with_meta:
            z_first, z_second, y_first, y_second = z_second, z_first, y_second, y_first
        left, right = outs[z_first], outs[2 + y_first]
        at = z_second * 4 + y_first * 2 + y_second
        left[at, 0:PATCH, :] = acc[4 * k + 1, PAD : PAD + PATCH, :]
        if with_meta:
            for slot in range(CAP):
                left[at, PATCH + 8 * slot : PATCH + 8 * slot + 8, :] = meta[k * CAP + slot]
        right[y_second * 4 + z_first * 2 + z_second, :, :] = acc[4 * k + 2, PAD : PAD + PATCH, :]


def warp(with_meta, first, own, other, own_tiles, other_tiles):
    smem, vmem = pl.BlockSpec(memory_space=pltpu.SMEM), pl.BlockSpec(memory_space=pltpu.VMEM)
    anywhere = pl.BlockSpec(memory_space=pl.ANY)
    rows = PATCH + META if with_meta else PATCH
    left = jax.ShapeDtypeStruct((8, rows, TS), F32)
    right = jax.ShapeDtypeStruct((8, PATCH, TS), F32)
    outs, specs = [left, left, right, right], [vmem] * 4
    scratch = [
        pltpu.VMEM((UNROLL, 2, TS + 16, TS), F32),
        pltpu.VMEM((64, 384, TS), F32),
        pltpu.VMEM((2 * TILES, TS, TS), F32),
        pltpu.SemaphoreType.DMA((2,)),
    ]
    if with_meta:
        outs, specs = outs + [jax.ShapeDtypeStruct((SLOTS,), jnp.int32)], specs + [smem]
        scratch += [
            pltpu.SMEM((2, 16 * CAP + ROUTES + 1), jnp.int32),
            pltpu.VMEM((16 * CAP, 8, TS), F32),
            pltpu.VMEM((2 * TILES, TS), F32),
            pltpu.SMEM((2, 17), jnp.int32),
        ]
    return pl.pallas_call(
        functools.partial(warp_kernel, with_meta),
        out_shape=outs,
        in_specs=[smem] * 3 + [anywhere] * 2,
        out_specs=specs,
        scratch_shapes=scratch,
        compiler_params=pltpu.CompilerParams(vmem_limit_bytes=40 << 20),
        cost_estimate=pl.CostEstimate(flops=WARP_COST, bytes_accessed=8 << 20, transcendentals=0),
        name="warp_meta" if with_meta else "warp",
    )(first, own, other, own_tiles, other_tiles)


def finish_kernel(num_left, num_right, var_left, var_right, coadd, coadd_var):
    place_of = lax.broadcasted_iota(jnp.int32, (PATCH, TS), 0).astype(F32)

    def cover(offset, shift):
        u = place_of - offset
        lower = jnp.where((u >= 0.0) & (u <= TS - 1.0), 1.0 - shift, 0.0)
        return lower + jnp.where((u >= 1.0) & (u <= float(TS)), shift, 0.0)

    den = jnp.zeros((PATCH, PATCH), F32)
    for slot in range(CAP):
        at = PATCH + 8 * slot
        weight, row, col, frac_row, frac_col = (var_left[at + f : at + f + 1, :] for f in range(5))
        down, across = cover(row, frac_row) * weight, cover(col, frac_col)
        den += lax.dot_general(
            down, across, (((1,), (1,)), ((), ())), precision=lax.Precision.HIGHEST, preferred_element_type=F32
        )
    safe = jnp.maximum(den, 1.0)
    for num, var, lo in ((num_left, var_left, 0), (num_right, var_right, TS)):
        part = safe[:, lo : lo + TS]
        coadd[:, lo : lo + TS] = num[0:PATCH, :] / part
        coadd_var[:, lo : lo + TS] = var[0:PATCH, :] / (part * part)


def finish(num_left, num_right, var_left, var_right):
    vmem = pl.BlockSpec(memory_space=pltpu.VMEM)
    return pl.pallas_call(
        finish_kernel,
        out_shape=[jax.ShapeDtypeStruct((PATCH, PATCH), F32)] * 2,
        in_specs=[vmem] * 4,
        out_specs=[vmem] * 2,
        name="finish",
    )(num_left, num_right, var_left, var_right)


EDGES = (((0, 1), (1, 0), (2, 3), (3, 2)), ((1, 2), (2, 1), (3, 0), (0, 3)))


def over_patch(axis, edge):
    pairs = []
    for a, b in EDGES[edge]:
        for other in range(4):
            for core in range(2):
                src, dst = ((a, other), (b, other)) if axis == "z" else ((other, a), (other, b))
                pairs.append((src[0] * 8 + src[1] * 2 + core, dst[0] * 8 + dst[1] * 2 + core))
    return pairs


def halve(keep, send, order):
    for step, (axis, edge) in enumerate(order):
        got = lax.ppermute(send, "patch", over_patch(axis, edge))
        n = keep.shape[0] // 2
        if step == len(order) - 1:
            return keep[0] + got[0]
        send, keep = keep[n:] + got[n:], keep[:n] + got[:n]


def double(x, first):
    for edge in (first, 1 - first):
        x = x + lax.ppermute(x, "visit", EDGES[edge])
    return x


def shards(image, variance, intersections, boxes, shifts, basis_ids, coefs, taps):
    swap = [(i, i ^ 1) for i in range(32)]
    patch = lax.axis_index("patch")
    z, y = patch >> 3, (patch >> 1) & 3
    chip = lax.axis_index("visit") * 16 + z * 4 + y
    z, y = z ^ (z >> 1), y ^ (y >> 1)
    mine = ((z & 1) << 3) | ((z >> 1) << 2) | ((y & 1) << 1) | (y >> 1)
    where = jnp.stack([mine, patch & 1, chip])

    other_variance = lax.ppermute(variance, "patch", swap)
    table = pack(where, intersections, boxes, shifts, basis_ids, coefs)
    other_table = lax.ppermute(table, "patch", swap)
    matched = match(table, taps, image, variance)
    other_matched = lax.ppermute(matched, "patch", swap)
    var_left_keep, var_left_send, var_right_keep, var_right_send, slots = warp(
        True, where, table, other_table, variance, other_variance
    )
    num_left_keep, num_left_send, num_right_keep, num_right_send = warp(
        False, slots, table, other_table, matched, other_matched
    )
    z1, z2, y1, y2 = ("z", 0), ("z", 1), ("y", 0), ("y", 1)
    var_left = double(halve(var_left_keep, var_left_send, (z1, z2, y1, y2)), 0)
    var_right = double(halve(var_right_keep, var_right_send, (y1, y2, z1, z2)), 1)
    num_left = double(halve(num_left_keep, num_left_send, (z2, z1, y2, y1)), 0)
    num_right = double(halve(num_right_keep, num_right_send, (y2, y1, z2, z1)), 1)
    return tuple(finish(num_left, num_right, var_left, var_right))


def solution(mesh):
    split_spec = ("visit", "patch")
    in_specs = (
        P(split_spec, None, None),
        P(split_spec, None, None),
        P(split_spec, None),
        P(split_spec, None, None),
        P(split_spec, None, None),
        P(split_spec, None),
        P(split_spec, None),
        P(),
    )
    out_specs = (P("patch", None), P("patch", None))
    return jax.shard_map(shards, mesh=mesh, in_specs=in_specs, out_specs=out_specs, check_vma=False)
```

time: 158 us -> 133 us (0.84)
  Pallas kernels: 58.6 us -> 35.8 us
  local copies, waits for them, and re-layouts: 7.62 us -> 4.58 us
  waiting for transfers between devices: 50.8 us -> 53.3 us
  other arithmetic: 6.08 us -> 4.38 us
    pallas_call x2, Pallas kernels: 37.5 us -> 19.4 us  [warp(): pl.pallas_call(functools.partial(warp_kernel, with_meta), out_shape=outs,...]
    pallas_call x1, Pallas kernels: 18.3 us -> 12.2 us  [match(): pl.pallas_call(match_kernel, out_shape=jax.ShapeDtypeStruct((TILES, TS, T...]
    convert_element_type x3 -> x0, other arithmetic: 2.06 us -> none  [the longest x1 0.69 us: shards(): basis_ids.reshape(-1).astype(F32)]
    slice x4 -> x0, local copies, waits for them, and re-layouts: 1.84 us -> none  [the longest x2 1.7 us: shards(): cols = jnp.concatenate([taps[:, 1, HALF:], gap, taps[:, 1, :HALF]], 1)]
    ppermute x16, waiting for transfers between devices: 40.9 us -> 42.6 us  [halve(): got = lax.ppermute(send, 'patch', over_patch(axis, edge))]
    unnamed x8 -> x14, local copies, waits for them, and re-layouts: 4.74 us -> 4.58 us
  transfers between devices with their start and end apart: 27 -> 27, of which waited for: 14 -> 15; matrix products, arithmetic and copies ran while one was open for 6% -> 3% of each run, Pallas kernels for 35% -> 25%
where the time goes in v2:
time: 133 us; the launch traced here: 132 us
  waiting for transfers between devices  53.3 us (40%)
  Pallas kernels  35.8 us (27%)
  starting transfers between devices  33.6 us (25%)
  local copies, waits for them, and re-layouts  4.58 us (3%)
  other arithmetic  4.38 us (3%)
    ppermute x16, waiting for transfers between devices, halve(): got = lax.ppermute(send, 'patch', over_patch(axis, edge))  42.6 us
    ppermute x16, starting transfers between devices, halve(): got = lax.ppermute(send, 'patch', over_patch(axis, edge))  22.2 us
    pallas_call x2, Pallas kernels, warp(): pl.pallas_call(functools.partial(warp_kernel, with_meta), out_shape=outs,...  19.4 us
    pallas_call x1, Pallas kernels, match(): pl.pallas_call(match_kernel, out_shape=jax.ShapeDtypeStruct((TILES, TS, T...  12.2 us
    ppermute x8, starting transfers between devices, double(): x = x + lax.ppermute(x, 'visit', EDGES[edge])  10.7 us
    ppermute x8, waiting for transfers between devices, double(): x = x + lax.ppermute(x, 'visit', EDGES[edge])  6.94 us
    unnamed x14, local copies, waits for them, and re-layouts  4.58 us
    ppermute x1, waiting for transfers between devices, shards(): other_table = lax.ppermute(table, 'patch', swap)  3.71 us
  transfers between devices with their start and end apart: 27, of which 15 were waited for; matrix products, arithmetic and copies ran while one was open for 3% of the time, Pallas kernels for 25%

profile of v2, /device:TPU:0, one launch (start us, length us, event | category | flops | bytes accessed | tf_op | source)
XLA Modules:
  0.0 132.5 jit_solution(6760244832416709093)
XLA Ops:
  7.3 12.2 %match.1.refs_3_ = f32[32,128,128]{2,1,0:T(8,128)S(1)} custom-call(f32[16,128]{1,0:T(8,128)S(1)} %copy-done, f32[8,2,41]{2,1,0:T(2,128)S(1)} %copy-done.6, f32[32,128,128]{2,1,0:T(8,128)S(1)} %copy-done.3, f32[32,128,128]{2,1,0:T(8,128)S(1)} %copy-done.4), custom_call_target="tpu_custom_call" | custom-call | flops 10000000000 | bytes 6291456 | tf_op jit(solution)/shard_map/match/pallas_call | solution.py:96
  20.2 3.7 %collective-permute-done.refs_2_ = f32[16,128]{1,0:T(8,128)S(1)} collective-permute-done((f32[16,128]{1,0:T(8,128)S(1)}, f32[16,128]{1,0:T(8,128)S(1)}, u32[]{:S(2)}, u32[]{:S(2)}) %collective-permute-start) | collective-permute-done | bytes 8224 | tf_op jit(solution)/shard_map/ppermute | solution.py:342
  23.9 11.5 %warp_meta.1 = (f32[8,280,128]{2,1,0:T(8,128)S(1)}, f32[8,280,128]{2,1,0:T(8,128)S(1)}, f32[8,256,128]{2,1,0:T(8,128)S(1)}, f32[8,256,128]{2,1,0:T(8,128)S(1)}, s32[256]{0:T(256)S(1)}) custom-call(s32[3]{0:T(128)S(1)} %copy-done.2, f32[16,128]{1,0:T(8,128)S(1)} %copy-done.1, f32[16,128]{1,0:T(8,128)S(1)} %collective-permute-done.refs_2_, ...), custom_call_target="tpu_custom_call" | custom-call | flops 10000000000 | bytes 8388608 | tf_op jit(solution)/shard_map/warp_meta/pallas_call | solution.py:257
  37.1 7.9 %warp.1 = (f32[8,256,128]{2,1,0:T(8,128)S(1)}, f32[8,256,128]{2,1,0:T(8,128)S(1)}, f32[8,256,128]{2,1,0:T(8,128)S(1)}, f32[8,256,128]{2,1,0:T(8,128)S(1)}) custom-call(s32[256]{0:T(256)S(1)} %get-tuple-element.11.refs_0_, f32[16,128]{1,0:T(8,128)S(1)} %copy-done.1, f32[16,128]{1,0:T(8,128)S(1)} %collective-permute-done.refs_2_, ...), custom_call_target="tpu_custom_call" | custom-call | flops 10000000000 | bytes 8388608 | tf_op jit(solution)/shard_map/warp/pallas_call | solution.py:257
  45.1 2.2 %collective-permute-start.9 = (f32[8,256,128]{2,1,0:T(8,128)S(1)}, f32[8,256,128]{2,1,0:T(8,128)S(1)}, u32[]{:S(2)}, u32[]{:S(2)}) collective-permute-start(f32[8,256,128]{2,1,0:T(8,128)S(1)} %get-tuple-element.15), channel_id=1, source_target_pairs={{2,4},{3,5},{10,12},{11,13},{18,20},{19,21},{26,28},{27,29},{4,2},... | collective-permute-start | bytes 3145736 | tf_op jit(solution)/shard_map/ppermute | solution.py:318
  47.3 4.0 %collective-permute-start.3 = (f32[8,256,128]{2,1,0:T(8,128)S(1)}, f32[8,256,128]{2,1,0:T(8,128)S(1)}, u32[]{:S(2)}, u32[]{:S(2)}) collective-permute-start(f32[8,256,128]{2,1,0:T(8,128)S(1)} %get-tuple-element.13), channel_id=1, source_target_pairs={{8,16},{9,17},{10,18},{11,19},{12,20},{13,21},{14,22},{15,23},{16,... | collective-permute-start | bytes 3145736 | tf_op jit(solution)/shard_map/ppermute | solution.py:318
  51.3 9.6 %collective-permute-done.21 = f32[8,256,128]{2,1,0:T(8,128)S(1)} collective-permute-done((f32[8,256,128]{2,1,0:T(8,128)S(1)}, f32[8,256,128]{2,1,0:T(8,128)S(1)}, u32[]{:S(2)}, u32[]{:S(2)}) %collective-permute-start.21) | collective-permute-done | bytes 1048608 | tf_op jit(solution)/shard_map/ppermute | solution.py:318
  61.0 3.2 %collective-permute-start.22 = (f32[4,256,128]{2,1,0:T(8,128)S(1)}, f32[4,256,128]{2,1,0:T(8,128)S(1)}, u32[]{:S(2)}, u32[]{:S(2)}) collective-permute-start(f32[4,256,128]{2,1,0:T(8,128)S(1)} %get-tuple-element.23), channel_id=1, source_target_pairs={{2,4},{3,5},{10,12},{11,13},{18,20},{19,21},{26,28},{27,29},{4,2},... | collective-permute-start | bytes 1572872 | tf_op jit(solution)/shard_map/ppermute | solution.py:318
  64.2 8.2 %collective-permute-done.9 = f32[8,256,128]{2,1,0:T(8,128)S(1)} collective-permute-done((f32[8,256,128]{2,1,0:T(8,128)S(1)}, f32[8,256,128]{2,1,0:T(8,128)S(1)}, u32[]{:S(2)}, u32[]{:S(2)}) %collective-permute-start.9) | collective-permute-done | bytes 1048608 | tf_op jit(solution)/shard_map/ppermute | solution.py:318
  72.6 2.2 %collective-permute-done.3 = f32[8,256,128]{2,1,0:T(8,128)S(1)} collective-permute-done((f32[8,256,128]{2,1,0:T(8,128)S(1)}, f32[8,256,128]{2,1,0:T(8,128)S(1)}, u32[]{:S(2)}, u32[]{:S(2)}) %collective-permute-start.3) | collective-permute-done | bytes 1048608 | tf_op jit(solution)/shard_map/ppermute | solution.py:318
  75.1 4.3 %collective-permute-done.15 = f32[8,280,128]{2,1,0:T(8,128)S(1)} collective-permute-done((f32[8,280,128]{2,1,0:T(8,128)S(1)}, f32[8,280,128]{2,1,0:T(8,128)S(1)}, u32[]{:S(2)}, u32[]{:S(2)}) %collective-permute-start.15) | collective-permute-done | bytes 1146912 | tf_op jit(solution)/shard_map/ppermute | solution.py:318
  79.6 3.1 %collective-permute-done.22 = f32[4,256,128]{2,1,0:T(8,128)S(1)} collective-permute-done((f32[4,256,128]{2,1,0:T(8,128)S(1)}, f32[4,256,128]{2,1,0:T(8,128)S(1)}, u32[]{:S(2)}, u32[]{:S(2)}) %collective-permute-start.22) | collective-permute-done | bytes 524320 | tf_op jit(solution)/shard_map/ppermute | solution.py:318
  82.8 2.0 %collective-permute-start.23 = (f32[2,256,128]{2,1,0:T(8,128)S(1)}, f32[2,256,128]{2,1,0:T(8,128)S(1)}, u32[]{:S(2)}, u32[]{:S(2)}) collective-permute-start(f32[2,256,128]{2,1,0:T(8,128)S(1)} %get-tuple-element.31), channel_id=1, source_target_pairs={{0,8},{1,9},{2,10},{3,11},{4,12},{5,13},{6,14},{7,15},{8,0},{9,1},... | collective-permute-start | bytes 786440 | tf_op jit(solution)/shard_map/ppermute | solution.py:318
  84.9 4.1 %collective-permute-start.11 = (f32[2,256,128]{2,1,0:T(8,128)S(1)}, f32[2,256,128]{2,1,0:T(8,128)S(1)}, u32[]{:S(2)}, u32[]{:S(2)}) collective-permute-start(f32[2,256,128]{2,1,0:T(8,128)S(1)} %get-tuple-element.33), channel_id=1, source_target_pairs={{8,16},{9,17},{10,18},{11,19},{12,20},{13,21},{14,22},{15,23},{16,... | collective-permute-start | bytes 786440 | tf_op jit(solution)/shard_map/ppermute | solution.py:318
  92.2 4.4 %collective-permute-done.16 = f32[4,280,128]{2,1,0:T(8,128)S(1)} collective-permute-done((f32[4,280,128]{2,1,0:T(8,128)S(1)}, f32[4,280,128]{2,1,0:T(8,128)S(1)}, u32[]{:S(2)}, u32[]{:S(2)}) %collective-permute-start.16) | collective-permute-done | bytes 573472 | tf_op jit(solution)/shard_map/ppermute | solution.py:318
  97.7 2.8 %collective-permute-done.11 = f32[2,256,128]{2,1,0:T(8,128)S(1)} collective-permute-done((f32[2,256,128]{2,1,0:T(8,128)S(1)}, f32[2,256,128]{2,1,0:T(8,128)S(1)}, u32[]{:S(2)}, u32[]{:S(2)}) %collective-permute-start.11) | collective-permute-done | bytes 262176 | tf_op jit(solution)/shard_map/ppermute | solution.py:318
  101.3 2.4 %collective-permute-done.24 = f32[1,256,128]{2,1,0:T(8,128)S(1)} collective-permute-done((f32[1,256,128]{2,1,0:T(8,128)S(1)}, f32[1,256,128]{2,1,0:T(8,128)S(1)}, u32[]{:S(2)}, u32[]{:S(2)}) %collective-permute-start.24) | collective-permute-done | bytes 131104 | tf_op jit(solution)/shard_map/ppermute | solution.py:318
  103.7 2.0 %collective-permute-start.25 = (f32[256,128]{1,0:T(8,128)S(1)}, f32[256,128]{1,0:T(8,128)S(1)}, u32[]{:S(2)}, u32[]{:S(2)}) collective-permute-start(f32[256,128]{1,0:T(8,128)S(1)} %fusion.3), channel_id=1, source_target_pairs={{32,64},{64,32},{96,0},{0,96},{33,65},{65,33},{97,1},{1,97},{34,66... | collective-permute-start | bytes 393224 | tf_op jit(solution)/shard_map/ppermute | solution.py:327
  108.1 4.0 %collective-permute-done.18 = f32[1,280,128]{2,1,0:T(8,128)S(1)} collective-permute-done((f32[1,280,128]{2,1,0:T(8,128)S(1)}, f32[1,280,128]{2,1,0:T(8,128)S(1)}, u32[]{:S(2)}, u32[]{:S(2)}) %collective-permute-start.18) | collective-permute-done | bytes 143392 | tf_op jit(solution)/shard_map/ppermute | solution.py:318
  112.5 1.9 %collective-permute-start.7 = (f32[256,128]{1,0:T(8,128)S(1)}, f32[256,128]{1,0:T(8,128)S(1)}, u32[]{:S(2)}, u32[]{:S(2)}) collective-permute-start(f32[256,128]{1,0:T(8,128)S(1)} %fusion.7), channel_id=1, source_target_pairs={{0,32},{32,0},{64,96},{96,64},{1,33},{33,1},{65,97},{97,65},{2,34}... | collective-permute-start | bytes 393224 | tf_op jit(solution)/shard_map/ppermute | solution.py:327
  114.4 4.4 %collective-permute-done.19 = f32[280,128]{1,0:T(8,128)S(1)} collective-permute-done((f32[280,128]{1,0:T(8,128)S(1)}, f32[280,128]{1,0:T(8,128)S(1)}, u32[]{:S(2)}, u32[]{:S(2)}) %collective-permute-start.19) | collective-permute-done | bytes 143392 | tf_op jit(solution)/shard_map/ppermute | solution.py:327
  119.9 2.1 %collective-permute-start.14 = (f32[256,128]{1,0:T(8,128)S(1)}, f32[256,128]{1,0:T(8,128)S(1)}, u32[]{:S(2)}, u32[]{:S(2)}) collective-permute-start(f32[256,128]{1,0:T(8,128)S(1)} %add.146), channel_id=1, source_target_pairs={{0,32},{32,0},{64,96},{96,64},{1,33},{33,1},{65,97},{97,65},{2,34}... | collective-permute-start | bytes 393224 | tf_op jit(solution)/shard_map/ppermute | solution.py:327
  122.1 2.4 %collective-permute-start.8 = (f32[256,128]{1,0:T(8,128)S(1)}, f32[256,128]{1,0:T(8,128)S(1)}, u32[]{:S(2)}, u32[]{:S(2)}) collective-permute-start(f32[256,128]{1,0:T(8,128)S(1)} %add.136), channel_id=1, source_target_pairs={{32,64},{64,32},{96,0},{0,96},{33,65},{65,33},{97,1},{1,97},{34,66... | collective-permute-start | bytes 393224 | tf_op jit(solution)/shard_map/ppermute | solution.py:327
  129.6 2.8 %finish.1 = (f32[256,256]{1,0:T(8,128)}, f32[256,256]{1,0:T(8,128)}) custom-call(f32[256,128]{1,0:T(8,128)} %add.137.num_left, f32[256,128]{1,0:T(8,128)} %add.147.num_right, f32[280,128]{1,0:T(8,128)} %add.157.var_left, f32[256,128]{1,0:T(8,128)} %add.167.var_right), custom_call_target="tpu_custom_call" | custom-call | tf_op jit(solution)/shard_map/finish/pallas_call | solution.py:294
  (74 shorter events, 24.3 us)
Async XLA Ops:
  0.6 23.2 %collective-permute-start.1 = (f32[32,128,128]{2,1,0:T(8,128)}, f32[32,128,128]{2,1,0:T(8,128)S(1)}, u32[]{:S(2)}, u32[]{:S(2)}) collective-permute-start(f32[32,128,128]{2,1,0:T(8,128)} %variance.1), channel_id=1, source_target_pairs={{0,1},{1,0},{2,3},{3,2},{4,5},{5,4},{6,7},{7,6},{8,9},{9,8},{10,11... | collective-permute-start | bytes 6291464 | tf_op jit(solution)/shard_map/ppermute | solution.py:340
  19.5 17.6 %collective-permute-start.2 = (f32[32,128,128]{2,1,0:T(8,128)S(1)}, f32[32,128,128]{2,1,0:T(8,128)S(1)}, u32[]{:S(2)}, u32[]{:S(2)}) collective-permute-start(f32[32,128,128]{2,1,0:T(8,128)S(1)} %match.1.refs_3_), channel_id=1, source_target_pairs={{0,1},{1,0},{2,3},{3,2},{4,5},{5,4},{6,7},{7,6},{8,9},{9,8},{10,11... | collective-permute-start | bytes 6291464 | tf_op jit(solution)/shard_map/ppermute | solution.py:344
  35.4 25.5 %collective-permute-start.21 = (f32[8,256,128]{2,1,0:T(8,128)S(1)}, f32[8,256,128]{2,1,0:T(8,128)S(1)}, u32[]{:S(2)}, u32[]{:S(2)}) collective-permute-start(f32[8,256,128]{2,1,0:T(8,128)S(1)} %get-tuple-element.19), channel_id=1, source_target_pairs={{0,2},{1,3},{8,10},{9,11},{16,18},{17,19},{24,26},{25,27},{2,0},{3... | collective-permute-start | bytes 3145736 | tf_op jit(solution)/shard_map/ppermute | solution.py:318
  45.1 27.3 %collective-permute-start.9 = (f32[8,256,128]{2,1,0:T(8,128)S(1)}, f32[8,256,128]{2,1,0:T(8,128)S(1)}, u32[]{:S(2)}, u32[]{:S(2)}) collective-permute-start(f32[8,256,128]{2,1,0:T(8,128)S(1)} %get-tuple-element.15), channel_id=1, source_target_pairs={{2,4},{3,5},{10,12},{11,13},{18,20},{19,21},{26,28},{27,29},{4,2},... | collective-permute-start | bytes 3145736 | tf_op jit(solution)/shard_map/ppermute | solution.py:318
  47.3 27.6 %collective-permute-start.3 = (f32[8,256,128]{2,1,0:T(8,128)S(1)}, f32[8,256,128]{2,1,0:T(8,128)S(1)}, u32[]{:S(2)}, u32[]{:S(2)}) collective-permute-start(f32[8,256,128]{2,1,0:T(8,128)S(1)} %get-tuple-element.13), channel_id=1, source_target_pairs={{8,16},{9,17},{10,18},{11,19},{12,20},{13,21},{14,22},{15,23},{16,... | collective-permute-start | bytes 3145736 | tf_op jit(solution)/shard_map/ppermute | solution.py:318
  51.3 28.1 %collective-permute-start.15 = (f32[8,280,128]{2,1,0:T(8,128)S(1)}, f32[8,280,128]{2,1,0:T(8,128)S(1)}, u32[]{:S(2)}, u32[]{:S(2)}) collective-permute-start(f32[8,280,128]{2,1,0:T(8,128)S(1)} %get-tuple-element.17), channel_id=1, source_target_pairs={{0,8},{1,9},{2,10},{3,11},{4,12},{5,13},{6,14},{7,15},{8,0},{9,1},... | collective-permute-start | bytes 3440648 | tf_op jit(solution)/shard_map/ppermute | solution.py:318
  61.0 21.7 %collective-permute-start.22 = (f32[4,256,128]{2,1,0:T(8,128)S(1)}, f32[4,256,128]{2,1,0:T(8,128)S(1)}, u32[]{:S(2)}, u32[]{:S(2)}) collective-permute-start(f32[4,256,128]{2,1,0:T(8,128)S(1)} %get-tuple-element.23), channel_id=1, source_target_pairs={{2,4},{3,5},{10,12},{11,13},{18,20},{19,21},{26,28},{27,29},{4,2},... | collective-permute-start | bytes 1572872 | tf_op jit(solution)/shard_map/ppermute | solution.py:318
  72.5 12.3 %collective-permute-start.10 = (f32[4,256,128]{2,1,0:T(8,128)S(1)}, f32[4,256,128]{2,1,0:T(8,128)S(1)}, u32[]{:S(2)}, u32[]{:S(2)}) collective-permute-start(f32[4,256,128]{2,1,0:T(8,128)S(1)} %get-tuple-element.25), channel_id=1, source_target_pairs={{0,2},{1,3},{8,10},{9,11},{16,18},{17,19},{24,26},{25,27},{2,0},{3... | collective-permute-start | bytes 1572872 | tf_op jit(solution)/shard_map/ppermute | solution.py:318
  75.0 15.6 %collective-permute-start.4 = (f32[4,256,128]{2,1,0:T(8,128)S(1)}, f32[4,256,128]{2,1,0:T(8,128)S(1)}, u32[]{:S(2)}, u32[]{:S(2)}) collective-permute-start(f32[4,256,128]{2,1,0:T(8,128)S(1)} %get-tuple-element.27), channel_id=1, source_target_pairs={{0,8},{1,9},{2,10},{3,11},{4,12},{5,13},{6,14},{7,15},{8,0},{9,1},... | collective-permute-start | bytes 1572872 | tf_op jit(solution)/shard_map/ppermute | solution.py:318
  79.5 17.1 %collective-permute-start.16 = (f32[4,280,128]{2,1,0:T(8,128)S(1)}, f32[4,280,128]{2,1,0:T(8,128)S(1)}, u32[]{:S(2)}, u32[]{:S(2)}) collective-permute-start(f32[4,280,128]{2,1,0:T(8,128)S(1)} %get-tuple-element.21), channel_id=1, source_target_pairs={{8,16},{9,17},{10,18},{11,19},{12,20},{13,21},{14,22},{15,23},{16,... | collective-permute-start | bytes 1720328 | tf_op jit(solution)/shard_map/ppermute | solution.py:318
  82.8 14.6 %collective-permute-start.23 = (f32[2,256,128]{2,1,0:T(8,128)S(1)}, f32[2,256,128]{2,1,0:T(8,128)S(1)}, u32[]{:S(2)}, u32[]{:S(2)}) collective-permute-start(f32[2,256,128]{2,1,0:T(8,128)S(1)} %get-tuple-element.31), channel_id=1, source_target_pairs={{0,8},{1,9},{2,10},{3,11},{4,12},{5,13},{6,14},{7,15},{8,0},{9,1},... | collective-permute-start | bytes 786440 | tf_op jit(solution)/shard_map/ppermute | solution.py:318
  84.9 15.6 %collective-permute-start.11 = (f32[2,256,128]{2,1,0:T(8,128)S(1)}, f32[2,256,128]{2,1,0:T(8,128)S(1)}, u32[]{:S(2)}, u32[]{:S(2)}) collective-permute-start(f32[2,256,128]{2,1,0:T(8,128)S(1)} %get-tuple-element.33), channel_id=1, source_target_pairs={{8,16},{9,17},{10,18},{11,19},{12,20},{13,21},{14,22},{15,23},{16,... | collective-permute-start | bytes 786440 | tf_op jit(solution)/shard_map/ppermute | solution.py:318
  90.7 9.9 %collective-permute-start.5 = (f32[2,256,128]{2,1,0:T(8,128)S(1)}, f32[2,256,128]{2,1,0:T(8,128)S(1)}, u32[]{:S(2)}, u32[]{:S(2)}) collective-permute-start(f32[2,256,128]{2,1,0:T(8,128)S(1)} %get-tuple-element.35), channel_id=1, source_target_pairs={{2,4},{3,5},{10,12},{11,13},{18,20},{19,21},{26,28},{27,29},{4,2},... | collective-permute-start | bytes 786440 | tf_op jit(solution)/shard_map/ppermute | solution.py:318
  96.7 9.0 %collective-permute-start.17 = (f32[2,280,128]{2,1,0:T(8,128)S(1)}, f32[2,280,128]{2,1,0:T(8,128)S(1)}, u32[]{:S(2)}, u32[]{:S(2)}) collective-permute-start(f32[2,280,128]{2,1,0:T(8,128)S(1)} %get-tuple-element.29), channel_id=1, source_target_pairs={{0,2},{1,3},{8,10},{9,11},{16,18},{17,19},{24,26},{25,27},{2,0},{3... | collective-permute-start | bytes 860168 | tf_op jit(solution)/shard_map/ppermute | solution.py:318
  97.4 6.3 %collective-permute-start.24 = (f32[1,256,128]{2,1,0:T(8,128)S(1)}, f32[1,256,128]{2,1,0:T(8,128)S(1)}, u32[]{:S(2)}, u32[]{:S(2)}) collective-permute-start(f32[1,256,128]{2,1,0:T(8,128)S(1)} %slice_add_fusion.18), channel_id=1, source_target_pairs={{8,16},{9,17},{10,18},{11,19},{12,20},{13,21},{14,22},{15,23},{16,... | collective-permute-start | bytes 393224 | tf_op jit(solution)/shard_map/ppermute | solution.py:318
  100.5 6.6 %collective-permute-start.12 = (f32[1,256,128]{2,1,0:T(8,128)S(1)}, f32[1,256,128]{2,1,0:T(8,128)S(1)}, u32[]{:S(2)}, u32[]{:S(2)}) collective-permute-start(f32[1,256,128]{2,1,0:T(8,128)S(1)} %slice_add_fusion.20), channel_id=1, source_target_pairs={{0,8},{1,9},{2,10},{3,11},{4,12},{5,13},{6,14},{7,15},{8,0},{9,1},... | collective-permute-start | bytes 393224 | tf_op jit(solution)/shard_map/ppermute | solution.py:318
  100.6 11.9 %collective-permute-start.6 = (f32[1,256,128]{2,1,0:T(8,128)S(1)}, f32[1,256,128]{2,1,0:T(8,128)S(1)}, u32[]{:S(2)}, u32[]{:S(2)}) collective-permute-start(f32[1,256,128]{2,1,0:T(8,128)S(1)} %slice_add_fusion.22), channel_id=1, source_target_pairs={{0,2},{1,3},{8,10},{9,11},{16,18},{17,19},{24,26},{25,27},{2,0},{3... | collective-permute-start | bytes 393224 | tf_op jit(solution)/shard_map/ppermute | solution.py:318
  103.7 16.1 %collective-permute-start.25 = (f32[256,128]{1,0:T(8,128)S(1)}, f32[256,128]{1,0:T(8,128)S(1)}, u32[]{:S(2)}, u32[]{:S(2)}) collective-permute-start(f32[256,128]{1,0:T(8,128)S(1)} %fusion.3), channel_id=1, source_target_pairs={{32,64},{64,32},{96,0},{0,96},{33,65},{65,33},{97,1},{1,97},{34,66... | collective-permute-start | bytes 393224 | tf_op jit(solution)/shard_map/ppermute | solution.py:327
  105.7 6.4 %collective-permute-start.18 = (f32[1,280,128]{2,1,0:T(8,128)S(1)}, f32[1,280,128]{2,1,0:T(8,128)S(1)}, u32[]{:S(2)}, u32[]{:S(2)}) collective-permute-start(f32[1,280,128]{2,1,0:T(8,128)S(1)} %slice_add_fusion.16), channel_id=1, source_target_pairs={{2,4},{3,5},{10,12},{11,13},{18,20},{19,21},{26,28},{27,29},{4,2},... | collective-permute-start | bytes 430088 | tf_op jit(solution)/shard_map/ppermute | solution.py:318
  107.1 12.8 %collective-permute-start.13 = (f32[256,128]{1,0:T(8,128)S(1)}, f32[256,128]{1,0:T(8,128)S(1)}, u32[]{:S(2)}, u32[]{:S(2)}) collective-permute-start(f32[256,128]{1,0:T(8,128)S(1)} %fusion.5), channel_id=1, source_target_pairs={{32,64},{64,32},{96,0},{0,96},{33,65},{65,33},{97,1},{1,97},{34,66... | collective-permute-start | bytes 393224 | tf_op jit(solution)/shard_map/ppermute | solution.py:327
  112.1 6.6 %collective-permute-start.19 = (f32[280,128]{1,0:T(8,128)S(1)}, f32[280,128]{1,0:T(8,128)S(1)}, u32[]{:S(2)}, u32[]{:S(2)}) collective-permute-start(f32[280,128]{1,0:T(8,128)S(1)} %fusion.1), channel_id=1, source_target_pairs={{0,32},{32,0},{64,96},{96,64},{1,33},{33,1},{65,97},{97,65},{2,34}... | collective-permute-start | bytes 430088 | tf_op jit(solution)/shard_map/ppermute | solution.py:327
  112.5 9.5 %collective-permute-start.7 = (f32[256,128]{1,0:T(8,128)S(1)}, f32[256,128]{1,0:T(8,128)S(1)}, u32[]{:S(2)}, u32[]{:S(2)}) collective-permute-start(f32[256,128]{1,0:T(8,128)S(1)} %fusion.7), channel_id=1, source_target_pairs={{0,32},{32,0},{64,96},{96,64},{1,33},{33,1},{65,97},{97,65},{2,34}... | collective-permute-start | bytes 393224 | tf_op jit(solution)/shard_map/ppermute | solution.py:327
  118.8 10.2 %collective-permute-start.20 = (f32[280,128]{1,0:T(8,128)S(1)}, f32[280,128]{1,0:T(8,128)S(1)}, u32[]{:S(2)}, u32[]{:S(2)}) collective-permute-start(f32[280,128]{1,0:T(8,128)S(1)} %add.156), channel_id=1, source_target_pairs={{32,64},{64,32},{96,0},{0,96},{33,65},{65,33},{97,1},{1,97},{34,66... | collective-permute-start | bytes 430088 | tf_op jit(solution)/shard_map/ppermute | solution.py:327
  119.9 6.3 %collective-permute-start.14 = (f32[256,128]{1,0:T(8,128)S(1)}, f32[256,128]{1,0:T(8,128)S(1)}, u32[]{:S(2)}, u32[]{:S(2)}) collective-permute-start(f32[256,128]{1,0:T(8,128)S(1)} %add.146), channel_id=1, source_target_pairs={{0,32},{32,0},{64,96},{96,64},{1,33},{33,1},{65,97},{97,65},{2,34}... | collective-permute-start | bytes 393224 | tf_op jit(solution)/shard_map/ppermute | solution.py:327
  (10 other events, 69.3 us)

commit v3 on v2

v3 whole, which is shorter than its diff:
```python
import functools

import jax
import jax.numpy as jnp
from jax import lax
from jax.experimental import pallas as pl
from jax.experimental.pallas import tpu as pltpu
from jax.sharding import PartitionSpec as P

TS = 128
PATCH = 256
NB = 3
NBASIS = 8
HALF = 20
TILES = 32
ROUTES = 2 * TILES
CAP = 3
META = 24
PAD = 64
F32 = jnp.float32
BF16 = jnp.bfloat16

EMPTY = 1 << 24
UNROLL = 2
MATCH_UNROLL = 8
CHUNKS = 2
MATCH_COST = 100_000_000_000
WARP_COST = 10_000_000_000


def split(x):
    high = x.astype(BF16)
    return high, (x - high.astype(F32)).astype(BF16)


def pack_kernel(mine, intersections, boxes, shifts, out):
    out[...] = jnp.zeros_like(out)
    z, y, core = intersections[...] >> 3, (intersections[...] >> 1) & 3, intersections[...] & 1
    z, y = z ^ (z >> 1), y ^ (y >> 1)
    code = ((z & 1) << 3) | ((z >> 1) << 2) | ((y & 1) << 1) | (y >> 1)
    out[0:2, 0:TILES] = ((code ^ mine[0]) + 16 * core).astype(F32)
    for route in range(2):
        out[2 + 2 * route : 4 + 2 * route, 0:TILES] = boxes[route].astype(F32)
        out[6 + 2 * route : 8 + 2 * route, 0:TILES] = shifts[route]


def pack(mine, intersections, boxes, shifts):
    vmem = pl.BlockSpec(memory_space=pltpu.VMEM)
    return pl.pallas_call(
        pack_kernel,
        out_shape=jax.ShapeDtypeStruct((16, TS), F32),
        in_specs=[pl.BlockSpec(memory_space=pltpu.SMEM)] + [vmem] * 3,
        out_specs=vmem,
        name="pack",
    )(mine, intersections.T, boxes.transpose(1, 2, 0), shifts.transpose(1, 2, 0))


def match_kernel(
    basis_ids, coefs, taps_hbm, image_hbm, variance_hbm, out, taps, line, row_mats, col_mats, image, variance, sems, taps_sem
):
    size = TILES // CHUNKS
    copies = [
        [
            pltpu.make_async_copy(source.at[pl.ds(c * size, size)], target.at[pl.ds(c * size, size)], sems.at[i, c])
            for i, (source, target) in enumerate(((image_hbm, image), (variance_hbm, variance)))
        ]
        for c in range(CHUNKS)
    ]
    fetch = pltpu.make_async_copy(taps_hbm, taps, taps_sem)
    fetch.start()
    for pair in copies:
        for copy in pair:
            copy.start()
    i = lax.broadcasted_iota(jnp.int32, (TS, TS), 0)
    k = lax.broadcasted_iota(jnp.int32, (TS, TS), 1)
    near = jnp.abs(i - k) <= HALF
    none = jnp.zeros((TS, TS), BF16)
    line[...] = jnp.zeros_like(line)
    fetch.wait()
    for b in range(NBASIS):
        line[2 * b : 2 * b + 2, 0 : 2 * HALF + 1] = taps[b]
    line[...] = pltpu.roll(line[...], TS - HALF, 1)

    def square(high, low):
        return jnp.concatenate([jnp.concatenate([high, low], 1), jnp.concatenate([high, none], 1)], 0)

    for b in range(NBASIS):
        for side in range(2):
            band = jnp.broadcast_to(line[2 * b + side : 2 * b + side + 1, :], (TS, TS))
            band = jnp.where(near, pltpu.roll(band, 0, 1, stride=1, stride_axis=0), 0.0)
            if side == 0:
                row_mats[b] = jnp.concatenate(split(band.T), 1)
            else:
                col_mats[b] = square(*split(band))

    for c in range(CHUNKS):
        for copy in copies[c]:
            copy.wait()

        @pl.loop(c * size, (c + 1) * size, step=MATCH_UNROLL)
        def _(first):
            for t in [first + u for u in range(MATCH_UNROLL)]:
                weight = float(TS * TS) / jnp.sum(variance[t], axis=(0, 1), keepdims=True)
                pixels = square(*split(image[t]))
                total = None
                for j in range(NB):
                    basis = basis_ids[j, t]
                    p = jnp.dot(row_mats[basis], pixels, preferred_element_type=F32)
                    part = (p[:, :TS] + p[:, TS:]) * coefs[j, t]
                    p = jnp.dot(jnp.concatenate(split(part), 1), col_mats[basis], preferred_element_type=F32)
                    total = p if total is None else total + p
                out[t] = (total[:, :TS] + total[:, TS:]) * weight


def match(basis_ids, coefs, taps, image, variance):
    vmem, hbm = pl.BlockSpec(memory_space=pltpu.VMEM), pl.BlockSpec(memory_space=pltpu.HBM)
    return pl.pallas_call(
        match_kernel,
        out_shape=jax.ShapeDtypeStruct((TILES, TS, TS), F32),
        in_specs=[pl.BlockSpec(memory_space=pltpu.SMEM)] * 2 + [hbm] * 3,
        out_specs=vmem,
        scratch_shapes=[
            pltpu.VMEM((NBASIS, 2, 2 * HALF + 1), F32),
            pltpu.VMEM((2 * NBASIS, TS), F32),
            pltpu.VMEM((NBASIS, TS, 2 * TS), BF16),
            pltpu.VMEM((NBASIS, 2 * TS, 2 * TS), BF16),
            pltpu.VMEM((TILES, TS, TS), F32),
            pltpu.VMEM((TILES, TS, TS), F32),
            pltpu.SemaphoreType.DMA((2, CHUNKS)),
            pltpu.SemaphoreType.DMA,
        ],
        compiler_params=pltpu.CompilerParams(vmem_limit_bytes=40 << 20),
        cost_estimate=pl.CostEstimate(flops=MATCH_COST, bytes_accessed=6 << 20, transcendentals=0),
        name="match",
    )(*(pltpu.with_memory_space_constraint(x, pltpu.HBM) for x in (basis_ids.T, coefs.T, taps, image, variance)))


def warp_kernel(with_meta, *refs):
    first, own, other, own_tiles, other_tiles = refs[:5]
    outs = refs[5:9]
    if with_meta:
        slots = refs[9]
        stage, acc, meta, weights, counts, seen = refs[10:]
    else:
        slots = first
        stage, acc = refs[9:]
    lane = lax.broadcasted_iota(jnp.int32, (8, TS), 1)
    stage[:, :, 0:8, :] = jnp.zeros((2 * UNROLL, 2, 8, TS), F32)
    stage[:, :, 8 + TS :, :] = jnp.zeros((2 * UNROLL, 2, 8, TS), F32)
    for k in range(16):
        for side in (1, 2):
            acc[4 * k + side, PAD : PAD + PATCH, :] = jnp.zeros((PATCH, TS), F32)

    if with_meta:
        core, chip = first[1], first[2]
        meta[...] = jnp.zeros_like(meta)
        for side in range(2):
            counts[side] = 0
            for k in range(17):
                seen[side, k] = 0

        for route in range(2):

            @pl.loop(0, TILES)
            def _(t, route=route):
                for side, table in ((0, own), (1, other)):
                    k = table[route, t].astype(jnp.int32) - 16 * core
                    ours = (k >= 0) & (k < 16)
                    k = jnp.where(ours, k, 16)
                    slot, n = seen[side, k], counts[side]
                    slots[side, 1 + n] = (k << 16) + (slot << 8) + (2 * t + route)
                    seen[side, k] = slot + 1
                    counts[side] = n + ours.astype(jnp.int32)

        for side in range(2):
            n = counts[side]
            slots[side, 0] = n
            for u in range(3 * UNROLL):
                slots[side, 1 + n + u] = EMPTY

        for side, tiles in ((0, own_tiles), (1, other_tiles)):

            @pl.loop(0, TILES, step=8)
            def _(t, side=side, tiles=tiles):
                sums = jnp.concatenate([jnp.sum(tiles[t + u], axis=0, keepdims=True) for u in range(8)], 0)
                sums = jnp.sum(sums, axis=1, keepdims=True)
                at = pl.multiple_of(side * TILES + t, 8)
                weights[pl.ds(at, 8), :] = jnp.broadcast_to(float(TS * TS) / sums, (8, TS))

    def place(entry, u, side, table, tiles):
        item, slot, k = entry & 255, (entry >> 8) & 255, (entry >> 16) & 15
        t, route = item >> 1, item & 1
        row, col = table[2 + 2 * route, t].astype(jnp.int32), table[3 + 2 * route, t].astype(jnp.int32)
        frac_row, frac_col = table[6 + 2 * route, t], table[7 + 2 * route, t]
        real = jnp.where(entry >= EMPTY, 0.0, 1.0)
        near, far = jnp.full((8, TS), (1.0 - frac_col) * real), jnp.full((8, TS), frac_col * real)
        if with_meta:
            weight = jnp.broadcast_to(weights[pl.ds(side * TILES + t, 1), :], (8, TS))
            field = lax.broadcasted_iota(jnp.int32, (8, TS), 0)
            value = jnp.where(field == 1, row.astype(F32), weight)
            value = jnp.where(field == 2, col.astype(F32), value)
            value = jnp.where(field == 3, frac_row, value)
            value = jnp.where(field == 4, frac_col, value)
            value = jnp.where((field < 5) & (lane == 2 * chip + side), value * real, 0.0)
            meta[k * CAP + slot] += value
            near, far = near * (weight * weight), far * (weight * weight)
        turn = (col + TS) & (TS - 1)
        here = jnp.where(lane >= turn, near, 0.0)
        here_next = jnp.where(lane >= turn + 1, far, 0.0)
        over, over_next = near - here, far - here_next
        tile = tiles[t]
        r0 = pltpu.roll(tile, turn, 1).reshape(TS // 8, 8, TS)
        r1 = pltpu.roll(tile, (turn + 1) & (TS - 1), 1).reshape(TS // 8, 8, TS)
        stage[u, 0, 8 : 8 + TS, :] = (r0 * here + r1 * here_next).reshape(TS, TS)
        stage[u, 1, 8 : 8 + TS, :] = (r0 * over + r1 * over_next).reshape(TS, TS)
        return 4 * k + ((col + TS) >> 7), row + PAD, frac_row

    def add_rows(u, first, row, frac_row):
        down = row & 7
        base = pl.multiple_of((row >> 3) * 8, 8)
        for side in range(2):
            upper = stage[u, side, pl.ds(8 - down, TS + 8), :]
            lower = stage[u, side, pl.ds(7 - down, TS + 8), :]
            acc[first + side, pl.ds(base, TS + 8), :] += upper * (1.0 - frac_row) + lower * frac_row

    for side, table, tiles in ((0, own, own_tiles), (1, other, other_tiles)):
        start = [place(slots[side, 1 + u], u, side, table, tiles) for u in range(UNROLL)]

        def body(m, placed, side=side, table=table, tiles=tiles):
            for half in range(2):
                group = 2 * m + half + 1
                then = [
                    place(slots[side, 1 + group * UNROLL + u], UNROLL * (1 - half) + u, side, table, tiles)
                    for u in range(UNROLL)
                ]
                for u in range(UNROLL):
                    add_rows(UNROLL * half + u, *placed[u])
                placed = then
            return placed

        lax.fori_loop(0, (slots[side, 0] + 2 * UNROLL - 1) // (2 * UNROLL), body, start)

    for k in range(16):
        z_first, z_second, y_first, y_second = k >> 3, (k >> 2) & 1, (k >> 1) & 1, k & 1
        if not with_meta:
            z_first, z_second, y_first, y_second = z_second, z_first, y_second, y_first
        left, right = outs[z_first], outs[2 + y_first]
        at = z_second * 4 + y_first * 2 + y_second
        left[at, 0:PATCH, :] = acc[4 * k + 1, PAD : PAD + PATCH, :]
        if with_meta:
            for slot in range(CAP):
                left[at, PATCH + 8 * slot : PATCH + 8 * slot + 8, :] = meta[k * CAP + slot]
        right[y_second * 4 + z_first * 2 + z_second, :, :] = acc[4 * k + 2, PAD : PAD + PATCH, :]


def warp(with_meta, first, own, other, own_tiles, other_tiles):
    smem, vmem = pl.BlockSpec(memory_space=pltpu.SMEM), pl.BlockSpec(memory_space=pltpu.VMEM)
    rows = PATCH + META if with_meta else PATCH
    left = jax.ShapeDtypeStruct((8, rows, TS), F32)
    right = jax.ShapeDtypeStruct((8, PATCH, TS), F32)
    outs, specs = [left, left, right, right], [vmem] * 4
    scratch = [
        pltpu.VMEM((2 * UNROLL, 2, TS + 16, TS), F32),
        pltpu.VMEM((64, 384, TS), F32),
    ]
    if with_meta:
        outs, specs = outs + [jax.ShapeDtypeStruct((2, 128), jnp.int32)], specs + [smem]
        scratch += [
            pltpu.VMEM((16 * CAP, 8, TS), F32),
            pltpu.VMEM((2 * TILES, TS), F32),
            pltpu.SMEM((2,), jnp.int32),
            pltpu.SMEM((2, 17), jnp.int32),
        ]
    return pl.pallas_call(
        functools.partial(warp_kernel, with_meta),
        out_shape=outs,
        in_specs=[smem] * 3 + [vmem] * 2,
        out_specs=specs,
        scratch_shapes=scratch,
        compiler_params=pltpu.CompilerParams(vmem_limit_bytes=40 << 20),
        cost_estimate=pl.CostEstimate(flops=WARP_COST, bytes_accessed=8 << 20, transcendentals=0),
        name="warp_meta" if with_meta else "warp",
    )(first, own, other, own_tiles, other_tiles)


def cover_kernel(left, left_got, right, right_got, coadd_var, safe_ref):
    place_of = lax.broadcasted_iota(jnp.int32, (PATCH, TS), 0).astype(F32)

    def cover(offset, shift):
        u = place_of - offset
        lower = jnp.where((u >= 0.0) & (u <= TS - 1.0), 1.0 - shift, 0.0)
        return lower + jnp.where((u >= 1.0) & (u <= float(TS)), shift, 0.0)

    den = jnp.zeros((PATCH, PATCH), F32)
    for slot in range(CAP):
        at = PATCH + 8 * slot
        fields = left[at : at + 8, :] + left_got[at : at + 8, :]
        weight, row, col, frac_row, frac_col = (fields[f : f + 1, :] for f in range(5))
        down, across = cover(row, frac_row) * weight, cover(col, frac_col)
        den += lax.dot_general(
            down, across, (((1,), (1,)), ((), ())), precision=lax.Precision.HIGHEST, preferred_element_type=F32
        )
    safe = jnp.maximum(den, 1.0)
    safe_ref[...] = safe
    for var, got, lo in ((left, left_got, 0), (right, right_got, TS)):
        part = safe[:, lo : lo + TS]
        coadd_var[:, lo : lo + TS] = (var[0:PATCH, :] + got[0:PATCH, :]) / (part * part)


def divide_kernel(left, left_got, right, right_got, safe, coadd):
    coadd[:, 0:TS] = (left[...] + left_got[...]) / safe[:, 0:TS]
    coadd[:, TS:] = (right[...] + right_got[...]) / safe[:, TS:]


def finish(kernel, name, outs, *args):
    vmem = pl.BlockSpec(memory_space=pltpu.VMEM)
    return pl.pallas_call(
        kernel,
        out_shape=[jax.ShapeDtypeStruct((PATCH, PATCH), F32)] * outs,
        in_specs=[vmem] * len(args),
        out_specs=[vmem] * outs,
        compiler_params=pltpu.CompilerParams(vmem_limit_bytes=8 << 20),
        cost_estimate=pl.CostEstimate(flops=1_000_000_000, bytes_accessed=1 << 20, transcendentals=0),
        name=name,
    )(*args)


EDGES = (((0, 1), (1, 0), (2, 3), (3, 2)), ((1, 2), (2, 1), (3, 0), (0, 3)))


def over_patch(axis, edge):
    pairs = []
    for a, b in EDGES[edge]:
        for other in range(4):
            for core in range(2):
                src, dst = ((a, other), (b, other)) if axis == "z" else ((other, a), (other, b))
                pairs.append((src[0] * 8 + src[1] * 2 + core, dst[0] * 8 + dst[1] * 2 + core))
    return pairs


def halve(left, right, orders, ahead=()):
    parts, received = [left, right], []
    for step in range(4):
        got = [lax.ppermute(send, "patch", over_patch(*order[step])) for (_, send), order in zip(parts, orders)]
        if step < len(ahead):
            got = lax.optimization_barrier((*got, *ahead[step]))[:2]
        received.append(tuple(got))
        if step < 3:
            n = 8 >> (step + 1)
            parts = [(keep[:n] + g[:n], keep[n:] + g[n:]) for (keep, _), g in zip(parts, got)]
        else:
            parts = [keep[0] + g[0] for (keep, _), g in zip(parts, got)]
    return parts, received


def double(left, right):
    parts = [x + lax.ppermute(x, "visit", EDGES[first]) for x, first in ((left, 0), (right, 1))]
    return [y for x, first in zip(parts, (1, 0)) for y in (x, lax.ppermute(x, "visit", EDGES[first]))]


def shards(image, variance, intersections, boxes, shifts, basis_ids, coefs, taps):
    swap = [(i, i ^ 1) for i in range(32)]
    patch = lax.axis_index("patch")
    z, y = patch >> 3, (patch >> 1) & 3
    chip = lax.axis_index("visit") * 16 + z * 4 + y
    z, y = z ^ (z >> 1), y ^ (y >> 1)
    mine = ((z & 1) << 3) | ((z >> 1) << 2) | ((y & 1) << 1) | (y >> 1)
    where = jnp.stack([mine, patch & 1, chip])

    other_variance = lax.ppermute(variance, "patch", swap)
    table = pack(where, intersections, boxes, shifts)
    other_table = lax.ppermute(table, "patch", swap)
    matched = match(basis_ids, coefs, taps, image, variance)
    matched, other_table = lax.optimization_barrier((matched, other_table))
    other_matched = lax.ppermute(matched, "patch", swap)
    var_left_keep, var_left_send, var_right_keep, var_right_send, slots = warp(
        True, where, table, other_table, variance, other_variance
    )
    num_left_keep, num_left_send, num_right_keep, num_right_send = warp(
        False, slots, table, other_table, matched, other_matched
    )
    z1, z2, y1, y2 = ("z", 0), ("z", 1), ("y", 0), ("y", 1)
    var, ahead = halve((var_left_keep, var_left_send), (var_right_keep, var_right_send), ((z1, z2, y1, y2), (y1, y2, z1, z2)))
    num, _ = halve(
        (num_left_keep, num_left_send), (num_right_keep, num_right_send), ((z2, z1, y2, y1), (y2, y1, z2, z1)), ahead
    )
    var, num = double(*var), double(*num)
    coadd_var, safe = finish(cover_kernel, "cover", 2, *var)
    (coadd,) = finish(divide_kernel, "divide", 1, *num, safe)
    return coadd, coadd_var


def solution(mesh):
    split_spec = ("visit", "patch")
    in_specs = (
        P(split_spec, None, None),
        P(split_spec, None, None),
        P(split_spec, None),
        P(split_spec, None, None),
        P(split_spec, None, None),
        P(split_spec, None),
        P(split_spec, None),
        P(),
    )
    out_specs = (P("patch", None), P("patch", None))
    return jax.shard_map(shards, mesh=mesh, in_specs=in_specs, out_specs=out_specs, check_vma=False)
```

time: 133 us -> 114 us (0.86); the launches traced: 132 us -> 115 us
  Pallas kernels: 35.8 us -> 27.4 us
  waiting for transfers between devices: 53.3 us -> 47.1 us
  starting transfers between devices: 33.6 us -> 38.4 us
  local copies, waits for them, and re-layouts: 4.58 us -> 0.01 us
  other arithmetic: 4.38 us -> 1.62 us
    ppermute x24, starting transfers between devices: 32.9 us -> 37.8 us  [the longest x16 23.9 us: halve(): lax.ppermute(send, 'patch', over_patch(*order[step]))]
    unnamed x14 -> x6, local copies, waits for them, and re-layouts: 4.58 us -> 0.01 us
    pallas_call x1, Pallas kernels: 12.2 us -> 7.73 us  [match(): pl.pallas_call(match_kernel, out_shape=jax.ShapeDtypeStruct((TILES, TS, T...]
    ppermute x1, waiting for transfers between devices: 3.71 us -> 0.01 us  [shards(): other_table = lax.ppermute(table, 'patch', swap)]
    pallas_call x2, Pallas kernels: 19.4 us -> 15.9 us  [warp(): pl.pallas_call(functools.partial(warp_kernel, with_meta), out_shape=outs,...]
    add x24 -> x20, other arithmetic: 3.78 us -> 1 us  [the longest x6 0.6 us: halve(): keep[:n] + g[:n]]
    ppermute x24, waiting for transfers between devices: 49.6 us -> 47.1 us  [the longest x16 41.5 us: halve(): lax.ppermute(send, 'patch', over_patch(*order[step]))]
    pallas_call x1 -> x2, Pallas kernels: 2.83 us -> 2.42 us  [finish(): pl.pallas_call(kernel, out_shape=[jax.ShapeDtypeStruct((PATCH, PATCH), F3...]
  transfers between devices with their start and end apart: 27 -> 27, of which waited for: 15 -> 12; matrix products, arithmetic and copies ran while one was open for 3% -> 1% of each run, Pallas kernels for 25% -> 22%
where the time goes in v3:
time: 114 us; the launch traced here: 115 us
  waiting for transfers between devices  47.1 us (41%)
  starting transfers between devices  38.4 us (34%)
  Pallas kernels  27.4 us (24%)
  other arithmetic  1.62 us (1%)
    ppermute x16, waiting for transfers between devices, halve(): lax.ppermute(send, 'patch', over_patch(*order[step]))  41.5 us
    ppermute x16, starting transfers between devices, halve(): lax.ppermute(send, 'patch', over_patch(*order[step]))  23.9 us
    pallas_call x2, Pallas kernels, warp(): pl.pallas_call(functools.partial(warp_kernel, with_meta), out_shape=outs,...  15.9 us
    ppermute x8, starting transfers between devices, double(): lax.ppermute(x, 'visit', EDGES[first])  13.8 us
    pallas_call x1, Pallas kernels, match(): pl.pallas_call(match_kernel, out_shape=jax.ShapeDtypeStruct((TILES, TS, T...  7.73 us
    ppermute x8, waiting for transfers between devices, double(): lax.ppermute(x, 'visit', EDGES[first])  5.58 us
    pallas_call x2, Pallas kernels, finish(): pl.pallas_call(kernel, out_shape=[jax.ShapeDtypeStruct((PATCH, PATCH), F3...  2.42 us
  transfers between devices with their start and end apart: 27, of which 12 were waited for; matrix products, arithmetic and copies ran while one was open for 1% of the time, Pallas kernels for 22%

profile of v3, /device:TPU:0, one launch (start us, length us, event | category | flops | bytes accessed | tf_op | source)
XLA Modules:
  0.0 115.4 jit_solution(16053051059492769478)
XLA Ops:
  3.2 7.7 %match.1.refs_3_ = f32[32,128,128]{2,1,0:T(8,128)S(1)} custom-call(s32[3,32]{1,0:T(4,128)} %bitcast.19, f32[3,32]{1,0:T(4,128)} %bitcast.20, f32[8,2,41]{2,1,0:T(2,128)} %taps_hbm.1, f32[32,128,128]{2,1,0:T(8,128)} %image_hbm.1, f32[32,128,128]{2,1,0:T(8,128)} %refs_3_.1), custom_call_target="tpu_custom_call" | custom-call | flops 99999997952 | bytes 6291456 | tf_op jit(solution)/shard_map/match/pallas_call | solution.py:117
  11.1 9.3 %warp_meta.1 = (f32[8,280,128]{2,1,0:T(8,128)S(1)}, f32[8,280,128]{2,1,0:T(8,128)S(1)}, f32[8,256,128]{2,1,0:T(8,128)S(1)}, f32[8,256,128]{2,1,0:T(8,128)S(1)}, s32[2,128]{1,0:T(2,128)S(1)}) custom-call(s32[3]{0:T(128)S(1)} %copy-done.1, f32[16,128]{1,0:T(8,128)S(1)} %copy-done, f32[16,128]{1,0:T(8,128)S(1)} %collective-permute-done.refs_2_, ...), custom_call_target="tpu_custom_call" | custom-call | flops 10000000000 | bytes 8388608 | tf_op jit(solution)/shard_map/warp_meta/pallas_call | solution.py:274
  20.4 1.7 %collective-permute-start.6 = (f32[8,256,128]{2,1,0:T(8,128)S(1)}, f32[8,256,128]{2,1,0:T(8,128)S(1)}, u32[]{:S(2)}, u32[]{:S(2)}) collective-permute-start(f32[8,256,128]{2,1,0:T(8,128)S(1)} %get-tuple-element.30), channel_id=1, source_target_pairs={{0,2},{1,3},{8,10},{9,11},{16,18},{17,19},{24,26},{25,27},{2,0},{3... | collective-permute-start | bytes 3145736 | tf_op jit(solution)/shard_map/ppermute | solution.py:344
  22.1 2.0 %collective-permute-start.5 = (f32[8,280,128]{2,1,0:T(8,128)S(1)}, f32[8,280,128]{2,1,0:T(8,128)S(1)}, u32[]{:S(2)}, u32[]{:S(2)}) collective-permute-start(f32[8,280,128]{2,1,0:T(8,128)S(1)} %get-tuple-element.29), channel_id=1, source_target_pairs={{0,8},{1,9},{2,10},{3,11},{4,12},{5,13},{6,14},{7,15},{8,0},{9,1},... | collective-permute-start | bytes 3440648 | tf_op jit(solution)/shard_map/ppermute | solution.py:344
  24.1 6.5 %warp.1 = (f32[8,256,128]{2,1,0:T(8,128)S(1)}, f32[8,256,128]{2,1,0:T(8,128)S(1)}, f32[8,256,128]{2,1,0:T(8,128)S(1)}, f32[8,256,128]{2,1,0:T(8,128)S(1)}) custom-call(s32[2,128]{1,0:T(2,128)S(1)} %get-tuple-element.24.refs_0_, f32[16,128]{1,0:T(8,128)S(1)} %copy-done, f32[16,128]{1,0:T(8,128)S(1)} %collective-permute-done.refs_2_, ...), custom_call_target="tpu_custom_call" | custom-call | flops 10000000000 | bytes 8388608 | tf_op jit(solution)/shard_map/warp/pallas_call | solution.py:274
  30.6 2.6 %collective-permute-start.3 = (f32[8,256,128]{2,1,0:T(8,128)S(1)}, f32[8,256,128]{2,1,0:T(8,128)S(1)}, u32[]{:S(2)}, u32[]{:S(2)}) collective-permute-start(f32[8,256,128]{2,1,0:T(8,128)S(1)} %get-tuple-element.27), channel_id=1, source_target_pairs={{8,16},{9,17},{10,18},{11,19},{12,20},{13,21},{14,22},{15,23},{16,... | collective-permute-start | bytes 3145736 | tf_op jit(solution)/shard_map/ppermute | solution.py:344
  33.2 2.2 %collective-permute-start.4 = (f32[8,256,128]{2,1,0:T(8,128)S(1)}, f32[8,256,128]{2,1,0:T(8,128)S(1)}, u32[]{:S(2)}, u32[]{:S(2)}) collective-permute-start(f32[8,256,128]{2,1,0:T(8,128)S(1)} %get-tuple-element.28), channel_id=1, source_target_pairs={{2,4},{3,5},{10,12},{11,13},{18,20},{19,21},{26,28},{27,29},{4,2},... | collective-permute-start | bytes 3145736 | tf_op jit(solution)/shard_map/ppermute | solution.py:344
  35.4 11.1 %collective-permute-done.6 = f32[8,256,128]{2,1,0:T(8,128)S(1)} collective-permute-done((f32[8,256,128]{2,1,0:T(8,128)S(1)}, f32[8,256,128]{2,1,0:T(8,128)S(1)}, u32[]{:S(2)}, u32[]{:S(2)}) %collective-permute-start.6) | collective-permute-done | bytes 1048608 | tf_op jit(solution)/shard_map/ppermute | solution.py:344
  46.6 3.1 %collective-permute-start.10 = (f32[4,256,128]{2,1,0:T(8,128)S(1)}, f32[4,256,128]{2,1,0:T(8,128)S(1)}, u32[]{:S(2)}, u32[]{:S(2)}) collective-permute-start(f32[4,256,128]{2,1,0:T(8,128)S(1)} %get-tuple-element.47), channel_id=1, source_target_pairs={{2,4},{3,5},{10,12},{11,13},{18,20},{19,21},{26,28},{27,29},{4,2},... | collective-permute-start | bytes 1572872 | tf_op jit(solution)/shard_map/ppermute | solution.py:344
  49.7 8.1 %collective-permute-done.3 = f32[8,256,128]{2,1,0:T(8,128)S(1)} collective-permute-done((f32[8,256,128]{2,1,0:T(8,128)S(1)}, f32[8,256,128]{2,1,0:T(8,128)S(1)}, u32[]{:S(2)}, u32[]{:S(2)}) %collective-permute-start.3) | collective-permute-done | bytes 1048608 | tf_op jit(solution)/shard_map/ppermute | solution.py:344
  57.8 2.6 %collective-permute-done.4 = f32[8,256,128]{2,1,0:T(8,128)S(1)} collective-permute-done((f32[8,256,128]{2,1,0:T(8,128)S(1)}, f32[8,256,128]{2,1,0:T(8,128)S(1)}, u32[]{:S(2)}, u32[]{:S(2)}) %collective-permute-start.4) | collective-permute-done | bytes 1048608 | tf_op jit(solution)/shard_map/ppermute | solution.py:344
  62.1 9.5 %collective-permute-done.10 = f32[4,256,128]{2,1,0:T(8,128)S(1)} collective-permute-done((f32[4,256,128]{2,1,0:T(8,128)S(1)}, f32[4,256,128]{2,1,0:T(8,128)S(1)}, u32[]{:S(2)}, u32[]{:S(2)}) %collective-permute-start.10) | collective-permute-done | bytes 524320 | tf_op jit(solution)/shard_map/ppermute | solution.py:344
  76.9 2.4 %collective-permute-start.12 = (f32[2,256,128]{2,1,0:T(8,128)S(1)}, f32[2,256,128]{2,1,0:T(8,128)S(1)}, u32[]{:S(2)}, u32[]{:S(2)}) collective-permute-start(f32[2,256,128]{2,1,0:T(8,128)S(1)} %get-tuple-element.57), channel_id=1, source_target_pairs={{8,16},{9,17},{10,18},{11,19},{12,20},{13,21},{14,22},{15,23},{16,... | collective-permute-start | bytes 786440 | tf_op jit(solution)/shard_map/ppermute | solution.py:344
  79.4 2.1 %collective-permute-start.13 = (f32[2,280,128]{2,1,0:T(8,128)S(1)}, f32[2,280,128]{2,1,0:T(8,128)S(1)}, u32[]{:S(2)}, u32[]{:S(2)}) collective-permute-start(f32[2,280,128]{2,1,0:T(8,128)S(1)} %get-tuple-element.53), channel_id=1, source_target_pairs={{0,2},{1,3},{8,10},{9,11},{16,18},{17,19},{24,26},{25,27},{2,0},{3... | collective-permute-start | bytes 860168 | tf_op jit(solution)/shard_map/ppermute | solution.py:344
  81.5 2.3 %collective-permute-start.11 = (f32[2,256,128]{2,1,0:T(8,128)S(1)}, f32[2,256,128]{2,1,0:T(8,128)S(1)}, u32[]{:S(2)}, u32[]{:S(2)}) collective-permute-start(f32[2,256,128]{2,1,0:T(8,128)S(1)} %get-tuple-element.58), channel_id=1, source_target_pairs={{2,4},{3,5},{10,12},{11,13},{18,20},{19,21},{26,28},{27,29},{4,2},... | collective-permute-start | bytes 786440 | tf_op jit(solution)/shard_map/ppermute | solution.py:344
  84.6 2.2 %collective-permute-done.12 = f32[2,256,128]{2,1,0:T(8,128)S(1)} collective-permute-done((f32[2,256,128]{2,1,0:T(8,128)S(1)}, f32[2,256,128]{2,1,0:T(8,128)S(1)}, u32[]{:S(2)}, u32[]{:S(2)}) %collective-permute-start.12) | collective-permute-done | bytes 262176 | tf_op jit(solution)/shard_map/ppermute | solution.py:344
  86.9 2.7 %collective-permute-done.11 = f32[2,256,128]{2,1,0:T(8,128)S(1)} collective-permute-done((f32[2,256,128]{2,1,0:T(8,128)S(1)}, f32[2,256,128]{2,1,0:T(8,128)S(1)}, u32[]{:S(2)}, u32[]{:S(2)}) %collective-permute-start.11) | collective-permute-done | bytes 262176 | tf_op jit(solution)/shard_map/ppermute | solution.py:344
  89.9 2.2 %collective-permute-start.17 = (f32[1,280,128]{2,1,0:T(8,128)S(1)}, f32[1,280,128]{2,1,0:T(8,128)S(1)}, u32[]{:S(2)}, u32[]{:S(2)}) collective-permute-start(f32[1,280,128]{2,1,0:T(8,128)S(1)} %slice_add_fusion.17), channel_id=1, source_target_pairs={{2,4},{3,5},{10,12},{11,13},{18,20},{19,21},{26,28},{27,29},{4,2},... | collective-permute-start | bytes 430088 | tf_op jit(solution)/shard_map/ppermute | solution.py:344
  92.1 2.9 %collective-permute-start.25 = (f32[256,128]{1,0:T(8,128)S(1)}, f32[256,128]{1,0:T(8,128)S(1)}, u32[]{:S(2)}, u32[]{:S(2)}) collective-permute-start(f32[256,128]{1,0:T(8,128)S(1)} %fusion.3), channel_id=1, source_target_pairs={{32,64},{64,32},{96,0},{0,96},{33,65},{65,33},{97,1},{1,97},{34,66... | collective-permute-start | bytes 393224 | tf_op jit(solution)/shard_map/ppermute | solution.py:357
  98.5 2.8 %collective-permute-start.21 = (f32[256,128]{1,0:T(8,128)S(1)}, f32[256,128]{1,0:T(8,128)S(1)}, u32[]{:S(2)}, u32[]{:S(2)}) collective-permute-start(f32[256,128]{1,0:T(8,128)S(1)} %fusion.5), channel_id=1, source_target_pairs={{32,64},{64,32},{96,0},{0,96},{33,65},{65,33},{97,1},{1,97},{34,66... | collective-permute-start | bytes 393224 | tf_op jit(solution)/shard_map/ppermute | solution.py:357
  101.4 2.9 %collective-permute-done.23 = f32[280,128]{1,0:T(8,128)S(1)} collective-permute-done((f32[280,128]{1,0:T(8,128)S(1)}, f32[280,128]{1,0:T(8,128)S(1)}, u32[]{:S(2)}, u32[]{:S(2)}) %collective-permute-start.23) | collective-permute-done | bytes 143392 | tf_op jit(solution)/shard_map/ppermute | solution.py:357
  104.2 3.7 %collective-permute-start.24 = (f32[280,128]{1,0:T(8,128)S(1)}, f32[280,128]{1,0:T(8,128)S(1)}, u32[]{:S(2)}, u32[]{:S(2)}) collective-permute-start(f32[280,128]{1,0:T(8,128)S(1)} %add.147.left), channel_id=1, source_target_pairs={{32,64},{64,32},{96,0},{0,96},{33,65},{65,33},{97,1},{1,97},{34,66... | collective-permute-start | bytes 430088 | tf_op jit(solution)/shard_map/ppermute | solution.py:358
  110.3 2.7 %collective-permute-done.26.right_got = f32[256,128]{1,0:T(8,128)S(1)} collective-permute-done((f32[256,128]{1,0:T(8,128)S(1)}, f32[256,128]{1,0:T(8,128)S(1)}, u32[]{:S(2)}, u32[]{:S(2)}) %collective-permute-start.26) | collective-permute-done | bytes 131104 | tf_op jit(solution)/shard_map/ppermute | solution.py:358
  113.0 1.7 %cover.1 = (f32[256,256]{1,0:T(8,128)}, f32[256,256]{1,0:T(8,128)S(1)}) custom-call(f32[280,128]{1,0:T(8,128)S(1)} %add.147.left, f32[280,128]{1,0:T(8,128)S(1)} %collective-permute-done.24.left_got, f32[256,128]{1,0:T(8,128)S(1)} %add.151.right, f32[256,128]{1,0:T(8,128)S(1)} %collective-permute-done.26.right_got), custom_call_target="tpu_custom_call" | custom-call | flops 1000000000 | bytes 1048576 | tf_op jit(solution)/shard_map/cover/pallas_call | solution.py:317
  (63 shorter events, 17.7 us)
Async XLA Ops:
  2.7 8.3 %collective-permute-start = (f32[16,128]{1,0:T(8,128)}, f32[16,128]{1,0:T(8,128)S(1)}, u32[]{:S(2)}, u32[]{:S(2)}) collective-permute-start(f32[16,128]{1,0:T(8,128)} %pack.1.refs_1_), channel_id=1, source_target_pairs={{0,1},{1,0},{2,3},{3,2},{4,5},{5,4},{6,7},{7,6},{8,9},{9,8},{10,11... | collective-permute-start | bytes 24584 | tf_op jit(solution)/shard_map/ppermute | solution.py:372
  2.7 8.4 %collective-permute-start.1 = (f32[32,128,128]{2,1,0:T(8,128)}, f32[32,128,128]{2,1,0:T(8,128)S(1)}, u32[]{:S(2)}, u32[]{:S(2)}) collective-permute-start(f32[32,128,128]{2,1,0:T(8,128)} %refs_3_.1), channel_id=1, source_target_pairs={{0,1},{1,0},{2,3},{3,2},{4,5},{5,4},{6,7},{7,6},{8,9},{9,8},{10,11... | collective-permute-start | bytes 6291464 | tf_op jit(solution)/shard_map/ppermute | solution.py:370
  10.9 13.2 %collective-permute-start.2 = (f32[32,128,128]{2,1,0:T(8,128)S(1)}, f32[32,128,128]{2,1,0:T(8,128)S(1)}, u32[]{:S(2)}, u32[]{:S(2)}) collective-permute-start(f32[32,128,128]{2,1,0:T(8,128)S(1)} %match.1.refs_3_), channel_id=1, source_target_pairs={{0,1},{1,0},{2,3},{3,2},{4,5},{5,4},{6,7},{7,6},{8,9},{9,8},{10,11... | collective-permute-start | bytes 6291464 | tf_op jit(solution)/shard_map/ppermute | solution.py:375
  20.4 26.0 %collective-permute-start.6 = (f32[8,256,128]{2,1,0:T(8,128)S(1)}, f32[8,256,128]{2,1,0:T(8,128)S(1)}, u32[]{:S(2)}, u32[]{:S(2)}) collective-permute-start(f32[8,256,128]{2,1,0:T(8,128)S(1)} %get-tuple-element.30), channel_id=1, source_target_pairs={{0,2},{1,3},{8,10},{9,11},{16,18},{17,19},{24,26},{25,27},{2,0},{3... | collective-permute-start | bytes 3145736 | tf_op jit(solution)/shard_map/ppermute | solution.py:344
  22.1 38.3 %collective-permute-start.5 = (f32[8,280,128]{2,1,0:T(8,128)S(1)}, f32[8,280,128]{2,1,0:T(8,128)S(1)}, u32[]{:S(2)}, u32[]{:S(2)}) collective-permute-start(f32[8,280,128]{2,1,0:T(8,128)S(1)} %get-tuple-element.29), channel_id=1, source_target_pairs={{0,8},{1,9},{2,10},{3,11},{4,12},{5,13},{6,14},{7,15},{8,0},{9,1},... | collective-permute-start | bytes 3440648 | tf_op jit(solution)/shard_map/ppermute | solution.py:344
  30.6 27.2 %collective-permute-start.3 = (f32[8,256,128]{2,1,0:T(8,128)S(1)}, f32[8,256,128]{2,1,0:T(8,128)S(1)}, u32[]{:S(2)}, u32[]{:S(2)}) collective-permute-start(f32[8,256,128]{2,1,0:T(8,128)S(1)} %get-tuple-element.27), channel_id=1, source_target_pairs={{8,16},{9,17},{10,18},{11,19},{12,20},{13,21},{14,22},{15,23},{16,... | collective-permute-start | bytes 3145736 | tf_op jit(solution)/shard_map/ppermute | solution.py:344
  33.2 27.2 %collective-permute-start.4 = (f32[8,256,128]{2,1,0:T(8,128)S(1)}, f32[8,256,128]{2,1,0:T(8,128)S(1)}, u32[]{:S(2)}, u32[]{:S(2)}) collective-permute-start(f32[8,256,128]{2,1,0:T(8,128)S(1)} %get-tuple-element.28), channel_id=1, source_target_pairs={{2,4},{3,5},{10,12},{11,13},{18,20},{19,21},{26,28},{27,29},{4,2},... | collective-permute-start | bytes 3145736 | tf_op jit(solution)/shard_map/ppermute | solution.py:344
  46.6 25.0 %collective-permute-start.10 = (f32[4,256,128]{2,1,0:T(8,128)S(1)}, f32[4,256,128]{2,1,0:T(8,128)S(1)}, u32[]{:S(2)}, u32[]{:S(2)}) collective-permute-start(f32[4,256,128]{2,1,0:T(8,128)S(1)} %get-tuple-element.47), channel_id=1, source_target_pairs={{2,4},{3,5},{10,12},{11,13},{18,20},{19,21},{26,28},{27,29},{4,2},... | collective-permute-start | bytes 1572872 | tf_op jit(solution)/shard_map/ppermute | solution.py:344
  60.5 13.8 %collective-permute-start.8 = (f32[4,256,128]{2,1,0:T(8,128)S(1)}, f32[4,256,128]{2,1,0:T(8,128)S(1)}, u32[]{:S(2)}, u32[]{:S(2)}) collective-permute-start(f32[4,256,128]{2,1,0:T(8,128)S(1)} %get-tuple-element.49), channel_id=1, source_target_pairs={{0,2},{1,3},{8,10},{9,11},{16,18},{17,19},{24,26},{25,27},{2,0},{3... | collective-permute-start | bytes 1572872 | tf_op jit(solution)/shard_map/ppermute | solution.py:344
  60.8 16.1 %collective-permute-start.9 = (f32[4,280,128]{2,1,0:T(8,128)S(1)}, f32[4,280,128]{2,1,0:T(8,128)S(1)}, u32[]{:S(2)}, u32[]{:S(2)}) collective-permute-start(f32[4,280,128]{2,1,0:T(8,128)S(1)} %get-tuple-element.45), channel_id=1, source_target_pairs={{8,16},{9,17},{10,18},{11,19},{12,20},{13,21},{14,22},{15,23},{16,... | collective-permute-start | bytes 1720328 | tf_op jit(solution)/shard_map/ppermute | solution.py:344
  61.7 14.3 %collective-permute-start.7 = (f32[4,256,128]{2,1,0:T(8,128)S(1)}, f32[4,256,128]{2,1,0:T(8,128)S(1)}, u32[]{:S(2)}, u32[]{:S(2)}) collective-permute-start(f32[4,256,128]{2,1,0:T(8,128)S(1)} %get-tuple-element.50), channel_id=1, source_target_pairs={{0,8},{1,9},{2,10},{3,11},{4,12},{5,13},{6,14},{7,15},{8,0},{9,1},... | collective-permute-start | bytes 1572872 | tf_op jit(solution)/shard_map/ppermute | solution.py:344
  71.6 12.2 %collective-permute-start.14 = (f32[2,256,128]{2,1,0:T(8,128)S(1)}, f32[2,256,128]{2,1,0:T(8,128)S(1)}, u32[]{:S(2)}, u32[]{:S(2)}) collective-permute-start(f32[2,256,128]{2,1,0:T(8,128)S(1)} %get-tuple-element.55), channel_id=1, source_target_pairs={{0,8},{1,9},{2,10},{3,11},{4,12},{5,13},{6,14},{7,15},{8,0},{9,1},... | collective-permute-start | bytes 786440 | tf_op jit(solution)/shard_map/ppermute | solution.py:344
  76.9 9.9 %collective-permute-start.12 = (f32[2,256,128]{2,1,0:T(8,128)S(1)}, f32[2,256,128]{2,1,0:T(8,128)S(1)}, u32[]{:S(2)}, u32[]{:S(2)}) collective-permute-start(f32[2,256,128]{2,1,0:T(8,128)S(1)} %get-tuple-element.57), channel_id=1, source_target_pairs={{8,16},{9,17},{10,18},{11,19},{12,20},{13,21},{14,22},{15,23},{16,... | collective-permute-start | bytes 786440 | tf_op jit(solution)/shard_map/ppermute | solution.py:344
  79.4 10.2 %collective-permute-start.13 = (f32[2,280,128]{2,1,0:T(8,128)S(1)}, f32[2,280,128]{2,1,0:T(8,128)S(1)}, u32[]{:S(2)}, u32[]{:S(2)}) collective-permute-start(f32[2,280,128]{2,1,0:T(8,128)S(1)} %get-tuple-element.53), channel_id=1, source_target_pairs={{0,2},{1,3},{8,10},{9,11},{16,18},{17,19},{24,26},{25,27},{2,0},{3... | collective-permute-start | bytes 860168 | tf_op jit(solution)/shard_map/ppermute | solution.py:344
  81.5 8.1 %collective-permute-start.11 = (f32[2,256,128]{2,1,0:T(8,128)S(1)}, f32[2,256,128]{2,1,0:T(8,128)S(1)}, u32[]{:S(2)}, u32[]{:S(2)}) collective-permute-start(f32[2,256,128]{2,1,0:T(8,128)S(1)} %get-tuple-element.58), channel_id=1, source_target_pairs={{2,4},{3,5},{10,12},{11,13},{18,20},{19,21},{26,28},{27,29},{4,2},... | collective-permute-start | bytes 786440 | tf_op jit(solution)/shard_map/ppermute | solution.py:344
  83.8 8.3 %collective-permute-start.18 = (f32[1,256,128]{2,1,0:T(8,128)S(1)}, f32[1,256,128]{2,1,0:T(8,128)S(1)}, u32[]{:S(2)}, u32[]{:S(2)}) collective-permute-start(f32[1,256,128]{2,1,0:T(8,128)S(1)} %slice_add_fusion.20), channel_id=1, source_target_pairs={{8,16},{9,17},{10,18},{11,19},{12,20},{13,21},{14,22},{15,23},{16,... | collective-permute-start | bytes 393224 | tf_op jit(solution)/shard_map/ppermute | solution.py:344
  89.6 5.4 %collective-permute-start.16 = (f32[1,256,128]{2,1,0:T(8,128)S(1)}, f32[1,256,128]{2,1,0:T(8,128)S(1)}, u32[]{:S(2)}, u32[]{:S(2)}) collective-permute-start(f32[1,256,128]{2,1,0:T(8,128)S(1)} %slice_add_fusion.21), channel_id=1, source_target_pairs={{0,8},{1,9},{2,10},{3,11},{4,12},{5,13},{6,14},{7,15},{8,0},{9,1},... | collective-permute-start | bytes 393224 | tf_op jit(solution)/shard_map/ppermute | solution.py:344
  89.9 6.4 %collective-permute-start.17 = (f32[1,280,128]{2,1,0:T(8,128)S(1)}, f32[1,280,128]{2,1,0:T(8,128)S(1)}, u32[]{:S(2)}, u32[]{:S(2)}) collective-permute-start(f32[1,280,128]{2,1,0:T(8,128)S(1)} %slice_add_fusion.17), channel_id=1, source_target_pairs={{2,4},{3,5},{10,12},{11,13},{18,20},{19,21},{26,28},{27,29},{4,2},... | collective-permute-start | bytes 430088 | tf_op jit(solution)/shard_map/ppermute | solution.py:344
  92.1 15.8 %collective-permute-start.25 = (f32[256,128]{1,0:T(8,128)S(1)}, f32[256,128]{1,0:T(8,128)S(1)}, u32[]{:S(2)}, u32[]{:S(2)}) collective-permute-start(f32[256,128]{1,0:T(8,128)S(1)} %fusion.3), channel_id=1, source_target_pairs={{32,64},{64,32},{96,0},{0,96},{33,65},{65,33},{97,1},{1,97},{34,66... | collective-permute-start | bytes 393224 | tf_op jit(solution)/shard_map/ppermute | solution.py:357
  96.3 11.9 %collective-permute-start.19 = (f32[256,128]{1,0:T(8,128)S(1)}, f32[256,128]{1,0:T(8,128)S(1)}, u32[]{:S(2)}, u32[]{:S(2)}) collective-permute-start(f32[256,128]{1,0:T(8,128)S(1)} %fusion.7), channel_id=1, source_target_pairs={{0,32},{32,0},{64,96},{96,64},{1,33},{33,1},{65,97},{97,65},{2,34}... | collective-permute-start | bytes 393224 | tf_op jit(solution)/shard_map/ppermute | solution.py:357
  97.7 6.5 %collective-permute-start.23 = (f32[280,128]{1,0:T(8,128)S(1)}, f32[280,128]{1,0:T(8,128)S(1)}, u32[]{:S(2)}, u32[]{:S(2)}) collective-permute-start(f32[280,128]{1,0:T(8,128)S(1)} %fusion.1), channel_id=1, source_target_pairs={{0,32},{32,0},{64,96},{96,64},{1,33},{33,1},{65,97},{97,65},{2,34}... | collective-permute-start | bytes 430088 | tf_op jit(solution)/shard_map/ppermute | solution.py:357
  98.5 11.0 %collective-permute-start.21 = (f32[256,128]{1,0:T(8,128)S(1)}, f32[256,128]{1,0:T(8,128)S(1)}, u32[]{:S(2)}, u32[]{:S(2)}) collective-permute-start(f32[256,128]{1,0:T(8,128)S(1)} %fusion.5), channel_id=1, source_target_pairs={{32,64},{64,32},{96,0},{0,96},{33,65},{65,33},{97,1},{1,97},{34,66... | collective-permute-start | bytes 393224 | tf_op jit(solution)/shard_map/ppermute | solution.py:357
  104.2 8.7 %collective-permute-start.24 = (f32[280,128]{1,0:T(8,128)S(1)}, f32[280,128]{1,0:T(8,128)S(1)}, u32[]{:S(2)}, u32[]{:S(2)}) collective-permute-start(f32[280,128]{1,0:T(8,128)S(1)} %add.147.left), channel_id=1, source_target_pairs={{32,64},{64,32},{96,0},{0,96},{33,65},{65,33},{97,1},{1,97},{34,66... | collective-permute-start | bytes 430088 | tf_op jit(solution)/shard_map/ppermute | solution.py:358
  108.2 6.4 %collective-permute-start.20 = (f32[256,128]{1,0:T(8,128)S(1)}, f32[256,128]{1,0:T(8,128)S(1)}, u32[]{:S(2)}, u32[]{:S(2)}) collective-permute-start(f32[256,128]{1,0:T(8,128)S(1)} %add.139.left), channel_id=1, source_target_pairs={{32,64},{64,32},{96,0},{0,96},{33,65},{65,33},{97,1},{1,97},{34,66... | collective-permute-start | bytes 393224 | tf_op jit(solution)/shard_map/ppermute | solution.py:358
  (6 other events, 39.0 us)

commit v4 on v3

--- a/solution.py
+++ b/solution.py
@@ -23,7 +23,7 @@
 EMPTY = 1 << 24
 UNROLL = 2
 MATCH_UNROLL = 8
-CHUNKS = 2
+CHUNKS = 4
 MATCH_COST = 100_000_000_000
 WARP_COST = 10_000_000_000
 
@@ -33,26 +33,57 @@
     return high, (x - high.astype(F32)).astype(BF16)
 
 
-def pack_kernel(mine, intersections, boxes, shifts, out):
+def here():
+    patch = lax.axis_index("patch")
+    z, y = patch >> 3, (patch >> 1) & 3
+    chip = lax.axis_index("visit") * 16 + z * 4 + y
+    return place_code(z, y), patch & 1, chip
+
+
+def place_code(z, y):
+    z, y = z ^ (z >> 1), y ^ (y >> 1)
+    return ((z & 1) << 3) | ((z >> 1) << 2) | ((y & 1) << 1) | (y >> 1)
+
+
+def pack_kernel(intersections, boxes, shifts, out):
+    mine = here()[0]
     out[...] = jnp.zeros_like(out)
-    z, y, core = intersections[...] >> 3, (intersections[...] >> 1) & 3, intersections[...] & 1
-    z, y = z ^ (z >> 1), y ^ (y >> 1)
-    code = ((z & 1) << 3) | ((z >> 1) << 2) | ((y & 1) << 1) | (y >> 1)
-    out[0:2, 0:TILES] = ((code ^ mine[0]) + 16 * core).astype(F32)
+    earlier_item = lax.broadcasted_iota(jnp.int32, (TILES, TILES), 0)
+    item = lax.broadcasted_iota(jnp.int32, (TILES, TILES), 1)
+    dest = [intersections[route : route + 1, :] for route in range(2)]
+
+    def earlier(rows):
+        columns = [jnp.sum(jnp.where(earlier_item == item, row, 0), axis=1, keepdims=True) for row in rows]
+        counts = []
+        for route, row in enumerate(rows):
+            same = jnp.where((columns[route] == row) & (earlier_item < item), 1, 0)
+            if route == 1:
+                same = same + jnp.where(columns[0] == row, 1, 0)
+            counts.append(jnp.sum(same, axis=0, keepdims=True))
+        return counts
+
+    slots, places = earlier(dest), earlier([d & 1 for d in dest])
     for route in range(2):
+        d = dest[route]
+        code = place_code(d >> 3, (d >> 1) & 3) ^ mine
+        out[route : route + 1, 0:TILES] = (code + (slots[route] << 4) + ((d & 1) << 8)).astype(F32)
+        out[10 + route : 11 + route, 0:TILES] = places[route].astype(F32)
         out[2 + 2 * route : 4 + 2 * route, 0:TILES] = boxes[route].astype(F32)
         out[6 + 2 * route : 8 + 2 * route, 0:TILES] = shifts[route]
-
-
-def pack(mine, intersections, boxes, shifts):
+    second = jnp.sum(intersections[...] & 1).astype(F32)
+    lane = lax.broadcasted_iota(jnp.int32, (1, TS), 1)
+    out[12:13, :] = jnp.where(lane == 0, ROUTES - second, second)
+
+
+def pack(intersections, boxes, shifts):
     vmem = pl.BlockSpec(memory_space=pltpu.VMEM)
     return pl.pallas_call(
         pack_kernel,
         out_shape=jax.ShapeDtypeStruct((16, TS), F32),
-        in_specs=[pl.BlockSpec(memory_space=pltpu.SMEM)] + [vmem] * 3,
+        in_specs=[vmem] * 3,
         out_specs=vmem,
         name="pack",
-    )(mine, intersections.T, boxes.transpose(1, 2, 0), shifts.transpose(1, 2, 0))
+    )(intersections.T, boxes.transpose(1, 2, 0), shifts.transpose(1, 2, 0))
 
 
 def match_kernel(
@@ -136,13 +167,13 @@
 
 
 def warp_kernel(with_meta, *refs):
-    first, own, other, own_tiles, other_tiles = refs[:5]
-    outs = refs[5:9]
     if with_meta:
-        slots = refs[9]
-        stage, acc, meta, weights, counts, seen = refs[10:]
+        own, other, own_tiles, other_tiles = refs[:4]
+        outs, slots = refs[4:8], refs[8]
+        stage, acc, meta, weights = refs[9:]
     else:
-        slots = first
+        slots, own, other, own_tiles, other_tiles = refs[:5]
+        outs = refs[5:9]
         stage, acc = refs[9:]
     lane = lax.broadcasted_iota(jnp.int32, (8, TS), 1)
     stage[:, :, 0:8, :] = jnp.zeros((2 * UNROLL, 2, 8, TS), F32)
@@ -152,43 +183,30 @@
             acc[4 * k + side, PAD : PAD + PATCH, :] = jnp.zeros((PATCH, TS), F32)
 
     if with_meta:
-        core, chip = first[1], first[2]
+        _, core, chip = here()
         meta[...] = jnp.zeros_like(meta)
-        for side in range(2):
-            counts[side] = 0
-            for k in range(17):
-                seen[side, k] = 0
-
-        for route in range(2):
-
-            @pl.loop(0, TILES)
-            def _(t, route=route):
-                for side, table in ((0, own), (1, other)):
-                    k = table[route, t].astype(jnp.int32) - 16 * core
-                    ours = (k >= 0) & (k < 16)
-                    k = jnp.where(ours, k, 16)
-                    slot, n = seen[side, k], counts[side]
-                    slots[side, 1 + n] = (k << 16) + (slot << 8) + (2 * t + route)
-                    seen[side, k] = slot + 1
-                    counts[side] = n + ours.astype(jnp.int32)
-
-        for side in range(2):
-            n = counts[side]
+
+        @pl.loop(0, TILES, step=8)
+        def _(first):
+            for side, table, tiles in ((0, own, own_tiles), (1, other, other_tiles)):
+                for route in range(2):
+                    for t in [first + u for u in range(8)]:
+                        what = table[route, t].astype(jnp.int32)
+                        at = jnp.where((what >> 8) == core, table[10 + route, t].astype(jnp.int32) + 1, 127)
+                        slots[side, at] = (what << 8) + (2 * t + route)
+                sums = jnp.concatenate([jnp.sum(tiles[first + u], axis=0, keepdims=True) for u in range(8)], 0)
+                sums = jnp.sum(sums, axis=1, keepdims=True)
+                at = pl.multiple_of(side * TILES + first, 8)
+                weights[pl.ds(at, 8), :] = jnp.broadcast_to(float(TS * TS) / sums, (8, TS))
+
+        for side, table in ((0, own), (1, other)):
+            n = table[12, core].astype(jnp.int32)
             slots[side, 0] = n
             for u in range(3 * UNROLL):
                 slots[side, 1 + n + u] = EMPTY
 
-        for side, tiles in ((0, own_tiles), (1, other_tiles)):
-
-            @pl.loop(0, TILES, step=8)
-            def _(t, side=side, tiles=tiles):
-                sums = jnp.concatenate([jnp.sum(tiles[t + u], axis=0, keepdims=True) for u in range(8)], 0)
-                sums = jnp.sum(sums, axis=1, keepdims=True)
-                at = pl.multiple_of(side * TILES + t, 8)
-                weights[pl.ds(at, 8), :] = jnp.broadcast_to(float(TS * TS) / sums, (8, TS))
-
     def place(entry, u, side, table, tiles):
-        item, slot, k = entry & 255, (entry >> 8) & 255, (entry >> 16) & 15
+        item, k, slot = entry & 255, (entry >> 8) & 15, (entry >> 12) & 3
         t, route = item >> 1, item & 1
         row, col = table[2 + 2 * route, t].astype(jnp.int32), table[3 + 2 * route, t].astype(jnp.int32)
         frac_row, frac_col = table[6 + 2 * route, t], table[7 + 2 * route, t]
@@ -245,15 +263,15 @@
         if not with_meta:
             z_first, z_second, y_first, y_second = z_second, z_first, y_second, y_first
         left, right = outs[z_first], outs[2 + y_first]
-        at = z_second * 4 + y_first * 2 + y_second
+        at = y_first * 4 + z_second * 2 + y_second
         left[at, 0:PATCH, :] = acc[4 * k + 1, PAD : PAD + PATCH, :]
         if with_meta:
             for slot in range(CAP):
                 left[at, PATCH + 8 * slot : PATCH + 8 * slot + 8, :] = meta[k * CAP + slot]
-        right[y_second * 4 + z_first * 2 + z_second, :, :] = acc[4 * k + 2, PAD : PAD + PATCH, :]
-
-
-def warp(with_meta, first, own, other, own_tiles, other_tiles):
+        right[z_first * 4 + y_second * 2 + z_second, :, :] = acc[4 * k + 2, PAD : PAD + PATCH, :]
+
+
+def warp(with_meta, *args):
     smem, vmem = pl.BlockSpec(memory_space=pltpu.SMEM), pl.BlockSpec(memory_space=pltpu.VMEM)
     rows = PATCH + META if with_meta else PATCH
     left = jax.ShapeDtypeStruct((8, rows, TS), F32)
@@ -268,19 +286,17 @@
         scratch += [
             pltpu.VMEM((16 * CAP, 8, TS), F32),
             pltpu.VMEM((2 * TILES, TS), F32),
-            pltpu.SMEM((2,), jnp.int32),
-            pltpu.SMEM((2, 17), jnp.int32),
         ]
     return pl.pallas_call(
         functools.partial(warp_kernel, with_meta),
         out_shape=outs,
-        in_specs=[smem] * 3 + [vmem] * 2,
+        in_specs=[smem] * (len(args) - 2) + [vmem] * 2,
         out_specs=specs,
         scratch_shapes=scratch,
         compiler_params=pltpu.CompilerParams(vmem_limit_bytes=40 << 20),
         cost_estimate=pl.CostEstimate(flops=WARP_COST, bytes_accessed=8 << 20, transcendentals=0),
         name="warp_meta" if with_meta else "warp",
-    )(first, own, other, own_tiles, other_tiles)
+    )(*args)
 
 
 def cover_kernel(left, left_got, right, right_got, coadd_var, safe_ref):
@@ -339,18 +355,19 @@
 
 
 def halve(left, right, orders, ahead=()):
-    parts, received = [left, right], []
+    parts, left_over = [left, right], []
     for step in range(4):
         got = [lax.ppermute(send, "patch", over_patch(*order[step])) for (_, send), order in zip(parts, orders)]
         if step < len(ahead):
             got = lax.optimization_barrier((*got, *ahead[step]))[:2]
-        received.append(tuple(got))
         if step < 3:
             n = 8 >> (step + 1)
             parts = [(keep[:n] + g[:n], keep[n:] + g[n:]) for (keep, _), g in zip(parts, got)]
+            left_over.append([send for _, send in parts])
         else:
             parts = [keep[0] + g[0] for (keep, _), g in zip(parts, got)]
-    return parts, received
+            left_over.append(parts)
+    return parts, left_over
 
 
 def double(left, right):
@@ -360,29 +377,22 @@
 
 def shards(image, variance, intersections, boxes, shifts, basis_ids, coefs, taps):
     swap = [(i, i ^ 1) for i in range(32)]
-    patch = lax.axis_index("patch")
-    z, y = patch >> 3, (patch >> 1) & 3
-    chip = lax.axis_index("visit") * 16 + z * 4 + y
-    z, y = z ^ (z >> 1), y ^ (y >> 1)
-    mine = ((z & 1) << 3) | ((z >> 1) << 2) | ((y & 1) << 1) | (y >> 1)
-    where = jnp.stack([mine, patch & 1, chip])
-
     other_variance = lax.ppermute(variance, "patch", swap)
-    table = pack(where, intersections, boxes, shifts)
+    table = pack(intersections, boxes, shifts)
     other_table = lax.ppermute(table, "patch", swap)
     matched = match(basis_ids, coefs, taps, image, variance)
     matched, other_table = lax.optimization_barrier((matched, other_table))
     other_matched = lax.ppermute(matched, "patch", swap)
     var_left_keep, var_left_send, var_right_keep, var_right_send, slots = warp(
-        True, where, table, other_table, variance, other_variance
+        True, table, other_table, variance, other_variance
     )
     num_left_keep, num_left_send, num_right_keep, num_right_send = warp(
         False, slots, table, other_table, matched, other_matched
     )
     z1, z2, y1, y2 = ("z", 0), ("z", 1), ("y", 0), ("y", 1)
-    var, ahead = halve((var_left_keep, var_left_send), (var_right_keep, var_right_send), ((z1, z2, y1, y2), (y1, y2, z1, z2)))
+    var, ahead = halve((var_left_keep, var_left_send), (var_right_keep, var_right_send), ((z1, y1, z2, y2), (y1, z1, y2, z2)))
     num, _ = halve(
-        (num_left_keep, num_left_send), (num_right_keep, num_right_send), ((z2, z1, y2, y1), (y2, y1, z2, z1)), ahead
+        (num_left_keep, num_left_send), (num_right_keep, num_right_send), ((z2, y2, z1, y1), (y2, z2, y1, z1)), ahead
     )
     var, num = double(*var), double(*num)
     coadd_var, safe = finish(cover_kernel, "cover", 2, *var)

time: 114 us -> 110 us (0.965); the launches traced: 115 us -> 109 us
  starting transfers between devices: 38.4 us -> 35.2 us
  waiting for transfers between devices: 47.1 us -> 44 us
    ppermute x8, starting transfers between devices: 13.8 us -> 10.9 us  [double(): lax.ppermute(x, 'visit', EDGES[first])]
    ppermute x16, waiting for transfers between devices: 41.5 us -> 38.8 us  [halve(): lax.ppermute(send, 'patch', over_patch(*order[step]))]
  transfers between devices with their start and end apart: 27 -> 27, of which waited for: 12 -> 16; matrix products, arithmetic and copies ran while one was open for 1% -> 1% of each run, Pallas kernels for 22% -> 23%
where the time goes in v4:
time: 110 us; the launch traced here: 109 us
  waiting for transfers between devices  44 us (40%)
  starting transfers between devices  35.2 us (32%)
  Pallas kernels  27.7 us (25%)
    ppermute x16, waiting for transfers between devices, halve(): lax.ppermute(send, 'patch', over_patch(*order[step]))  38.8 us
    ppermute x16, starting transfers between devices, halve(): lax.ppermute(send, 'patch', over_patch(*order[step]))  23.7 us
    pallas_call x2, Pallas kernels, warp(): pl.pallas_call(functools.partial(warp_kernel, with_meta), out_shape=outs,...  15.8 us
    ppermute x8, starting transfers between devices, double(): lax.ppermute(x, 'visit', EDGES[first])  10.9 us
    pallas_call x1, Pallas kernels, match(): pl.pallas_call(match_kernel, out_shape=jax.ShapeDtypeStruct((TILES, TS, T...  8.04 us
    ppermute x8, waiting for transfers between devices, double(): lax.ppermute(x, 'visit', EDGES[first])  5.23 us
    pallas_call x2, Pallas kernels, finish(): pl.pallas_call(kernel, out_shape=[jax.ShapeDtypeStruct((PATCH, PATCH), F3...  2.41 us
  transfers between devices with their start and end apart: 27, of which 16 were waited for; matrix products, arithmetic and copies ran while one was open for 1% of the time, Pallas kernels for 23%

profile of v4, /device:TPU:0, one launch (start us, length us, event | category | flops | bytes accessed | tf_op | source)
XLA Modules:
  0.0 108.7 jit_solution(13685611245940917028)
XLA Ops:
  2.6 8.0 %match.1.refs_3_ = f32[32,128,128]{2,1,0:T(8,128)S(1)} custom-call(s32[3,32]{1,0:T(4,128)} %bitcast.16, f32[3,32]{1,0:T(4,128)} %bitcast.17, f32[8,2,41]{2,1,0:T(2,128)} %taps_hbm.1, f32[32,128,128]{2,1,0:T(8,128)} %image_hbm.1, f32[32,128,128]{2,1,0:T(8,128)} %refs_2_.1), custom_call_target="tpu_custom_call" | custom-call | flops 99999997952 | bytes 6291456 | tf_op jit(solution)/shard_map/match/pallas_call | solution.py:148
  10.8 8.7 %warp_meta.1 = (f32[8,280,128]{2,1,0:T(8,128)S(1)}, f32[8,280,128]{2,1,0:T(8,128)S(1)}, f32[8,256,128]{2,1,0:T(8,128)S(1)}, f32[8,256,128]{2,1,0:T(8,128)S(1)}, s32[2,128]{1,0:T(2,128)S(1)}) custom-call(f32[16,128]{1,0:T(8,128)S(1)} %copy-done, f32[16,128]{1,0:T(8,128)S(1)} %collective-permute-done.refs_1_.refs_2_, f32[32,128,128]{2,1,0:T(8,128)S(1)} %copy-done.1, ...), custom_call_target="tpu_custom_call" | custom-call | flops 10000000000 | bytes 8388608 | tf_op jit(solution)/shard_map/warp_meta/pallas_call | solution.py:290
  21.2 1.9 %collective-permute-start.5 = (f32[8,280,128]{2,1,0:T(8,128)S(1)}, f32[8,280,128]{2,1,0:T(8,128)S(1)}, u32[]{:S(2)}, u32[]{:S(2)}) collective-permute-start(f32[8,280,128]{2,1,0:T(8,128)S(1)} %get-tuple-element.30), channel_id=1, source_target_pairs={{0,8},{1,9},{2,10},{3,11},{4,12},{5,13},{6,14},{7,15},{8,0},{9,1},... | collective-permute-start | bytes 3440648 | tf_op jit(solution)/shard_map/ppermute | solution.py:360
  23.1 7.1 %warp.1 = (f32[8,256,128]{2,1,0:T(8,128)S(1)}, f32[8,256,128]{2,1,0:T(8,128)S(1)}, f32[8,256,128]{2,1,0:T(8,128)S(1)}, f32[8,256,128]{2,1,0:T(8,128)S(1)}) custom-call(s32[2,128]{1,0:T(2,128)S(1)} %get-tuple-element.24.refs_0_, f32[16,128]{1,0:T(8,128)S(1)} %copy-done, f32[16,128]{1,0:T(8,128)S(1)} %collective-permute-done.refs_1_.refs_2_, ...), custom_call_target="tpu_custom_call" | custom-call | flops 10000000000 | bytes 8388608 | tf_op jit(solution)/shard_map/warp/pallas_call | solution.py:290
  30.2 2.6 %collective-permute-start.3 = (f32[8,256,128]{2,1,0:T(8,128)S(1)}, f32[8,256,128]{2,1,0:T(8,128)S(1)}, u32[]{:S(2)}, u32[]{:S(2)}) collective-permute-start(f32[8,256,128]{2,1,0:T(8,128)S(1)} %get-tuple-element.27), channel_id=1, source_target_pairs={{8,16},{9,17},{10,18},{11,19},{12,20},{13,21},{14,22},{15,23},{16,... | collective-permute-start | bytes 3145736 | tf_op jit(solution)/shard_map/ppermute | solution.py:360
  32.9 2.2 %collective-permute-start.4 = (f32[8,256,128]{2,1,0:T(8,128)S(1)}, f32[8,256,128]{2,1,0:T(8,128)S(1)}, u32[]{:S(2)}, u32[]{:S(2)}) collective-permute-start(f32[8,256,128]{2,1,0:T(8,128)S(1)} %get-tuple-element.28), channel_id=1, source_target_pairs={{2,4},{3,5},{10,12},{11,13},{18,20},{19,21},{26,28},{27,29},{4,2},... | collective-permute-start | bytes 3145736 | tf_op jit(solution)/shard_map/ppermute | solution.py:360
  35.1 9.4 %collective-permute-done.6 = f32[8,256,128]{2,1,0:T(8,128)S(1)} collective-permute-done((f32[8,256,128]{2,1,0:T(8,128)S(1)}, f32[8,256,128]{2,1,0:T(8,128)S(1)}, u32[]{:S(2)}, u32[]{:S(2)}) %collective-permute-start.6) | collective-permute-done | bytes 1048608 | tf_op jit(solution)/shard_map/ppermute | solution.py:360
  44.6 2.1 %collective-permute-start.10 = (f32[4,256,128]{2,1,0:T(8,128)S(1)}, f32[4,256,128]{2,1,0:T(8,128)S(1)}, u32[]{:S(2)}, u32[]{:S(2)}) collective-permute-start(f32[4,256,128]{2,1,0:T(8,128)S(1)} %get-tuple-element.49), channel_id=1, source_target_pairs={{0,8},{1,9},{2,10},{3,11},{4,12},{5,13},{6,14},{7,15},{8,0},{9,1},... | collective-permute-start | bytes 1572872 | tf_op jit(solution)/shard_map/ppermute | solution.py:360
  46.7 2.7 %collective-permute-done.5 = f32[8,280,128]{2,1,0:T(8,128)S(1)} collective-permute-done((f32[8,280,128]{2,1,0:T(8,128)S(1)}, f32[8,280,128]{2,1,0:T(8,128)S(1)}, u32[]{:S(2)}, u32[]{:S(2)}) %collective-permute-start.5) | collective-permute-done | bytes 1146912 | tf_op jit(solution)/shard_map/ppermute | solution.py:360
  49.6 5.7 %collective-permute-done.3 = f32[8,256,128]{2,1,0:T(8,128)S(1)} collective-permute-done((f32[8,256,128]{2,1,0:T(8,128)S(1)}, f32[8,256,128]{2,1,0:T(8,128)S(1)}, u32[]{:S(2)}, u32[]{:S(2)}) %collective-permute-start.3) | collective-permute-done | bytes 1048608 | tf_op jit(solution)/shard_map/ppermute | solution.py:360
  55.3 2.2 %collective-permute-done.4 = f32[8,256,128]{2,1,0:T(8,128)S(1)} collective-permute-done((f32[8,256,128]{2,1,0:T(8,128)S(1)}, f32[8,256,128]{2,1,0:T(8,128)S(1)}, u32[]{:S(2)}, u32[]{:S(2)}) %collective-permute-start.4) | collective-permute-done | bytes 1048608 | tf_op jit(solution)/shard_map/ppermute | solution.py:360
  58.6 2.2 %collective-permute-start.7 = (f32[4,256,128]{2,1,0:T(8,128)S(1)}, f32[4,256,128]{2,1,0:T(8,128)S(1)}, u32[]{:S(2)}, u32[]{:S(2)}) collective-permute-start(f32[4,256,128]{2,1,0:T(8,128)S(1)} %get-tuple-element.50), channel_id=1, source_target_pairs={{2,4},{3,5},{10,12},{11,13},{18,20},{19,21},{26,28},{27,29},{4,2},... | collective-permute-start | bytes 1572872 | tf_op jit(solution)/shard_map/ppermute | solution.py:360
  62.2 3.9 %collective-permute-start.13 = (f32[2,280,128]{2,1,0:T(8,128)S(1)}, f32[2,280,128]{2,1,0:T(8,128)S(1)}, u32[]{:S(2)}, u32[]{:S(2)}) collective-permute-start(f32[2,280,128]{2,1,0:T(8,128)S(1)} %get-tuple-element.53), channel_id=1, source_target_pairs={{8,16},{9,17},{10,18},{11,19},{12,20},{13,21},{14,22},{15,23},{16,... | collective-permute-start | bytes 860168 | tf_op jit(solution)/shard_map/ppermute | solution.py:360
  66.1 7.3 %collective-permute-done.8 = f32[4,256,128]{2,1,0:T(8,128)S(1)} collective-permute-done((f32[4,256,128]{2,1,0:T(8,128)S(1)}, f32[4,256,128]{2,1,0:T(8,128)S(1)}, u32[]{:S(2)}, u32[]{:S(2)}) %collective-permute-start.8) | collective-permute-done | bytes 524320 | tf_op jit(solution)/shard_map/ppermute | solution.py:360
  73.9 2.7 %collective-permute-done.14 = f32[2,256,128]{2,1,0:T(8,128)S(1)} collective-permute-done((f32[2,256,128]{2,1,0:T(8,128)S(1)}, f32[2,256,128]{2,1,0:T(8,128)S(1)}, u32[]{:S(2)}, u32[]{:S(2)}) %collective-permute-start.14) | collective-permute-done | bytes 262176 | tf_op jit(solution)/shard_map/ppermute | solution.py:360
  76.5 2.6 %collective-permute-start.18 = (f32[1,256,128]{2,1,0:T(8,128)S(1)}, f32[1,256,128]{2,1,0:T(8,128)S(1)}, u32[]{:S(2)}, u32[]{:S(2)}) collective-permute-start(f32[1,256,128]{2,1,0:T(8,128)S(1)} %slice_add_fusion.22), channel_id=1, source_target_pairs={{8,16},{9,17},{10,18},{11,19},{12,20},{13,21},{14,22},{15,23},{16,... | collective-permute-start | bytes 393224 | tf_op jit(solution)/shard_map/ppermute | solution.py:360
  79.3 3.5 %collective-permute-done.18 = f32[1,256,128]{2,1,0:T(8,128)S(1)} collective-permute-done((f32[1,256,128]{2,1,0:T(8,128)S(1)}, f32[1,256,128]{2,1,0:T(8,128)S(1)}, u32[]{:S(2)}, u32[]{:S(2)}) %collective-permute-start.18) | collective-permute-done | bytes 131104 | tf_op jit(solution)/shard_map/ppermute | solution.py:360
  82.8 3.0 %collective-permute-start.25 = (f32[256,128]{1,0:T(8,128)S(1)}, f32[256,128]{1,0:T(8,128)S(1)}, u32[]{:S(2)}, u32[]{:S(2)}) collective-permute-start(f32[256,128]{1,0:T(8,128)S(1)} %fusion.5), channel_id=1, source_target_pairs={{32,64},{64,32},{96,0},{0,96},{33,65},{65,33},{97,1},{1,97},{34,66... | collective-permute-start | bytes 393224 | tf_op jit(solution)/shard_map/ppermute | solution.py:374
  85.9 2.0 %collective-permute-start.17 = (f32[1,280,128]{2,1,0:T(8,128)S(1)}, f32[1,280,128]{2,1,0:T(8,128)S(1)}, u32[]{:S(2)}, u32[]{:S(2)}) collective-permute-start(f32[1,280,128]{2,1,0:T(8,128)S(1)} %slice_add_fusion.17), channel_id=1, source_target_pairs={{2,4},{3,5},{10,12},{11,13},{18,20},{19,21},{26,28},{27,29},{4,2},... | collective-permute-start | bytes 430088 | tf_op jit(solution)/shard_map/ppermute | solution.py:360
  88.2 4.1 %collective-permute-done.17 = f32[1,280,128]{2,1,0:T(8,128)S(1)} collective-permute-done((f32[1,280,128]{2,1,0:T(8,128)S(1)}, f32[1,280,128]{2,1,0:T(8,128)S(1)}, u32[]{:S(2)}, u32[]{:S(2)}) %collective-permute-start.17) | collective-permute-done | bytes 143392 | tf_op jit(solution)/shard_map/ppermute | solution.py:360
  93.1 2.3 %collective-permute-start.21 = (f32[256,128]{1,0:T(8,128)S(1)}, f32[256,128]{1,0:T(8,128)S(1)}, u32[]{:S(2)}, u32[]{:S(2)}) collective-permute-start(f32[256,128]{1,0:T(8,128)S(1)} %fusion.3), channel_id=1, source_target_pairs={{32,64},{64,32},{96,0},{0,96},{33,65},{65,33},{97,1},{1,97},{34,66... | collective-permute-start | bytes 393224 | tf_op jit(solution)/shard_map/ppermute | solution.py:374
  95.6 2.4 %collective-permute-done.23 = f32[280,128]{1,0:T(8,128)S(1)} collective-permute-done((f32[280,128]{1,0:T(8,128)S(1)}, f32[280,128]{1,0:T(8,128)S(1)}, u32[]{:S(2)}, u32[]{:S(2)}) %collective-permute-start.23) | collective-permute-done | bytes 143392 | tf_op jit(solution)/shard_map/ppermute | solution.py:374
  101.7 2.0 %collective-permute-start.20 = (f32[256,128]{1,0:T(8,128)S(1)}, f32[256,128]{1,0:T(8,128)S(1)}, u32[]{:S(2)}, u32[]{:S(2)}) collective-permute-start(f32[256,128]{1,0:T(8,128)S(1)} %add.137.left), channel_id=1, source_target_pairs={{32,64},{64,32},{96,0},{0,96},{33,65},{65,33},{97,1},{1,97},{34,66... | collective-permute-start | bytes 393224 | tf_op jit(solution)/shard_map/ppermute | solution.py:375
  106.1 1.8 %collective-permute-done.20.left_got = f32[256,128]{1,0:T(8,128)S(1)} collective-permute-done((f32[256,128]{1,0:T(8,128)S(1)}, f32[256,128]{1,0:T(8,128)S(1)}, u32[]{:S(2)}, u32[]{:S(2)}) %collective-permute-start.20) | collective-permute-done | bytes 131104 | tf_op jit(solution)/shard_map/ppermute | solution.py:375
  (60 shorter events, 15.4 us)
Async XLA Ops:
  2.1 8.6 %collective-permute-start = (f32[16,128]{1,0:T(8,128)}, f32[16,128]{1,0:T(8,128)S(1)}, u32[]{:S(2)}, u32[]{:S(2)}) collective-permute-start(f32[16,128]{1,0:T(8,128)} %pack.1.refs_0_.refs_1_), channel_id=1, source_target_pairs={{0,1},{1,0},{2,3},{3,2},{4,5},{5,4},{6,7},{7,6},{8,9},{9,8},{10,11... | collective-permute-start | bytes 24584 | tf_op jit(solution)/shard_map/ppermute | solution.py:382
  2.1 8.7 %collective-permute-start.1 = (f32[32,128,128]{2,1,0:T(8,128)}, f32[32,128,128]{2,1,0:T(8,128)S(1)}, u32[]{:S(2)}, u32[]{:S(2)}) collective-permute-start(f32[32,128,128]{2,1,0:T(8,128)} %refs_2_.1), channel_id=1, source_target_pairs={{0,1},{1,0},{2,3},{3,2},{4,5},{5,4},{6,7},{7,6},{8,9},{9,8},{10,11... | collective-permute-start | bytes 6291464 | tf_op jit(solution)/shard_map/ppermute | solution.py:380
  10.7 12.5 %collective-permute-start.2 = (f32[32,128,128]{2,1,0:T(8,128)S(1)}, f32[32,128,128]{2,1,0:T(8,128)S(1)}, u32[]{:S(2)}, u32[]{:S(2)}) collective-permute-start(f32[32,128,128]{2,1,0:T(8,128)S(1)} %match.1.refs_3_), channel_id=1, source_target_pairs={{0,1},{1,0},{2,3},{3,2},{4,5},{5,4},{6,7},{7,6},{8,9},{9,8},{10,11... | collective-permute-start | bytes 6291464 | tf_op jit(solution)/shard_map/ppermute | solution.py:385
  19.4 25.0 %collective-permute-start.6 = (f32[8,256,128]{2,1,0:T(8,128)S(1)}, f32[8,256,128]{2,1,0:T(8,128)S(1)}, u32[]{:S(2)}, u32[]{:S(2)}) collective-permute-start(f32[8,256,128]{2,1,0:T(8,128)S(1)} %get-tuple-element.32), channel_id=1, source_target_pairs={{0,2},{1,3},{8,10},{9,11},{16,18},{17,19},{24,26},{25,27},{2,0},{3... | collective-permute-start | bytes 3145736 | tf_op jit(solution)/shard_map/ppermute | solution.py:360
  21.2 28.2 %collective-permute-start.5 = (f32[8,280,128]{2,1,0:T(8,128)S(1)}, f32[8,280,128]{2,1,0:T(8,128)S(1)}, u32[]{:S(2)}, u32[]{:S(2)}) collective-permute-start(f32[8,280,128]{2,1,0:T(8,128)S(1)} %get-tuple-element.30), channel_id=1, source_target_pairs={{0,8},{1,9},{2,10},{3,11},{4,12},{5,13},{6,14},{7,15},{8,0},{9,1},... | collective-permute-start | bytes 3440648 | tf_op jit(solution)/shard_map/ppermute | solution.py:360
  30.2 25.1 %collective-permute-start.3 = (f32[8,256,128]{2,1,0:T(8,128)S(1)}, f32[8,256,128]{2,1,0:T(8,128)S(1)}, u32[]{:S(2)}, u32[]{:S(2)}) collective-permute-start(f32[8,256,128]{2,1,0:T(8,128)S(1)} %get-tuple-element.27), channel_id=1, source_target_pairs={{8,16},{9,17},{10,18},{11,19},{12,20},{13,21},{14,22},{15,23},{16,... | collective-permute-start | bytes 3145736 | tf_op jit(solution)/shard_map/ppermute | solution.py:360
  32.9 24.7 %collective-permute-start.4 = (f32[8,256,128]{2,1,0:T(8,128)S(1)}, f32[8,256,128]{2,1,0:T(8,128)S(1)}, u32[]{:S(2)}, u32[]{:S(2)}) collective-permute-start(f32[8,256,128]{2,1,0:T(8,128)S(1)} %get-tuple-element.28), channel_id=1, source_target_pairs={{2,4},{3,5},{10,12},{11,13},{18,20},{19,21},{26,28},{27,29},{4,2},... | collective-permute-start | bytes 3145736 | tf_op jit(solution)/shard_map/ppermute | solution.py:360
  44.6 16.2 %collective-permute-start.10 = (f32[4,256,128]{2,1,0:T(8,128)S(1)}, f32[4,256,128]{2,1,0:T(8,128)S(1)}, u32[]{:S(2)}, u32[]{:S(2)}) collective-permute-start(f32[4,256,128]{2,1,0:T(8,128)S(1)} %get-tuple-element.49), channel_id=1, source_target_pairs={{0,8},{1,9},{2,10},{3,11},{4,12},{5,13},{6,14},{7,15},{8,0},{9,1},... | collective-permute-start | bytes 1572872 | tf_op jit(solution)/shard_map/ppermute | solution.py:360
  49.5 12.6 %collective-permute-start.9 = (f32[4,280,128]{2,1,0:T(8,128)S(1)}, f32[4,280,128]{2,1,0:T(8,128)S(1)}, u32[]{:S(2)}, u32[]{:S(2)}) collective-permute-start(f32[4,280,128]{2,1,0:T(8,128)S(1)} %get-tuple-element.45), channel_id=1, source_target_pairs={{0,2},{1,3},{8,10},{9,11},{16,18},{17,19},{24,26},{25,27},{2,0},{3... | collective-permute-start | bytes 1720328 | tf_op jit(solution)/shard_map/ppermute | solution.py:360
  57.6 15.7 %collective-permute-start.8 = (f32[4,256,128]{2,1,0:T(8,128)S(1)}, f32[4,256,128]{2,1,0:T(8,128)S(1)}, u32[]{:S(2)}, u32[]{:S(2)}) collective-permute-start(f32[4,256,128]{2,1,0:T(8,128)S(1)} %get-tuple-element.47), channel_id=1, source_target_pairs={{8,16},{9,17},{10,18},{11,19},{12,20},{13,21},{14,22},{15,23},{16,... | collective-permute-start | bytes 1572872 | tf_op jit(solution)/shard_map/ppermute | solution.py:360
  58.6 15.1 %collective-permute-start.7 = (f32[4,256,128]{2,1,0:T(8,128)S(1)}, f32[4,256,128]{2,1,0:T(8,128)S(1)}, u32[]{:S(2)}, u32[]{:S(2)}) collective-permute-start(f32[4,256,128]{2,1,0:T(8,128)S(1)} %get-tuple-element.50), channel_id=1, source_target_pairs={{2,4},{3,5},{10,12},{11,13},{18,20},{19,21},{26,28},{27,29},{4,2},... | collective-permute-start | bytes 1572872 | tf_op jit(solution)/shard_map/ppermute | solution.py:360
  60.9 15.6 %collective-permute-start.14 = (f32[2,256,128]{2,1,0:T(8,128)S(1)}, f32[2,256,128]{2,1,0:T(8,128)S(1)}, u32[]{:S(2)}, u32[]{:S(2)}) collective-permute-start(f32[2,256,128]{2,1,0:T(8,128)S(1)} %get-tuple-element.57), channel_id=1, source_target_pairs={{2,4},{3,5},{10,12},{11,13},{18,20},{19,21},{26,28},{27,29},{4,2},... | collective-permute-start | bytes 786440 | tf_op jit(solution)/shard_map/ppermute | solution.py:360
  62.2 23.7 %collective-permute-start.13 = (f32[2,280,128]{2,1,0:T(8,128)S(1)}, f32[2,280,128]{2,1,0:T(8,128)S(1)}, u32[]{:S(2)}, u32[]{:S(2)}) collective-permute-start(f32[2,280,128]{2,1,0:T(8,128)S(1)} %get-tuple-element.53), channel_id=1, source_target_pairs={{8,16},{9,17},{10,18},{11,19},{12,20},{13,21},{14,22},{15,23},{16,... | collective-permute-start | bytes 860168 | tf_op jit(solution)/shard_map/ppermute | solution.py:360
  73.8 14.1 %collective-permute-start.12 = (f32[2,256,128]{2,1,0:T(8,128)S(1)}, f32[2,256,128]{2,1,0:T(8,128)S(1)}, u32[]{:S(2)}, u32[]{:S(2)}) collective-permute-start(f32[2,256,128]{2,1,0:T(8,128)S(1)} %get-tuple-element.55), channel_id=1, source_target_pairs={{0,2},{1,3},{8,10},{9,11},{16,18},{17,19},{24,26},{25,27},{2,0},{3... | collective-permute-start | bytes 786440 | tf_op jit(solution)/shard_map/ppermute | solution.py:360
  76.5 6.3 %collective-permute-start.18 = (f32[1,256,128]{2,1,0:T(8,128)S(1)}, f32[1,256,128]{2,1,0:T(8,128)S(1)}, u32[]{:S(2)}, u32[]{:S(2)}) collective-permute-start(f32[1,256,128]{2,1,0:T(8,128)S(1)} %slice_add_fusion.22), channel_id=1, source_target_pairs={{8,16},{9,17},{10,18},{11,19},{12,20},{13,21},{14,22},{15,23},{16,... | collective-permute-start | bytes 393224 | tf_op jit(solution)/shard_map/ppermute | solution.py:360
  79.2 8.7 %collective-permute-start.11 = (f32[2,256,128]{2,1,0:T(8,128)S(1)}, f32[2,256,128]{2,1,0:T(8,128)S(1)}, u32[]{:S(2)}, u32[]{:S(2)}) collective-permute-start(f32[2,256,128]{2,1,0:T(8,128)S(1)} %get-tuple-element.58), channel_id=1, source_target_pairs={{0,8},{1,9},{2,10},{3,11},{4,12},{5,13},{6,14},{7,15},{8,0},{9,1},... | collective-permute-start | bytes 786440 | tf_op jit(solution)/shard_map/ppermute | solution.py:360
  82.8 16.6 %collective-permute-start.25 = (f32[256,128]{1,0:T(8,128)S(1)}, f32[256,128]{1,0:T(8,128)S(1)}, u32[]{:S(2)}, u32[]{:S(2)}) collective-permute-start(f32[256,128]{1,0:T(8,128)S(1)} %fusion.5), channel_id=1, source_target_pairs={{32,64},{64,32},{96,0},{0,96},{33,65},{65,33},{97,1},{1,97},{34,66... | collective-permute-start | bytes 393224 | tf_op jit(solution)/shard_map/ppermute | solution.py:374
  85.9 6.4 %collective-permute-start.17 = (f32[1,280,128]{2,1,0:T(8,128)S(1)}, f32[1,280,128]{2,1,0:T(8,128)S(1)}, u32[]{:S(2)}, u32[]{:S(2)}) collective-permute-start(f32[1,280,128]{2,1,0:T(8,128)S(1)} %slice_add_fusion.17), channel_id=1, source_target_pairs={{2,4},{3,5},{10,12},{11,13},{18,20},{19,21},{26,28},{27,29},{4,2},... | collective-permute-start | bytes 430088 | tf_op jit(solution)/shard_map/ppermute | solution.py:360
  92.3 5.7 %collective-permute-start.23 = (f32[280,128]{1,0:T(8,128)S(1)}, f32[280,128]{1,0:T(8,128)S(1)}, u32[]{:S(2)}, u32[]{:S(2)}) collective-permute-start(f32[280,128]{1,0:T(8,128)S(1)} %fusion.1), channel_id=1, source_target_pairs={{0,32},{32,0},{64,96},{96,64},{1,33},{33,1},{65,97},{97,65},{2,34}... | collective-permute-start | bytes 430088 | tf_op jit(solution)/shard_map/ppermute | solution.py:374
  93.1 6.8 %collective-permute-start.21 = (f32[256,128]{1,0:T(8,128)S(1)}, f32[256,128]{1,0:T(8,128)S(1)}, u32[]{:S(2)}, u32[]{:S(2)}) collective-permute-start(f32[256,128]{1,0:T(8,128)S(1)} %fusion.3), channel_id=1, source_target_pairs={{32,64},{64,32},{96,0},{0,96},{33,65},{65,33},{97,1},{1,97},{34,66... | collective-permute-start | bytes 393224 | tf_op jit(solution)/shard_map/ppermute | solution.py:374
  95.5 6.2 %collective-permute-start.19 = (f32[256,128]{1,0:T(8,128)S(1)}, f32[256,128]{1,0:T(8,128)S(1)}, u32[]{:S(2)}, u32[]{:S(2)}) collective-permute-start(f32[256,128]{1,0:T(8,128)S(1)} %fusion.7), channel_id=1, source_target_pairs={{0,32},{32,0},{64,96},{96,64},{1,33},{33,1},{65,97},{97,65},{2,34}... | collective-permute-start | bytes 393224 | tf_op jit(solution)/shard_map/ppermute | solution.py:374
  98.0 6.5 %collective-permute-start.24 = (f32[280,128]{1,0:T(8,128)S(1)}, f32[280,128]{1,0:T(8,128)S(1)}, u32[]{:S(2)}, u32[]{:S(2)}) collective-permute-start(f32[280,128]{1,0:T(8,128)S(1)} %add.142.left), channel_id=1, source_target_pairs={{32,64},{64,32},{96,0},{0,96},{33,65},{65,33},{97,1},{1,97},{34,66... | collective-permute-start | bytes 430088 | tf_op jit(solution)/shard_map/ppermute | solution.py:375
  100.0 6.2 %collective-permute-start.22 = (f32[256,128]{1,0:T(8,128)S(1)}, f32[256,128]{1,0:T(8,128)S(1)}, u32[]{:S(2)}, u32[]{:S(2)}) collective-permute-start(f32[256,128]{1,0:T(8,128)S(1)} %add.141.right), channel_id=1, source_target_pairs={{0,32},{32,0},{64,96},{96,64},{1,33},{33,1},{65,97},{97,65},{2,34}... | collective-permute-start | bytes 393224 | tf_op jit(solution)/shard_map/ppermute | solution.py:375
  101.7 6.3 %collective-permute-start.20 = (f32[256,128]{1,0:T(8,128)S(1)}, f32[256,128]{1,0:T(8,128)S(1)}, u32[]{:S(2)}, u32[]{:S(2)}) collective-permute-start(f32[256,128]{1,0:T(8,128)S(1)} %add.137.left), channel_id=1, source_target_pairs={{32,64},{64,32},{96,0},{0,96},{33,65},{65,33},{97,1},{1,97},{34,66... | collective-permute-start | bytes 393224 | tf_op jit(solution)/shard_map/ppermute | solution.py:375
  (5 other events, 31.5 us)

commit v5 on v4

--- a/solution.py
+++ b/solution.py
@@ -36,17 +36,17 @@
 def here():
     patch = lax.axis_index("patch")
     z, y = patch >> 3, (patch >> 1) & 3
-    chip = lax.axis_index("visit") * 16 + z * 4 + y
-    return place_code(z, y), patch & 1, chip
-
-
-def place_code(z, y):
-    z, y = z ^ (z >> 1), y ^ (y >> 1)
-    return ((z & 1) << 3) | ((z >> 1) << 2) | ((y & 1) << 1) | (y >> 1)
+    return z, y, patch & 1, lax.axis_index("visit") * 16 + z * 4 + y
+
+
+def place_code(z, y, core):
+    first, second = jnp.where(core == 0, z, y), jnp.where(core == 0, y, z)
+    first, second = first ^ (first >> 1), second ^ (second >> 1)
+    return ((first & 1) << 3) | ((first >> 1) << 2) | ((second & 1) << 1) | (second >> 1)
 
 
 def pack_kernel(intersections, boxes, shifts, out):
-    mine = here()[0]
+    z, y, _, _ = here()
     out[...] = jnp.zeros_like(out)
     earlier_item = lax.broadcasted_iota(jnp.int32, (TILES, TILES), 0)
     item = lax.broadcasted_iota(jnp.int32, (TILES, TILES), 1)
@@ -65,7 +65,7 @@
     slots, places = earlier(dest), earlier([d & 1 for d in dest])
     for route in range(2):
         d = dest[route]
-        code = place_code(d >> 3, (d >> 1) & 3) ^ mine
+        code = place_code(d >> 3, (d >> 1) & 3, d & 1) ^ place_code(z, y, d & 1)
         out[route : route + 1, 0:TILES] = (code + (slots[route] << 4) + ((d & 1) << 8)).astype(F32)
         out[10 + route : 11 + route, 0:TILES] = places[route].astype(F32)
         out[2 + 2 * route : 4 + 2 * route, 0:TILES] = boxes[route].astype(F32)
@@ -169,12 +169,12 @@
 def warp_kernel(with_meta, *refs):
     if with_meta:
         own, other, own_tiles, other_tiles = refs[:4]
-        outs, slots = refs[4:8], refs[8]
-        stage, acc, meta, weights = refs[9:]
+        outs, slots = refs[4:6], refs[6]
+        stage, acc, meta, weights = refs[7:]
     else:
         slots, own, other, own_tiles, other_tiles = refs[:5]
-        outs = refs[5:9]
-        stage, acc = refs[9:]
+        outs = refs[5:7]
+        stage, acc = refs[7:]
     lane = lax.broadcasted_iota(jnp.int32, (8, TS), 1)
     stage[:, :, 0:8, :] = jnp.zeros((2 * UNROLL, 2, 8, TS), F32)
     stage[:, :, 8 + TS :, :] = jnp.zeros((2 * UNROLL, 2, 8, TS), F32)
@@ -183,7 +183,7 @@
             acc[4 * k + side, PAD : PAD + PATCH, :] = jnp.zeros((PATCH, TS), F32)
 
     if with_meta:
-        _, core, chip = here()
+        _, _, core, chip = here()
         meta[...] = jnp.zeros_like(meta)
 
         @pl.loop(0, TILES, step=8)
@@ -259,24 +259,21 @@
         lax.fori_loop(0, (slots[side, 0] + 2 * UNROLL - 1) // (2 * UNROLL), body, start)
 
     for k in range(16):
-        z_first, z_second, y_first, y_second = k >> 3, (k >> 2) & 1, (k >> 1) & 1, k & 1
+        a, b, c, d = k >> 3, (k >> 2) & 1, (k >> 1) & 1, k & 1
         if not with_meta:
-            z_first, z_second, y_first, y_second = z_second, z_first, y_second, y_first
-        left, right = outs[z_first], outs[2 + y_first]
-        at = y_first * 4 + z_second * 2 + y_second
-        left[at, 0:PATCH, :] = acc[4 * k + 1, PAD : PAD + PATCH, :]
+            a, b, c, d = b, a, d, c
+        out, at = outs[a], c * 4 + b * 2 + d
+        out[at, 0:PATCH, :] = acc[4 * k + 1, PAD : PAD + PATCH, :]
+        out[at, PATCH : 2 * PATCH, :] = acc[4 * k + 2, PAD : PAD + PATCH, :]
         if with_meta:
             for slot in range(CAP):
-                left[at, PATCH + 8 * slot : PATCH + 8 * slot + 8, :] = meta[k * CAP + slot]
-        right[z_first * 4 + y_second * 2 + z_second, :, :] = acc[4 * k + 2, PAD : PAD + PATCH, :]
+                out[at, 2 * PATCH + 8 * slot : 2 * PATCH + 8 * slot + 8, :] = meta[k * CAP + slot]
 
 
 def warp(with_meta, *args):
     smem, vmem = pl.BlockSpec(memory_space=pltpu.SMEM), pl.BlockSpec(memory_space=pltpu.VMEM)
-    rows = PATCH + META if with_meta else PATCH
-    left = jax.ShapeDtypeStruct((8, rows, TS), F32)
-    right = jax.ShapeDtypeStruct((8, PATCH, TS), F32)
-    outs, specs = [left, left, right, right], [vmem] * 4
+    rows = 2 * PATCH + META if with_meta else 2 * PATCH
+    outs, specs = [jax.ShapeDtypeStruct((8, rows, TS), F32)] * 2, [vmem] * 2
     scratch = [
         pltpu.VMEM((2 * UNROLL, 2, TS + 16, TS), F32),
         pltpu.VMEM((64, 384, TS), F32),
@@ -299,7 +296,7 @@
     )(*args)
 
 
-def cover_kernel(left, left_got, right, right_got, coadd_var, safe_ref):
+def cover_kernel(var, got, coadd_var, safe_ref):
     place_of = lax.broadcasted_iota(jnp.int32, (PATCH, TS), 0).astype(F32)
 
     def cover(offset, shift):
@@ -309,8 +306,8 @@
 
     den = jnp.zeros((PATCH, PATCH), F32)
     for slot in range(CAP):
-        at = PATCH + 8 * slot
-        fields = left[at : at + 8, :] + left_got[at : at + 8, :]
+        at = 2 * PATCH + 8 * slot
+        fields = var[at : at + 8, :] + got[at : at + 8, :]
         weight, row, col, frac_row, frac_col = (fields[f : f + 1, :] for f in range(5))
         down, across = cover(row, frac_row) * weight, cover(col, frac_col)
         den += lax.dot_general(
@@ -318,14 +315,16 @@
         )
     safe = jnp.maximum(den, 1.0)
     safe_ref[...] = safe
-    for var, got, lo in ((left, left_got, 0), (right, right_got, TS)):
-        part = safe[:, lo : lo + TS]
-        coadd_var[:, lo : lo + TS] = (var[0:PATCH, :] + got[0:PATCH, :]) / (part * part)
-
-
-def divide_kernel(left, left_got, right, right_got, safe, coadd):
-    coadd[:, 0:TS] = (left[...] + left_got[...]) / safe[:, 0:TS]
-    coadd[:, TS:] = (right[...] + right_got[...]) / safe[:, TS:]
+    for half in range(2):
+        rows, lanes = slice(half * PATCH, (half + 1) * PATCH), slice(half * TS, (half + 1) * TS)
+        part = safe[:, lanes]
+        coadd_var[:, lanes] = (var[rows, :] + got[rows, :]) / (part * part)
+
+
+def divide_kernel(num, got, safe, coadd):
+    for half in range(2):
+        rows, lanes = slice(half * PATCH, (half + 1) * PATCH), slice(half * TS, (half + 1) * TS)
+        coadd[:, lanes] = (num[rows, :] + got[rows, :]) / safe[:, lanes]
 
 
 def finish(kernel, name, outs, *args):
@@ -349,30 +348,39 @@
     for a, b in EDGES[edge]:
         for other in range(4):
             for core in range(2):
-                src, dst = ((a, other), (b, other)) if axis == "z" else ((other, a), (other, b))
+                src, dst = ((a, other), (b, other)) if axis == core else ((other, a), (other, b))
                 pairs.append((src[0] * 8 + src[1] * 2 + core, dst[0] * 8 + dst[1] * 2 + core))
     return pairs
 
 
-def halve(left, right, orders, ahead=()):
-    parts, left_over = [left, right], []
-    for step in range(4):
-        got = [lax.ppermute(send, "patch", over_patch(*order[step])) for (_, send), order in zip(parts, orders)]
+def over_visit(edge):
+    return [
+        (a * 32 + 2 * chip + core, b * 32 + 2 * chip + core)
+        for core in range(2)
+        for a, b in EDGES[edge ^ core]
+        for chip in range(16)
+    ]
+
+
+def halve(keep, send, order, ahead=()):
+    left_over = []
+    for step, (axis, edge) in enumerate(order):
+        got = lax.ppermute(send, "patch", over_patch(axis, edge))
         if step < len(ahead):
-            got = lax.optimization_barrier((*got, *ahead[step]))[:2]
+            got, _ = lax.optimization_barrier((got, ahead[step]))
         if step < 3:
             n = 8 >> (step + 1)
-            parts = [(keep[:n] + g[:n], keep[n:] + g[n:]) for (keep, _), g in zip(parts, got)]
-            left_over.append([send for _, send in parts])
+            keep, send = keep[:n] + got[:n], keep[n:] + got[n:]
+            left_over.append(send)
         else:
-            parts = [keep[0] + g[0] for (keep, _), g in zip(parts, got)]
-            left_over.append(parts)
-    return parts, left_over
-
-
-def double(left, right):
-    parts = [x + lax.ppermute(x, "visit", EDGES[first]) for x, first in ((left, 0), (right, 1))]
-    return [y for x, first in zip(parts, (1, 0)) for y in (x, lax.ppermute(x, "visit", EDGES[first]))]
+            keep = keep[0] + got[0]
+            left_over.append(keep)
+    return keep, left_over
+
+
+def double(x):
+    x = x + lax.ppermute(x, ("visit", "patch"), over_visit(0))
+    return x, lax.ppermute(x, ("visit", "patch"), over_visit(1))
 
 
 def shards(image, variance, intersections, boxes, shifts, basis_ids, coefs, taps):
@@ -383,18 +391,11 @@
     matched = match(basis_ids, coefs, taps, image, variance)
     matched, other_table = lax.optimization_barrier((matched, other_table))
     other_matched = lax.ppermute(matched, "patch", swap)
-    var_left_keep, var_left_send, var_right_keep, var_right_send, slots = warp(
-        True, table, other_table, variance, other_variance
-    )
-    num_left_keep, num_left_send, num_right_keep, num_right_send = warp(
-        False, slots, table, other_table, matched, other_matched
-    )
-    z1, z2, y1, y2 = ("z", 0), ("z", 1), ("y", 0), ("y", 1)
-    var, ahead = halve((var_left_keep, var_left_send), (var_right_keep, var_right_send), ((z1, y1, z2, y2), (y1, z1, y2, z2)))
-    num, _ = halve(
-        (num_left_keep, num_left_send), (num_right_keep, num_right_send), ((z2, y2, z1, y1), (y2, z2, y1, z1)), ahead
-    )
-    var, num = double(*var), double(*num)
+    var_keep, var_send, slots = warp(True, table, other_table, variance, other_variance)
+    num_keep, num_send = warp(False, slots, table, other_table, matched, other_matched)
+    var, ahead = halve(var_keep, var_send, ((0, 0), (1, 0), (0, 1), (1, 1)))
+    num, _ = halve(num_keep, num_send, ((0, 1), (1, 1), (0, 0), (1, 0)), ahead)
+    var, num = double(var), double(num)
     coadd_var, safe = finish(cover_kernel, "cover", 2, *var)
     (coadd,) = finish(divide_kernel, "divide", 1, *num, safe)
     return coadd, coadd_var

time: 110 us -> 115 us (1.045)
  waiting for transfers between devices: 44 us -> 58.9 us
  starting transfers between devices: 35.2 us -> 26.2 us
    ppermute x24 -> x12, waiting for transfers between devices: 44 us -> 58.9 us  [the longest x8 50.4 us: halve(): got = lax.ppermute(send, 'patch', over_patch(axis, edge))]
    ppermute x24 -> x12, starting transfers between devices: 34.6 us -> 25.6 us  [the longest x8 17.5 us: halve(): got = lax.ppermute(send, 'patch', over_patch(axis, edge))]
  transfers between devices with their start and end apart: 27 -> 15, of which waited for: 16 -> 10; matrix products, arithmetic and copies ran while one was open for 1% -> 1% of each run, Pallas kernels for 23% -> 22%
where the time goes in v5:
time: 115 us
  waiting for transfers between devices  58.9 us (51%)
  Pallas kernels  27.7 us (24%)
  starting transfers between devices  26.2 us (23%)
    ppermute x8, waiting for transfers between devices, halve(): got = lax.ppermute(send, 'patch', over_patch(axis, edge))  50.4 us
    ppermute x8, starting transfers between devices, halve(): got = lax.ppermute(send, 'patch', over_patch(axis, edge))  17.5 us
    pallas_call x2, Pallas kernels, warp(): pl.pallas_call(functools.partial(warp_kernel, with_meta), out_shape=outs,...  15.8 us
    pallas_call x1, Pallas kernels, match(): pl.pallas_call(match_kernel, out_shape=jax.ShapeDtypeStruct((TILES, TS, T...  8.03 us
    ppermute x2, starting transfers between devices, double(): return (x, lax.ppermute(x, ('visit', 'patch'), over_visit(1)))  4.92 us
    ppermute x2, waiting for transfers between devices, double(): x = x + lax.ppermute(x, ('visit', 'patch'), over_visit(0))  4.67 us
    ppermute x2, waiting for transfers between devices, double(): return (x, lax.ppermute(x, ('visit', 'patch'), over_visit(1)))  3.88 us
    ppermute x2, starting transfers between devices, double(): x = x + lax.ppermute(x, ('visit', 'patch'), over_visit(0))  3.15 us
  transfers between devices with their start and end apart: 15, of which 10 were waited for; matrix products, arithmetic and copies ran while one was open for 1% of the time, Pallas kernels for 22%

profile of v5, /device:TPU:0, one launch (start us, length us, event | category | flops | bytes accessed | tf_op | source)
XLA Modules:
  0.0 114.6 jit_solution(6890287820917501160)
XLA Ops:
  0.6 1.4 %pack.1.refs_0_.refs_1_ = f32[16,128]{1,0:T(8,128)} custom-call(s32[2,32]{1,0:T(2,128)} %bitcast.11, s32[2,2,32]{2,1,0:T(2,128)} %bitcast.9, f32[2,2,32]{2,1,0:T(2,128)} %bitcast.10), custom_call_target="tpu_custom_call" | custom-call | tf_op jit(solution)/shard_map/pack/pallas_call | solution.py:80
  2.6 8.0 %match.1.refs_3_ = f32[32,128,128]{2,1,0:T(8,128)S(1)} custom-call(s32[3,32]{1,0:T(4,128)} %bitcast.12, f32[3,32]{1,0:T(4,128)} %bitcast.13, f32[8,2,41]{2,1,0:T(2,128)} %taps_hbm.1, f32[32,128,128]{2,1,0:T(8,128)} %image_hbm.1, f32[32,128,128]{2,1,0:T(8,128)} %refs_2_.1), custom_call_target="tpu_custom_call" | custom-call | flops 99999997952 | bytes 6291456 | tf_op jit(solution)/shard_map/match/pallas_call | solution.py:148
  10.8 8.7 %warp_meta.1 = (f32[8,536,128]{2,1,0:T(8,128)S(1)}, f32[8,536,128]{2,1,0:T(8,128)S(1)}, s32[2,128]{1,0:T(2,128)S(1)}) custom-call(f32[16,128]{1,0:T(8,128)S(1)} %copy-done, f32[16,128]{1,0:T(8,128)S(1)} %collective-permute-done.refs_1_.refs_2_, f32[32,128,128]{2,1,0:T(8,128)S(1)} %copy-done.1, f32[32,128,128]{2,1,0:T(8,128)S(1)} %collective-permute-done.1.refs_3_), custom_call_target="tpu_custom_call" | custom-call | flops 10000000000 | bytes 8388608 | tf_op jit(solution)/shard_map/warp_meta/pallas_call | solution.py:287
  19.4 2.1 %collective-permute-start.4 = (f32[8,536,128]{2,1,0:T(8,128)S(1)}, f32[8,536,128]{2,1,0:T(8,128)S(1)}, u32[]{:S(2)}, u32[]{:S(2)}) collective-permute-start(f32[8,536,128]{2,1,0:T(8,128)S(1)} %get-tuple-element.21), channel_id=1, source_target_pairs={{0,8},{1,3},{2,10},{9,11},{4,12},{17,19},{6,14},{25,27},{8,0},{3,1... | collective-permute-start | bytes 6586376 | tf_op jit(solution)/shard_map/ppermute | solution.py:368
  21.5 7.1 %warp.1 = (f32[8,512,128]{2,1,0:T(8,128)S(1)}, f32[8,512,128]{2,1,0:T(8,128)S(1)}) custom-call(s32[2,128]{1,0:T(2,128)S(1)} %get-tuple-element.16.refs_0_, f32[16,128]{1,0:T(8,128)S(1)} %copy-done, f32[16,128]{1,0:T(8,128)S(1)} %collective-permute-done.refs_1_.refs_2_, f32[32,128,128]{2,1,0:T(8,128)S(1)} %match.1.refs_3_, ...), custom_call_target="tpu_custom_call" | custom-call | flops 10000000000 | bytes 8388608 | tf_op jit(solution)/shard_map/warp/pallas_call | solution.py:287
  28.7 2.6 %collective-permute-start.3 = (f32[8,512,128]{2,1,0:T(8,128)S(1)}, f32[8,512,128]{2,1,0:T(8,128)S(1)}, u32[]{:S(2)}, u32[]{:S(2)}) collective-permute-start(f32[8,512,128]{2,1,0:T(8,128)S(1)} %get-tuple-element.19), channel_id=1, source_target_pairs={{8,16},{3,5},{10,18},{11,13},{12,20},{19,21},{14,22},{27,29},{16,8... | collective-permute-start | bytes 6291464 | tf_op jit(solution)/shard_map/ppermute | solution.py:368
  31.3 15.3 %collective-permute-done.4 = f32[8,536,128]{2,1,0:T(8,128)S(1)} collective-permute-done((f32[8,536,128]{2,1,0:T(8,128)S(1)}, f32[8,536,128]{2,1,0:T(8,128)S(1)}, u32[]{:S(2)}, u32[]{:S(2)}) %collective-permute-start.4) | collective-permute-done | bytes 2195488 | tf_op jit(solution)/shard_map/ppermute | solution.py:368
  46.8 1.7 %collective-permute-start.6 = (f32[4,536,128]{2,1,0:T(8,128)S(1)}, f32[4,536,128]{2,1,0:T(8,128)S(1)}, u32[]{:S(2)}, u32[]{:S(2)}) collective-permute-start(f32[4,536,128]{2,1,0:T(8,128)S(1)} %get-tuple-element.29), channel_id=1, source_target_pairs={{0,2},{1,9},{8,10},{3,11},{16,18},{5,13},{24,26},{7,15},{2,0},{9,1... | collective-permute-start | bytes 3293192 | tf_op jit(solution)/shard_map/ppermute | solution.py:368
  48.6 7.4 %collective-permute-done.3 = f32[8,512,128]{2,1,0:T(8,128)S(1)} collective-permute-done((f32[8,512,128]{2,1,0:T(8,128)S(1)}, f32[8,512,128]{2,1,0:T(8,128)S(1)}, u32[]{:S(2)}, u32[]{:S(2)}) %collective-permute-start.3) | collective-permute-done | bytes 2097184 | tf_op jit(solution)/shard_map/ppermute | solution.py:368
  56.3 3.0 %collective-permute-start.5 = (f32[4,512,128]{2,1,0:T(8,128)S(1)}, f32[4,512,128]{2,1,0:T(8,128)S(1)}, u32[]{:S(2)}, u32[]{:S(2)}) collective-permute-start(f32[4,512,128]{2,1,0:T(8,128)S(1)} %get-tuple-element.30), channel_id=1, source_target_pairs={{2,4},{9,17},{10,12},{11,19},{18,20},{13,21},{26,28},{15,23},{4,2}... | collective-permute-start | bytes 3145736 | tf_op jit(solution)/shard_map/ppermute | solution.py:368
  59.4 2.8 %collective-permute-done.6 = f32[4,536,128]{2,1,0:T(8,128)S(1)} collective-permute-done((f32[4,536,128]{2,1,0:T(8,128)S(1)}, f32[4,536,128]{2,1,0:T(8,128)S(1)}, u32[]{:S(2)}, u32[]{:S(2)}) %collective-permute-start.6) | collective-permute-done | bytes 1097760 | tf_op jit(solution)/shard_map/ppermute | solution.py:368
  62.3 4.2 %collective-permute-start.8 = (f32[2,536,128]{2,1,0:T(8,128)S(1)}, f32[2,536,128]{2,1,0:T(8,128)S(1)}, u32[]{:S(2)}, u32[]{:S(2)}) collective-permute-start(f32[2,536,128]{2,1,0:T(8,128)S(1)} %get-tuple-element.33), channel_id=1, source_target_pairs={{8,16},{3,5},{10,18},{11,13},{12,20},{19,21},{14,22},{27,29},{16,8... | collective-permute-start | bytes 1646600 | tf_op jit(solution)/shard_map/ppermute | solution.py:368
  66.6 11.8 %collective-permute-done.5 = f32[4,512,128]{2,1,0:T(8,128)S(1)} collective-permute-done((f32[4,512,128]{2,1,0:T(8,128)S(1)}, f32[4,512,128]{2,1,0:T(8,128)S(1)}, u32[]{:S(2)}, u32[]{:S(2)}) %collective-permute-start.5) | collective-permute-done | bytes 1048608 | tf_op jit(solution)/shard_map/ppermute | solution.py:368
  78.9 3.1 %collective-permute-start.10 = (f32[1,536,128]{2,1,0:T(8,128)S(1)}, f32[1,536,128]{2,1,0:T(8,128)S(1)}, u32[]{:S(2)}, u32[]{:S(2)}) collective-permute-start(f32[1,536,128]{2,1,0:T(8,128)S(1)} %slice_add_fusion.9), channel_id=1, source_target_pairs={{2,4},{9,17},{10,12},{11,19},{18,20},{13,21},{26,28},{15,23},{4,2}... | collective-permute-start | bytes 823304 | tf_op jit(solution)/shard_map/ppermute | solution.py:368
  82.0 8.6 %collective-permute-done.7 = f32[2,512,128]{2,1,0:T(8,128)S(1)} collective-permute-done((f32[2,512,128]{2,1,0:T(8,128)S(1)}, f32[2,512,128]{2,1,0:T(8,128)S(1)}, u32[]{:S(2)}, u32[]{:S(2)}) %collective-permute-start.7) | collective-permute-done | bytes 524320 | tf_op jit(solution)/shard_map/ppermute | solution.py:368
  91.0 1.6 %collective-permute-start.13 = (f32[536,128]{1,0:T(8,128)S(1)}, f32[536,128]{1,0:T(8,128)S(1)}, u32[]{:S(2)}, u32[]{:S(2)}) collective-permute-start(f32[536,128]{1,0:T(8,128)S(1)} %fusion.1), channel_id=1, source_target_pairs={{0,32},{2,34},{4,36},{6,38},{8,40},{10,42},{12,44},{14,46},{16,48}... | collective-permute-start | bytes 823304 | tf_op jit(solution)/shard_map/ppermute | solution.py:382
  92.6 4.4 %collective-permute-done.9 = f32[1,512,128]{2,1,0:T(8,128)S(1)} collective-permute-done((f32[1,512,128]{2,1,0:T(8,128)S(1)}, f32[1,512,128]{2,1,0:T(8,128)S(1)}, u32[]{:S(2)}, u32[]{:S(2)}) %collective-permute-start.9) | collective-permute-done | bytes 262176 | tf_op jit(solution)/shard_map/ppermute | solution.py:368
  97.1 1.6 %collective-permute-start.11 = (f32[512,128]{1,0:T(8,128)S(1)}, f32[512,128]{1,0:T(8,128)S(1)}, u32[]{:S(2)}, u32[]{:S(2)}) collective-permute-start(f32[512,128]{1,0:T(8,128)S(1)} %fusion.3), channel_id=1, source_target_pairs={{0,32},{2,34},{4,36},{6,38},{8,40},{10,42},{12,44},{14,46},{16,48}... | collective-permute-start | bytes 786440 | tf_op jit(solution)/shard_map/ppermute | solution.py:382
  98.6 1.9 %collective-permute-done.13 = f32[536,128]{1,0:T(8,128)S(1)} collective-permute-done((f32[536,128]{1,0:T(8,128)S(1)}, f32[536,128]{1,0:T(8,128)S(1)}, u32[]{:S(2)}, u32[]{:S(2)}) %collective-permute-start.13) | collective-permute-done | bytes 274464 | tf_op jit(solution)/shard_map/ppermute | solution.py:382
  100.6 2.8 %collective-permute-start.14 = (f32[536,128]{1,0:T(8,128)S(1)}, f32[536,128]{1,0:T(8,128)S(1)}, u32[]{:S(2)}, u32[]{:S(2)}) collective-permute-start(f32[536,128]{1,0:T(8,128)S(1)} %add.71.var), channel_id=1, source_target_pairs={{32,64},{34,66},{36,68},{38,70},{40,72},{42,74},{44,76},{46,78},{4... | collective-permute-start | bytes 823304 | tf_op jit(solution)/shard_map/ppermute | solution.py:383
  103.4 2.7 %collective-permute-done.11 = f32[512,128]{1,0:T(8,128)S(1)} collective-permute-done((f32[512,128]{1,0:T(8,128)S(1)}, f32[512,128]{1,0:T(8,128)S(1)}, u32[]{:S(2)}, u32[]{:S(2)}) %collective-permute-start.11) | collective-permute-done | bytes 262176 | tf_op jit(solution)/shard_map/ppermute | solution.py:382
  106.2 2.1 %collective-permute-start.12 = (f32[512,128]{1,0:T(8,128)S(1)}, f32[512,128]{1,0:T(8,128)S(1)}, u32[]{:S(2)}, u32[]{:S(2)}) collective-permute-start(f32[512,128]{1,0:T(8,128)S(1)} %add.70.num), channel_id=1, source_target_pairs={{32,64},{34,66},{36,68},{38,70},{40,72},{42,74},{44,76},{46,78},{4... | collective-permute-start | bytes 786440 | tf_op jit(solution)/shard_map/ppermute | solution.py:383
  108.4 1.6 %cover.1 = (f32[256,256]{1,0:T(8,128)}, f32[256,256]{1,0:T(8,128)S(1)}) custom-call(f32[536,128]{1,0:T(8,128)S(1)} %add.71.var, f32[536,128]{1,0:T(8,128)S(1)} %collective-permute-done.14.got), custom_call_target="tpu_custom_call" | custom-call | flops 1000000000 | bytes 1048576 | tf_op jit(solution)/shard_map/cover/pallas_call | solution.py:332
  110.0 3.8 %collective-permute-done.12.got = f32[512,128]{1,0:T(8,128)S(1)} collective-permute-done((f32[512,128]{1,0:T(8,128)S(1)}, f32[512,128]{1,0:T(8,128)S(1)}, u32[]{:S(2)}, u32[]{:S(2)}) %collective-permute-start.12) | collective-permute-done | bytes 262176 | tf_op jit(solution)/shard_map/ppermute | solution.py:383
  (26 shorter events, 3.3 us)
Async XLA Ops:
  2.1 8.6 %collective-permute-start = (f32[16,128]{1,0:T(8,128)}, f32[16,128]{1,0:T(8,128)S(1)}, u32[]{:S(2)}, u32[]{:S(2)}) collective-permute-start(f32[16,128]{1,0:T(8,128)} %pack.1.refs_0_.refs_1_), channel_id=1, source_target_pairs={{0,1},{1,0},{2,3},{3,2},{4,5},{5,4},{6,7},{7,6},{8,9},{9,8},{10,11... | collective-permute-start | bytes 24584 | tf_op jit(solution)/shard_map/ppermute | solution.py:390
  2.1 8.7 %collective-permute-start.1 = (f32[32,128,128]{2,1,0:T(8,128)}, f32[32,128,128]{2,1,0:T(8,128)S(1)}, u32[]{:S(2)}, u32[]{:S(2)}) collective-permute-start(f32[32,128,128]{2,1,0:T(8,128)} %refs_2_.1), channel_id=1, source_target_pairs={{0,1},{1,0},{2,3},{3,2},{4,5},{5,4},{6,7},{7,6},{8,9},{9,8},{10,11... | collective-permute-start | bytes 6291464 | tf_op jit(solution)/shard_map/ppermute | solution.py:388
  2.6 8.2 %copy-start = (f32[16,128]{1,0:T(8,128)S(1)}, f32[16,128]{1,0:T(8,128)}, u32[]{:S(2)}) copy-start(f32[16,128]{1,0:T(8,128)} %pack.1.refs_0_.refs_1_) | copy-start | bytes 24580
  2.6 8.2 %copy-start.1 = (f32[32,128,128]{2,1,0:T(8,128)S(1)}, f32[32,128,128]{2,1,0:T(8,128)}, u32[]{:S(2)}) copy-start(f32[32,128,128]{2,1,0:T(8,128)} %refs_2_.1) | copy-start | bytes 6291460
  10.6 10.9 %collective-permute-start.2 = (f32[32,128,128]{2,1,0:T(8,128)S(1)}, f32[32,128,128]{2,1,0:T(8,128)S(1)}, u32[]{:S(2)}, u32[]{:S(2)}) collective-permute-start(f32[32,128,128]{2,1,0:T(8,128)S(1)} %match.1.refs_3_), channel_id=1, source_target_pairs={{0,1},{1,0},{2,3},{3,2},{4,5},{5,4},{6,7},{7,6},{8,9},{9,8},{10,11... | collective-permute-start | bytes 6291464 | tf_op jit(solution)/shard_map/ppermute | solution.py:393
  19.4 27.2 %collective-permute-start.4 = (f32[8,536,128]{2,1,0:T(8,128)S(1)}, f32[8,536,128]{2,1,0:T(8,128)S(1)}, u32[]{:S(2)}, u32[]{:S(2)}) collective-permute-start(f32[8,536,128]{2,1,0:T(8,128)S(1)} %get-tuple-element.21), channel_id=1, source_target_pairs={{0,8},{1,3},{2,10},{9,11},{4,12},{17,19},{6,14},{25,27},{8,0},{3,1... | collective-permute-start | bytes 6586376 | tf_op jit(solution)/shard_map/ppermute | solution.py:368
  28.7 27.3 %collective-permute-start.3 = (f32[8,512,128]{2,1,0:T(8,128)S(1)}, f32[8,512,128]{2,1,0:T(8,128)S(1)}, u32[]{:S(2)}, u32[]{:S(2)}) collective-permute-start(f32[8,512,128]{2,1,0:T(8,128)S(1)} %get-tuple-element.19), channel_id=1, source_target_pairs={{8,16},{3,5},{10,18},{11,13},{12,20},{19,21},{14,22},{27,29},{16,8... | collective-permute-start | bytes 6291464 | tf_op jit(solution)/shard_map/ppermute | solution.py:368
  46.8 15.4 %collective-permute-start.6 = (f32[4,536,128]{2,1,0:T(8,128)S(1)}, f32[4,536,128]{2,1,0:T(8,128)S(1)}, u32[]{:S(2)}, u32[]{:S(2)}) collective-permute-start(f32[4,536,128]{2,1,0:T(8,128)S(1)} %get-tuple-element.29), channel_id=1, source_target_pairs={{0,2},{1,9},{8,10},{3,11},{16,18},{5,13},{24,26},{7,15},{2,0},{9,1... | collective-permute-start | bytes 3293192 | tf_op jit(solution)/shard_map/ppermute | solution.py:368
  56.3 22.0 %collective-permute-start.5 = (f32[4,512,128]{2,1,0:T(8,128)S(1)}, f32[4,512,128]{2,1,0:T(8,128)S(1)}, u32[]{:S(2)}, u32[]{:S(2)}) collective-permute-start(f32[4,512,128]{2,1,0:T(8,128)S(1)} %get-tuple-element.30), channel_id=1, source_target_pairs={{2,4},{9,17},{10,12},{11,19},{18,20},{13,21},{26,28},{15,23},{4,2}... | collective-permute-start | bytes 3145736 | tf_op jit(solution)/shard_map/ppermute | solution.py:368
  62.3 16.5 %collective-permute-start.8 = (f32[2,536,128]{2,1,0:T(8,128)S(1)}, f32[2,536,128]{2,1,0:T(8,128)S(1)}, u32[]{:S(2)}, u32[]{:S(2)}) collective-permute-start(f32[2,536,128]{2,1,0:T(8,128)S(1)} %get-tuple-element.33), channel_id=1, source_target_pairs={{8,16},{3,5},{10,18},{11,13},{12,20},{19,21},{14,22},{27,29},{16,8... | collective-permute-start | bytes 1646600 | tf_op jit(solution)/shard_map/ppermute | solution.py:368
  78.5 12.1 %collective-permute-start.7 = (f32[2,512,128]{2,1,0:T(8,128)S(1)}, f32[2,512,128]{2,1,0:T(8,128)S(1)}, u32[]{:S(2)}, u32[]{:S(2)}) collective-permute-start(f32[2,512,128]{2,1,0:T(8,128)S(1)} %get-tuple-element.34), channel_id=1, source_target_pairs={{0,8},{1,3},{2,10},{9,11},{4,12},{17,19},{6,14},{25,27},{8,0},{3,1... | collective-permute-start | bytes 1572872 | tf_op jit(solution)/shard_map/ppermute | solution.py:368
  78.9 12.1 %collective-permute-start.10 = (f32[1,536,128]{2,1,0:T(8,128)S(1)}, f32[1,536,128]{2,1,0:T(8,128)S(1)}, u32[]{:S(2)}, u32[]{:S(2)}) collective-permute-start(f32[1,536,128]{2,1,0:T(8,128)S(1)} %slice_add_fusion.9), channel_id=1, source_target_pairs={{2,4},{9,17},{10,12},{11,19},{18,20},{13,21},{26,28},{15,23},{4,2}... | collective-permute-start | bytes 823304 | tf_op jit(solution)/shard_map/ppermute | solution.py:368
  90.6 6.5 %collective-permute-start.9 = (f32[1,512,128]{2,1,0:T(8,128)S(1)}, f32[1,512,128]{2,1,0:T(8,128)S(1)}, u32[]{:S(2)}, u32[]{:S(2)}) collective-permute-start(f32[1,512,128]{2,1,0:T(8,128)S(1)} %slice_add_fusion.10), channel_id=1, source_target_pairs={{0,2},{1,9},{8,10},{3,11},{16,18},{5,13},{24,26},{7,15},{2,0},{9,1... | collective-permute-start | bytes 786440 | tf_op jit(solution)/shard_map/ppermute | solution.py:368
  91.0 9.5 %collective-permute-start.13 = (f32[536,128]{1,0:T(8,128)S(1)}, f32[536,128]{1,0:T(8,128)S(1)}, u32[]{:S(2)}, u32[]{:S(2)}) collective-permute-start(f32[536,128]{1,0:T(8,128)S(1)} %fusion.1), channel_id=1, source_target_pairs={{0,32},{2,34},{4,36},{6,38},{8,40},{10,42},{12,44},{14,46},{16,48}... | collective-permute-start | bytes 823304 | tf_op jit(solution)/shard_map/ppermute | solution.py:382
  97.1 9.1 %collective-permute-start.11 = (f32[512,128]{1,0:T(8,128)S(1)}, f32[512,128]{1,0:T(8,128)S(1)}, u32[]{:S(2)}, u32[]{:S(2)}) collective-permute-start(f32[512,128]{1,0:T(8,128)S(1)} %fusion.3), channel_id=1, source_target_pairs={{0,32},{2,34},{4,36},{6,38},{8,40},{10,42},{12,44},{14,46},{16,48}... | collective-permute-start | bytes 786440 | tf_op jit(solution)/shard_map/ppermute | solution.py:382
  100.6 7.8 %collective-permute-start.14 = (f32[536,128]{1,0:T(8,128)S(1)}, f32[536,128]{1,0:T(8,128)S(1)}, u32[]{:S(2)}, u32[]{:S(2)}) collective-permute-start(f32[536,128]{1,0:T(8,128)S(1)} %add.71.var), channel_id=1, source_target_pairs={{32,64},{34,66},{36,68},{38,70},{40,72},{42,74},{44,76},{46,78},{4... | collective-permute-start | bytes 823304 | tf_op jit(solution)/shard_map/ppermute | solution.py:383
  106.2 7.7 %collective-permute-start.12 = (f32[512,128]{1,0:T(8,128)S(1)}, f32[512,128]{1,0:T(8,128)S(1)}, u32[]{:S(2)}, u32[]{:S(2)}) collective-permute-start(f32[512,128]{1,0:T(8,128)S(1)} %add.70.num), channel_id=1, source_target_pairs={{32,64},{34,66},{36,68},{38,70},{40,72},{42,74},{44,76},{46,78},{4... | collective-permute-start | bytes 786440 | tf_op jit(solution)/shard_map/ppermute | solution.py:383

commit v6 on v5

--- a/solution.py
+++ b/solution.py
@@ -169,12 +169,12 @@
 def warp_kernel(with_meta, *refs):
     if with_meta:
         own, other, own_tiles, other_tiles = refs[:4]
-        outs, slots = refs[4:6], refs[6]
-        stage, acc, meta, weights = refs[7:]
+        outs, slots = refs[4:8], refs[8]
+        stage, acc, meta, weights = refs[9:]
     else:
         slots, own, other, own_tiles, other_tiles = refs[:5]
-        outs = refs[5:7]
-        stage, acc = refs[7:]
+        outs = refs[5:9]
+        stage, acc = refs[9:]
     lane = lax.broadcasted_iota(jnp.int32, (8, TS), 1)
     stage[:, :, 0:8, :] = jnp.zeros((2 * UNROLL, 2, 8, TS), F32)
     stage[:, :, 8 + TS :, :] = jnp.zeros((2 * UNROLL, 2, 8, TS), F32)
@@ -260,20 +260,20 @@
 
     for k in range(16):
         a, b, c, d = k >> 3, (k >> 2) & 1, (k >> 1) & 1, k & 1
-        if not with_meta:
-            a, b, c, d = b, a, d, c
-        out, at = outs[a], c * 4 + b * 2 + d
-        out[at, 0:PATCH, :] = acc[4 * k + 1, PAD : PAD + PATCH, :]
-        out[at, PATCH : 2 * PATCH, :] = acc[4 * k + 2, PAD : PAD + PATCH, :]
+        rest = 2 * c + d if with_meta else 2 * d + c
+        left, right = outs[a], outs[2 + b]
+        left[4 * b + rest, 0:PATCH, :] = acc[4 * k + 1, PAD : PAD + PATCH, :]
+        right[4 * a + rest, :, :] = acc[4 * k + 2, PAD : PAD + PATCH, :]
         if with_meta:
             for slot in range(CAP):
-                out[at, 2 * PATCH + 8 * slot : 2 * PATCH + 8 * slot + 8, :] = meta[k * CAP + slot]
+                left[4 * b + rest, PATCH + 8 * slot : PATCH + 8 * slot + 8, :] = meta[k * CAP + slot]
 
 
 def warp(with_meta, *args):
     smem, vmem = pl.BlockSpec(memory_space=pltpu.SMEM), pl.BlockSpec(memory_space=pltpu.VMEM)
-    rows = 2 * PATCH + META if with_meta else 2 * PATCH
-    outs, specs = [jax.ShapeDtypeStruct((8, rows, TS), F32)] * 2, [vmem] * 2
+    left = jax.ShapeDtypeStruct((8, PATCH + META if with_meta else PATCH, TS), F32)
+    right = jax.ShapeDtypeStruct((8, PATCH, TS), F32)
+    outs, specs = [left, left, right, right], [vmem] * 4
     scratch = [
         pltpu.VMEM((2 * UNROLL, 2, TS + 16, TS), F32),
         pltpu.VMEM((64, 384, TS), F32),
@@ -306,7 +306,7 @@
 
     den = jnp.zeros((PATCH, PATCH), F32)
     for slot in range(CAP):
-        at = 2 * PATCH + 8 * slot
+        at = PATCH + 8 * slot
         fields = var[at : at + 8, :] + got[at : at + 8, :]
         weight, row, col, frac_row, frac_col = (fields[f : f + 1, :] for f in range(5))
         down, across = cover(row, frac_row) * weight, cover(col, frac_col)
@@ -316,7 +316,8 @@
     safe = jnp.maximum(den, 1.0)
     safe_ref[...] = safe
     for half in range(2):
-        rows, lanes = slice(half * PATCH, (half + 1) * PATCH), slice(half * TS, (half + 1) * TS)
+        lo = half * (PATCH + META)
+        rows, lanes = slice(lo, lo + PATCH), slice(half * TS, (half + 1) * TS)
         part = safe[:, lanes]
         coadd_var[:, lanes] = (var[rows, :] + got[rows, :]) / (part * part)
 
@@ -362,20 +363,30 @@
     ]
 
 
-def halve(keep, send, order, ahead=()):
-    left_over = []
-    for step, (axis, edge) in enumerate(order):
-        got = lax.ppermute(send, "patch", over_patch(axis, edge))
-        if step < len(ahead):
-            got, _ = lax.optimization_barrier((got, ahead[step]))
-        if step < 3:
-            n = 8 >> (step + 1)
-            keep, send = keep[:n] + got[:n], keep[n:] + got[n:]
-            left_over.append(send)
-        else:
-            keep = keep[0] + got[0]
-            left_over.append(keep)
-    return keep, left_over
+def halve(left_keep, left_send, right_keep, right_send, last, ahead=()):
+    def after(step, *got):
+        return lax.optimization_barrier((*got, *ahead[step]))[: len(got)] if step < len(ahead) else got
+
+    left, right = after(
+        0, lax.ppermute(left_send, "patch", over_patch(0, 0)), lax.ppermute(right_send, "patch", over_patch(0, 1))
+    )
+    left_keep, left_send = left_keep[:4] + left[:4], left_keep[4:] + left[4:]
+    right_keep, right_send = right_keep[:4] + right[:4], right_keep[4:] + right[4:]
+    left_over = [(left_send, right_send)]
+    left, right = after(
+        1, lax.ppermute(left_send, "patch", over_patch(0, 1)), lax.ppermute(right_send, "patch", over_patch(0, 0))
+    )
+    keep, send = (
+        jnp.concatenate([left_keep[part] + left[part], right_keep[part] + right[part]], 1)
+        for part in (slice(0, 2), slice(2, 4))
+    )
+    left_over.append((send,))
+    (got,) = after(2, lax.ppermute(send, "patch", over_patch(1, last)))
+    keep, send = keep[:1] + got[:1], keep[1:] + got[1:]
+    left_over.append((send,))
+    (got,) = after(3, lax.ppermute(send, "patch", over_patch(1, 1 - last)))
+    left_over.append((keep[0] + got[0],))
+    return left_over[-1][0], left_over
 
 
 def double(x):
@@ -391,10 +402,10 @@
     matched = match(basis_ids, coefs, taps, image, variance)
     matched, other_table = lax.optimization_barrier((matched, other_table))
     other_matched = lax.ppermute(matched, "patch", swap)
-    var_keep, var_send, slots = warp(True, table, other_table, variance, other_variance)
-    num_keep, num_send = warp(False, slots, table, other_table, matched, other_matched)
-    var, ahead = halve(var_keep, var_send, ((0, 0), (1, 0), (0, 1), (1, 1)))
-    num, _ = halve(num_keep, num_send, ((0, 1), (1, 1), (0, 0), (1, 0)), ahead)
+    *var, slots = warp(True, table, other_table, variance, other_variance)
+    num = warp(False, slots, table, other_table, matched, other_matched)
+    var, ahead = halve(*var, 0)
+    num, _ = halve(*num, 1, ahead)
     var, num = double(var), double(num)
     coadd_var, safe = finish(cover_kernel, "cover", 2, *var)
     (coadd,) = finish(divide_kernel, "divide", 1, *num, safe)

time: 115 us -> 102 us (0.89)
  the two profiles are of different devices: /device:TPU:0 before, /device:TPU:24 now
where the time goes in v6:
time: 102 us; the launch traced here: 101 us
  waiting for transfers between devices  46.8 us (46%)
  Pallas kernels  26.4 us (26%)
  starting transfers between devices  25.8 us (25%)
  other arithmetic  1.02 us (1%)
    pallas_call x2, Pallas kernels, warp(): pl.pallas_call(functools.partial(warp_kernel, with_meta), out_shape=outs,...  14.6 us
    pallas_call x1, Pallas kernels, match(): pl.pallas_call(match_kernel, out_shape=jax.ShapeDtypeStruct((TILES, TS, T...  8.03 us
    ppermute x2, waiting for transfers between devices, halve(): lax.ppermute(right_send, 'patch', over_patch(0, 1))  7.35 us
    ppermute x2, waiting for transfers between devices, halve(): lax.ppermute(left_send, 'patch', over_patch(0, 1))  7.06 us
    ppermute x2, waiting for transfers between devices, halve(): got, = after(2, lax.ppermute(send, 'patch', over_patch(1, last)))  7.04 us
    ppermute x2, waiting for transfers between devices, double(): x = x + lax.ppermute(x, ('visit', 'patch'), over_visit(0))  6.59 us
    ppermute x2, waiting for transfers between devices, halve(): lax.ppermute(left_send, 'patch', over_patch(0, 0))  5.79 us
    ppermute x2, starting transfers between devices, double(): return (x, lax.ppermute(x, ('visit', 'patch'), over_visit(1)))  5.64 us
  transfers between devices with their start and end apart: 19, of which 13 were waited for; matrix products, arithmetic and copies ran while one was open for 1% of the time, Pallas kernels for 24%

profile of v6, /device:TPU:24, one launch (start us, length us, event | category | flops | bytes accessed | tf_op | source)
XLA Modules:
  0.0 100.9 jit_solution(1545142116060289987)
XLA Ops:
  2.6 8.0 %match.1.refs_3_ = f32[32,128,128]{2,1,0:T(8,128)S(1)} custom-call(s32[3,32]{1,0:T(4,128)} %bitcast.12, f32[3,32]{1,0:T(4,128)} %bitcast.13, f32[8,2,41]{2,1,0:T(2,128)} %taps_hbm.1, f32[32,128,128]{2,1,0:T(8,128)} %image_hbm.1, f32[32,128,128]{2,1,0:T(8,128)} %refs_2_.1), custom_call_target="tpu_custom_call" | custom-call | flops 99999997952 | bytes 6291456 | tf_op jit(solution)/shard_map/match/pallas_call | solution.py:148
  10.8 8.1 %warp_meta.1 = (f32[8,280,128]{2,1,0:T(8,128)S(1)}, f32[8,280,128]{2,1,0:T(8,128)S(1)}, f32[8,256,128]{2,1,0:T(8,128)S(1)}, f32[8,256,128]{2,1,0:T(8,128)S(1)}, s32[2,128]{1,0:T(2,128)S(1)}) custom-call(f32[16,128]{1,0:T(8,128)S(1)} %copy-done, f32[16,128]{1,0:T(8,128)S(1)} %collective-permute-done.refs_1_.refs_2_, f32[32,128,128]{2,1,0:T(8,128)S(1)} %copy-done.1, ...), custom_call_target="tpu_custom_call" | custom-call | flops 10000000000 | bytes 8388608 | tf_op jit(solution)/shard_map/warp_meta/pallas_call | solution.py:287
  18.8 2.0 %collective-permute-start.5 = (f32[8,280,128]{2,1,0:T(8,128)S(1)}, f32[8,280,128]{2,1,0:T(8,128)S(1)}, u32[]{:S(2)}, u32[]{:S(2)}) collective-permute-start(f32[8,280,128]{2,1,0:T(8,128)S(1)} %get-tuple-element.28), channel_id=1, source_target_pairs={{0,8},{1,3},{2,10},{9,11},{4,12},{17,19},{6,14},{25,27},{8,0},{3,1... | collective-permute-start | bytes 3440648 | tf_op jit(solution)/shard_map/ppermute | solution.py:371
  20.9 2.5 %collective-permute-start.6 = (f32[8,256,128]{2,1,0:T(8,128)S(1)}, f32[8,256,128]{2,1,0:T(8,128)S(1)}, u32[]{:S(2)}, u32[]{:S(2)}) collective-permute-start(f32[8,256,128]{2,1,0:T(8,128)S(1)} %get-tuple-element.30), channel_id=1, source_target_pairs={{8,16},{3,5},{10,18},{11,13},{12,20},{19,21},{14,22},{27,29},{16,8... | collective-permute-start | bytes 3145736 | tf_op jit(solution)/shard_map/ppermute | solution.py:371
  23.4 6.5 %warp.1 = (f32[8,256,128]{2,1,0:T(8,128)S(1)}, f32[8,256,128]{2,1,0:T(8,128)S(1)}, f32[8,256,128]{2,1,0:T(8,128)S(1)}, f32[8,256,128]{2,1,0:T(8,128)S(1)}) custom-call(s32[2,128]{1,0:T(2,128)S(1)} %get-tuple-element.22.refs_0_, f32[16,128]{1,0:T(8,128)S(1)} %copy-done, f32[16,128]{1,0:T(8,128)S(1)} %collective-permute-done.refs_1_.refs_2_, ...), custom_call_target="tpu_custom_call" | custom-call | flops 10000000000 | bytes 8388608 | tf_op jit(solution)/shard_map/warp/pallas_call | solution.py:287
  31.6 5.3 %collective-permute-done.6 = f32[8,256,128]{2,1,0:T(8,128)S(1)} collective-permute-done((f32[8,256,128]{2,1,0:T(8,128)S(1)}, f32[8,256,128]{2,1,0:T(8,128)S(1)}, u32[]{:S(2)}, u32[]{:S(2)}) %collective-permute-start.6) | collective-permute-done | bytes 1048608 | tf_op jit(solution)/shard_map/ppermute | solution.py:371
  37.5 2.7 %collective-permute-start.9 = (f32[4,280,128]{2,1,0:T(8,128)S(1)}, f32[4,280,128]{2,1,0:T(8,128)S(1)}, u32[]{:S(2)}, u32[]{:S(2)}) collective-permute-start(f32[4,280,128]{2,1,0:T(8,128)S(1)} %get-tuple-element.41), channel_id=1, source_target_pairs={{8,16},{3,5},{10,18},{11,13},{12,20},{19,21},{14,22},{27,29},{16,8... | collective-permute-start | bytes 1720328 | tf_op jit(solution)/shard_map/ppermute | solution.py:377
  40.2 5.8 %collective-permute-done.3 = f32[8,256,128]{2,1,0:T(8,128)S(1)} collective-permute-done((f32[8,256,128]{2,1,0:T(8,128)S(1)}, f32[8,256,128]{2,1,0:T(8,128)S(1)}, u32[]{:S(2)}, u32[]{:S(2)}) %collective-permute-start.3) | collective-permute-done | bytes 1048608 | tf_op jit(solution)/shard_map/ppermute | solution.py:371
  46.0 2.1 %collective-permute-done.4 = f32[8,256,128]{2,1,0:T(8,128)S(1)} collective-permute-done((f32[8,256,128]{2,1,0:T(8,128)S(1)}, f32[8,256,128]{2,1,0:T(8,128)S(1)}, u32[]{:S(2)}, u32[]{:S(2)}) %collective-permute-start.4) | collective-permute-done | bytes 1048608 | tf_op jit(solution)/shard_map/ppermute | solution.py:371
  48.2 2.6 %collective-permute-start.7 = (f32[4,256,128]{2,1,0:T(8,128)S(1)}, f32[4,256,128]{2,1,0:T(8,128)S(1)}, u32[]{:S(2)}, u32[]{:S(2)}) collective-permute-start(f32[4,256,128]{2,1,0:T(8,128)S(1)} %get-tuple-element.43), channel_id=1, source_target_pairs={{8,16},{3,5},{10,18},{11,13},{12,20},{19,21},{14,22},{27,29},{16,8... | collective-permute-start | bytes 1572872 | tf_op jit(solution)/shard_map/ppermute | solution.py:377
  51.7 2.5 %collective-permute-done.9 = f32[4,280,128]{2,1,0:T(8,128)S(1)} collective-permute-done((f32[4,280,128]{2,1,0:T(8,128)S(1)}, f32[4,280,128]{2,1,0:T(8,128)S(1)}, u32[]{:S(2)}, u32[]{:S(2)}) %collective-permute-start.9) | collective-permute-done | bytes 573472 | tf_op jit(solution)/shard_map/ppermute | solution.py:377
  55.3 4.5 %collective-permute-done.7 = f32[4,256,128]{2,1,0:T(8,128)S(1)} collective-permute-done((f32[4,256,128]{2,1,0:T(8,128)S(1)}, f32[4,256,128]{2,1,0:T(8,128)S(1)}, u32[]{:S(2)}, u32[]{:S(2)}) %collective-permute-start.7) | collective-permute-done | bytes 524320 | tf_op jit(solution)/shard_map/ppermute | solution.py:377
  59.9 4.4 %collective-permute-done.8 = f32[4,256,128]{2,1,0:T(8,128)S(1)} collective-permute-done((f32[4,256,128]{2,1,0:T(8,128)S(1)}, f32[4,256,128]{2,1,0:T(8,128)S(1)}, u32[]{:S(2)}, u32[]{:S(2)}) %collective-permute-start.8) | collective-permute-done | bytes 524320 | tf_op jit(solution)/shard_map/ppermute | solution.py:377
  64.6 3.3 %collective-permute-start.14 = (f32[1,536,128]{2,1,0:T(8,128)S(1)}, f32[1,536,128]{2,1,0:T(8,128)S(1)}, u32[]{:S(2)}, u32[]{:S(2)}) collective-permute-start(f32[1,536,128]{2,1,0:T(8,128)S(1)} %fusion.1), channel_id=1, source_target_pairs={{2,4},{9,17},{10,12},{11,19},{18,20},{13,21},{26,28},{15,23},{4,2}... | collective-permute-start | bytes 823304 | tf_op jit(solution)/shard_map/ppermute | solution.py:387
  67.9 7.0 %collective-permute-done.11 = f32[2,512,128]{2,1,0:T(8,128)S(1)} collective-permute-done((f32[2,512,128]{2,1,0:T(8,128)S(1)}, f32[2,512,128]{2,1,0:T(8,128)S(1)}, u32[]{:S(2)}, u32[]{:S(2)}) %collective-permute-start.11) | collective-permute-done | bytes 524320 | tf_op jit(solution)/shard_map/ppermute | solution.py:384
  75.1 2.8 %collective-permute-done.14 = f32[1,536,128]{2,1,0:T(8,128)S(1)} collective-permute-done((f32[1,536,128]{2,1,0:T(8,128)S(1)}, f32[1,536,128]{2,1,0:T(8,128)S(1)}, u32[]{:S(2)}, u32[]{:S(2)}) %collective-permute-start.14) | collective-permute-done | bytes 274464 | tf_op jit(solution)/shard_map/ppermute | solution.py:387
  79.5 1.9 %collective-permute-done.13 = f32[1,512,128]{2,1,0:T(8,128)S(1)} collective-permute-done((f32[1,512,128]{2,1,0:T(8,128)S(1)}, f32[1,512,128]{2,1,0:T(8,128)S(1)}, u32[]{:S(2)}, u32[]{:S(2)}) %collective-permute-start.13) | collective-permute-done | bytes 262176 | tf_op jit(solution)/shard_map/ppermute | solution.py:387
  81.5 1.5 %collective-permute-start.15 = (f32[512,128]{1,0:T(8,128)S(1)}, f32[512,128]{1,0:T(8,128)S(1)}, u32[]{:S(2)}, u32[]{:S(2)}) collective-permute-start(f32[512,128]{1,0:T(8,128)S(1)} %fusion.7), channel_id=1, source_target_pairs={{0,32},{2,34},{4,36},{6,38},{8,40},{10,42},{12,44},{14,46},{16,48}... | collective-permute-start | bytes 786440 | tf_op jit(solution)/shard_map/ppermute | solution.py:393
  83.0 3.8 %collective-permute-done.17 = f32[536,128]{1,0:T(8,128)S(1)} collective-permute-done((f32[536,128]{1,0:T(8,128)S(1)}, f32[536,128]{1,0:T(8,128)S(1)}, u32[]{:S(2)}, u32[]{:S(2)}) %collective-permute-start.17) | collective-permute-done | bytes 274464 | tf_op jit(solution)/shard_map/ppermute | solution.py:393
  86.9 2.8 %collective-permute-start.18 = (f32[536,128]{1,0:T(8,128)S(1)}, f32[536,128]{1,0:T(8,128)S(1)}, u32[]{:S(2)}, u32[]{:S(2)}) collective-permute-start(f32[536,128]{1,0:T(8,128)S(1)} %add.103.var), channel_id=1, source_target_pairs={{32,64},{34,66},{36,68},{38,70},{40,72},{42,74},{44,76},{46,78},{4... | collective-permute-start | bytes 823304 | tf_op jit(solution)/shard_map/ppermute | solution.py:394
  89.7 2.8 %collective-permute-done.15 = f32[512,128]{1,0:T(8,128)S(1)} collective-permute-done((f32[512,128]{1,0:T(8,128)S(1)}, f32[512,128]{1,0:T(8,128)S(1)}, u32[]{:S(2)}, u32[]{:S(2)}) %collective-permute-start.15) | collective-permute-done | bytes 262176 | tf_op jit(solution)/shard_map/ppermute | solution.py:393
  92.5 2.8 %collective-permute-start.16 = (f32[512,128]{1,0:T(8,128)S(1)}, f32[512,128]{1,0:T(8,128)S(1)}, u32[]{:S(2)}, u32[]{:S(2)}) collective-permute-start(f32[512,128]{1,0:T(8,128)S(1)} %add.102.num), channel_id=1, source_target_pairs={{32,64},{34,66},{36,68},{38,70},{40,72},{42,74},{44,76},{46,78},{4... | collective-permute-start | bytes 786440 | tf_op jit(solution)/shard_map/ppermute | solution.py:394
  95.3 1.7 %cover.1 = (f32[256,256]{1,0:T(8,128)}, f32[256,256]{1,0:T(8,128)S(1)}) custom-call(f32[536,128]{1,0:T(8,128)S(1)} %add.103.var, f32[536,128]{1,0:T(8,128)S(1)} %collective-permute-done.18.got), custom_call_target="tpu_custom_call" | custom-call | flops 1000000000 | bytes 1048576 | tf_op jit(solution)/shard_map/cover/pallas_call | solution.py:333
  97.0 3.2 %collective-permute-done.16.got = f32[512,128]{1,0:T(8,128)S(1)} collective-permute-done((f32[512,128]{1,0:T(8,128)S(1)}, f32[512,128]{1,0:T(8,128)S(1)}, u32[]{:S(2)}, u32[]{:S(2)}) %collective-permute-start.16) | collective-permute-done | bytes 262176 | tf_op jit(solution)/shard_map/ppermute | solution.py:394
  (39 shorter events, 9.4 us)
Async XLA Ops:
  2.1 8.6 %collective-permute-start = (f32[16,128]{1,0:T(8,128)}, f32[16,128]{1,0:T(8,128)S(1)}, u32[]{:S(2)}, u32[]{:S(2)}) collective-permute-start(f32[16,128]{1,0:T(8,128)} %pack.1.refs_0_.refs_1_), channel_id=1, source_target_pairs={{0,1},{1,0},{2,3},{3,2},{4,5},{5,4},{6,7},{7,6},{8,9},{9,8},{10,11... | collective-permute-start | bytes 24584 | tf_op jit(solution)/shard_map/ppermute | solution.py:401
  2.1 8.7 %collective-permute-start.1 = (f32[32,128,128]{2,1,0:T(8,128)}, f32[32,128,128]{2,1,0:T(8,128)S(1)}, u32[]{:S(2)}, u32[]{:S(2)}) collective-permute-start(f32[32,128,128]{2,1,0:T(8,128)} %refs_2_.1), channel_id=1, source_target_pairs={{0,1},{1,0},{2,3},{3,2},{4,5},{5,4},{6,7},{7,6},{8,9},{9,8},{10,11... | collective-permute-start | bytes 6291464 | tf_op jit(solution)/shard_map/ppermute | solution.py:399
  2.6 8.2 %copy-start = (f32[16,128]{1,0:T(8,128)S(1)}, f32[16,128]{1,0:T(8,128)}, u32[]{:S(2)}) copy-start(f32[16,128]{1,0:T(8,128)} %pack.1.refs_0_.refs_1_) | copy-start | bytes 24580
  2.6 8.2 %copy-start.1 = (f32[32,128,128]{2,1,0:T(8,128)S(1)}, f32[32,128,128]{2,1,0:T(8,128)}, u32[]{:S(2)}) copy-start(f32[32,128,128]{2,1,0:T(8,128)} %refs_2_.1) | copy-start | bytes 6291460
  10.6 12.7 %collective-permute-start.2 = (f32[32,128,128]{2,1,0:T(8,128)S(1)}, f32[32,128,128]{2,1,0:T(8,128)S(1)}, u32[]{:S(2)}, u32[]{:S(2)}) collective-permute-start(f32[32,128,128]{2,1,0:T(8,128)S(1)} %match.1.refs_3_), channel_id=1, source_target_pairs={{0,1},{1,0},{2,3},{3,2},{4,5},{5,4},{6,7},{7,6},{8,9},{9,8},{10,11... | collective-permute-start | bytes 6291464 | tf_op jit(solution)/shard_map/ppermute | solution.py:404
  18.8 18.6 %collective-permute-start.5 = (f32[8,280,128]{2,1,0:T(8,128)S(1)}, f32[8,280,128]{2,1,0:T(8,128)S(1)}, u32[]{:S(2)}, u32[]{:S(2)}) collective-permute-start(f32[8,280,128]{2,1,0:T(8,128)S(1)} %get-tuple-element.28), channel_id=1, source_target_pairs={{0,8},{1,3},{2,10},{9,11},{4,12},{17,19},{6,14},{25,27},{8,0},{3,1... | collective-permute-start | bytes 3440648 | tf_op jit(solution)/shard_map/ppermute | solution.py:371
  20.9 16.0 %collective-permute-start.6 = (f32[8,256,128]{2,1,0:T(8,128)S(1)}, f32[8,256,128]{2,1,0:T(8,128)S(1)}, u32[]{:S(2)}, u32[]{:S(2)}) collective-permute-start(f32[8,256,128]{2,1,0:T(8,128)S(1)} %get-tuple-element.30), channel_id=1, source_target_pairs={{8,16},{3,5},{10,18},{11,13},{12,20},{19,21},{14,22},{27,29},{16,8... | collective-permute-start | bytes 3145736 | tf_op jit(solution)/shard_map/ppermute | solution.py:371
  29.9 16.1 %collective-permute-start.3 = (f32[8,256,128]{2,1,0:T(8,128)S(1)}, f32[8,256,128]{2,1,0:T(8,128)S(1)}, u32[]{:S(2)}, u32[]{:S(2)}) collective-permute-start(f32[8,256,128]{2,1,0:T(8,128)S(1)} %get-tuple-element.25), channel_id=1, source_target_pairs={{0,8},{1,3},{2,10},{9,11},{4,12},{17,19},{6,14},{25,27},{8,0},{3,1... | collective-permute-start | bytes 3145736 | tf_op jit(solution)/shard_map/ppermute | solution.py:371
  31.0 17.1 %collective-permute-start.4 = (f32[8,256,128]{2,1,0:T(8,128)S(1)}, f32[8,256,128]{2,1,0:T(8,128)S(1)}, u32[]{:S(2)}, u32[]{:S(2)}) collective-permute-start(f32[8,256,128]{2,1,0:T(8,128)S(1)} %get-tuple-element.26), channel_id=1, source_target_pairs={{8,16},{3,5},{10,18},{11,13},{12,20},{19,21},{14,22},{27,29},{16,8... | collective-permute-start | bytes 3145736 | tf_op jit(solution)/shard_map/ppermute | solution.py:371
  37.0 14.6 %collective-permute-start.10 = (f32[4,256,128]{2,1,0:T(8,128)S(1)}, f32[4,256,128]{2,1,0:T(8,128)S(1)}, u32[]{:S(2)}, u32[]{:S(2)}) collective-permute-start(f32[4,256,128]{2,1,0:T(8,128)S(1)} %get-tuple-element.45), channel_id=1, source_target_pairs={{0,8},{1,3},{2,10},{9,11},{4,12},{17,19},{6,14},{25,27},{8,0},{3,1... | collective-permute-start | bytes 1572872 | tf_op jit(solution)/shard_map/ppermute | solution.py:377
  37.5 16.7 %collective-permute-start.9 = (f32[4,280,128]{2,1,0:T(8,128)S(1)}, f32[4,280,128]{2,1,0:T(8,128)S(1)}, u32[]{:S(2)}, u32[]{:S(2)}) collective-permute-start(f32[4,280,128]{2,1,0:T(8,128)S(1)} %get-tuple-element.41), channel_id=1, source_target_pairs={{8,16},{3,5},{10,18},{11,13},{12,20},{19,21},{14,22},{27,29},{16,8... | collective-permute-start | bytes 1720328 | tf_op jit(solution)/shard_map/ppermute | solution.py:377
  48.2 11.6 %collective-permute-start.7 = (f32[4,256,128]{2,1,0:T(8,128)S(1)}, f32[4,256,128]{2,1,0:T(8,128)S(1)}, u32[]{:S(2)}, u32[]{:S(2)}) collective-permute-start(f32[4,256,128]{2,1,0:T(8,128)S(1)} %get-tuple-element.43), channel_id=1, source_target_pairs={{8,16},{3,5},{10,18},{11,13},{12,20},{19,21},{14,22},{27,29},{16,8... | collective-permute-start | bytes 1572872 | tf_op jit(solution)/shard_map/ppermute | solution.py:377
  50.9 13.4 %collective-permute-start.8 = (f32[4,256,128]{2,1,0:T(8,128)S(1)}, f32[4,256,128]{2,1,0:T(8,128)S(1)}, u32[]{:S(2)}, u32[]{:S(2)}) collective-permute-start(f32[4,256,128]{2,1,0:T(8,128)S(1)} %get-tuple-element.46), channel_id=1, source_target_pairs={{0,8},{1,3},{2,10},{9,11},{4,12},{17,19},{6,14},{25,27},{8,0},{3,1... | collective-permute-start | bytes 1572872 | tf_op jit(solution)/shard_map/ppermute | solution.py:377
  54.4 10.2 %collective-permute-start.12 = (f32[2,536,128]{2,1,0:T(8,128)S(1)}, f32[2,536,128]{2,1,0:T(8,128)S(1)}, u32[]{:S(2)}, u32[]{:S(2)}) collective-permute-start(f32[2,536,128]{2,1,0:T(8,128)S(1)} %pad_maximum_fusion), channel_id=1, source_target_pairs={{0,2},{1,9},{8,10},{3,11},{16,18},{5,13},{24,26},{7,15},{2,0},{9,1... | collective-permute-start | bytes 1646600 | tf_op jit(solution)/shard_map/ppermute | solution.py:384
  64.5 10.5 %collective-permute-start.11 = (f32[2,512,128]{2,1,0:T(8,128)S(1)}, f32[2,512,128]{2,1,0:T(8,128)S(1)}, u32[]{:S(2)}, u32[]{:S(2)}) collective-permute-start(f32[2,512,128]{2,1,0:T(8,128)S(1)} %pad_maximum_fusion.1), channel_id=1, source_target_pairs={{2,4},{9,17},{10,12},{11,19},{18,20},{13,21},{26,28},{15,23},{4,2}... | collective-permute-start | bytes 1572872 | tf_op jit(solution)/shard_map/ppermute | solution.py:384
  64.6 13.3 %collective-permute-start.14 = (f32[1,536,128]{2,1,0:T(8,128)S(1)}, f32[1,536,128]{2,1,0:T(8,128)S(1)}, u32[]{:S(2)}, u32[]{:S(2)}) collective-permute-start(f32[1,536,128]{2,1,0:T(8,128)S(1)} %fusion.1), channel_id=1, source_target_pairs={{2,4},{9,17},{10,12},{11,19},{18,20},{13,21},{26,28},{15,23},{4,2}... | collective-permute-start | bytes 823304 | tf_op jit(solution)/shard_map/ppermute | solution.py:387
  75.0 6.5 %collective-permute-start.13 = (f32[1,512,128]{2,1,0:T(8,128)S(1)}, f32[1,512,128]{2,1,0:T(8,128)S(1)}, u32[]{:S(2)}, u32[]{:S(2)}) collective-permute-start(f32[1,512,128]{2,1,0:T(8,128)S(1)} %fusion.8), channel_id=1, source_target_pairs={{0,2},{1,9},{8,10},{3,11},{16,18},{5,13},{24,26},{7,15},{2,0},{9,1... | collective-permute-start | bytes 786440 | tf_op jit(solution)/shard_map/ppermute | solution.py:387
  78.0 8.9 %collective-permute-start.17 = (f32[536,128]{1,0:T(8,128)S(1)}, f32[536,128]{1,0:T(8,128)S(1)}, u32[]{:S(2)}, u32[]{:S(2)}) collective-permute-start(f32[536,128]{1,0:T(8,128)S(1)} %fusion.3), channel_id=1, source_target_pairs={{0,32},{2,34},{4,36},{6,38},{8,40},{10,42},{12,44},{14,46},{16,48}... | collective-permute-start | bytes 823304 | tf_op jit(solution)/shard_map/ppermute | solution.py:393
  81.5 11.0 %collective-permute-start.15 = (f32[512,128]{1,0:T(8,128)S(1)}, f32[512,128]{1,0:T(8,128)S(1)}, u32[]{:S(2)}, u32[]{:S(2)}) collective-permute-start(f32[512,128]{1,0:T(8,128)S(1)} %fusion.7), channel_id=1, source_target_pairs={{0,32},{2,34},{4,36},{6,38},{8,40},{10,42},{12,44},{14,46},{16,48}... | collective-permute-start | bytes 786440 | tf_op jit(solution)/shard_map/ppermute | solution.py:393
  86.9 8.4 %collective-permute-start.18 = (f32[536,128]{1,0:T(8,128)S(1)}, f32[536,128]{1,0:T(8,128)S(1)}, u32[]{:S(2)}, u32[]{:S(2)}) collective-permute-start(f32[536,128]{1,0:T(8,128)S(1)} %add.103.var), channel_id=1, source_target_pairs={{32,64},{34,66},{36,68},{38,70},{40,72},{42,74},{44,76},{46,78},{4... | collective-permute-start | bytes 823304 | tf_op jit(solution)/shard_map/ppermute | solution.py:394
  92.5 7.7 %collective-permute-start.16 = (f32[512,128]{1,0:T(8,128)S(1)}, f32[512,128]{1,0:T(8,128)S(1)}, u32[]{:S(2)}, u32[]{:S(2)}) collective-permute-start(f32[512,128]{1,0:T(8,128)S(1)} %add.102.num), channel_id=1, source_target_pairs={{32,64},{34,66},{36,68},{38,70},{40,72},{42,74},{44,76},{46,78},{4... | collective-permute-start | bytes 786440 | tf_op jit(solution)/shard_map/ppermute | solution.py:394

commit v7 on v6

--- a/solution.py
+++ b/solution.py
@@ -16,14 +16,15 @@
 ROUTES = 2 * TILES
 CAP = 3
 META = 24
+PITCH = TS + 8
 PAD = 64
 F32 = jnp.float32
 BF16 = jnp.bfloat16
 
 EMPTY = 1 << 24
-UNROLL = 2
-MATCH_UNROLL = 8
-CHUNKS = 4
+UNROLL = 8
+MATCH_UNROLL = 16
+CHUNKS = 2
 MATCH_COST = 100_000_000_000
 WARP_COST = 10_000_000_000
 
@@ -87,21 +88,17 @@
 
 
 def match_kernel(
-    basis_ids, coefs, taps_hbm, image_hbm, variance_hbm, out, taps, line, row_mats, col_mats, image, variance, sems, taps_sem
+    basis_ids, coefs, taps_hbm, image_hbm, out, taps, line, row_mats, col_mats, image, sems, taps_sem
 ):
     size = TILES // CHUNKS
     copies = [
-        [
-            pltpu.make_async_copy(source.at[pl.ds(c * size, size)], target.at[pl.ds(c * size, size)], sems.at[i, c])
-            for i, (source, target) in enumerate(((image_hbm, image), (variance_hbm, variance)))
-        ]
+        pltpu.make_async_copy(image_hbm.at[pl.ds(c * size, size)], image.at[pl.ds(c * size, size)], sems.at[c])
         for c in range(CHUNKS)
     ]
     fetch = pltpu.make_async_copy(taps_hbm, taps, taps_sem)
     fetch.start()
-    for pair in copies:
-        for copy in pair:
-            copy.start()
+    for copy in copies:
+        copy.start()
     i = lax.broadcasted_iota(jnp.int32, (TS, TS), 0)
     k = lax.broadcasted_iota(jnp.int32, (TS, TS), 1)
     near = jnp.abs(i - k) <= HALF
@@ -124,14 +121,13 @@
             else:
                 col_mats[b] = square(*split(band))
 
+    out[TILES * PITCH :, :] = jnp.zeros((8, TS), F32)
     for c in range(CHUNKS):
-        for copy in copies[c]:
-            copy.wait()
+        copies[c].wait()
 
         @pl.loop(c * size, (c + 1) * size, step=MATCH_UNROLL)
         def _(first):
             for t in [first + u for u in range(MATCH_UNROLL)]:
-                weight = float(TS * TS) / jnp.sum(variance[t], axis=(0, 1), keepdims=True)
                 pixels = square(*split(image[t]))
                 total = None
                 for j in range(NB):
@@ -140,15 +136,17 @@
                     part = (p[:, :TS] + p[:, TS:]) * coefs[j, t]
                     p = jnp.dot(jnp.concatenate(split(part), 1), col_mats[basis], preferred_element_type=F32)
                     total = p if total is None else total + p
-                out[t] = (total[:, :TS] + total[:, TS:]) * weight
-
-
-def match(basis_ids, coefs, taps, image, variance):
+                at = pl.multiple_of(t * PITCH, 8)
+                out[pl.ds(at, 8), :] = jnp.zeros((8, TS), F32)
+                out[pl.ds(at + 8, TS), :] = total[:, :TS] + total[:, TS:]
+
+
+def match(basis_ids, coefs, taps, image):
     vmem, hbm = pl.BlockSpec(memory_space=pltpu.VMEM), pl.BlockSpec(memory_space=pltpu.HBM)
     return pl.pallas_call(
         match_kernel,
-        out_shape=jax.ShapeDtypeStruct((TILES, TS, TS), F32),
-        in_specs=[pl.BlockSpec(memory_space=pltpu.SMEM)] * 2 + [hbm] * 3,
+        out_shape=jax.ShapeDtypeStruct((TILES * PITCH + 8, TS), F32),
+        in_specs=[pl.BlockSpec(memory_space=pltpu.SMEM)] * 2 + [hbm] * 2,
         out_specs=vmem,
         scratch_shapes=[
             pltpu.VMEM((NBASIS, 2, 2 * HALF + 1), F32),
@@ -156,28 +154,24 @@
             pltpu.VMEM((NBASIS, TS, 2 * TS), BF16),
             pltpu.VMEM((NBASIS, 2 * TS, 2 * TS), BF16),
             pltpu.VMEM((TILES, TS, TS), F32),
-            pltpu.VMEM((TILES, TS, TS), F32),
-            pltpu.SemaphoreType.DMA((2, CHUNKS)),
+            pltpu.SemaphoreType.DMA((CHUNKS,)),
             pltpu.SemaphoreType.DMA,
         ],
         compiler_params=pltpu.CompilerParams(vmem_limit_bytes=40 << 20),
         cost_estimate=pl.CostEstimate(flops=MATCH_COST, bytes_accessed=6 << 20, transcendentals=0),
         name="match",
-    )(*(pltpu.with_memory_space_constraint(x, pltpu.HBM) for x in (basis_ids.T, coefs.T, taps, image, variance)))
+    )(*(pltpu.with_memory_space_constraint(x, pltpu.HBM) for x in (basis_ids.T, coefs.T, taps, image)))
 
 
 def warp_kernel(with_meta, *refs):
     if with_meta:
-        own, other, own_tiles, other_tiles = refs[:4]
-        outs, slots = refs[4:8], refs[8]
-        stage, acc, meta, weights = refs[9:]
+        own, other, own_raw, other_raw = refs[:4]
+        outs, slots, weights = refs[4:8], refs[8], refs[9]
+        acc, meta, own_tiles, other_tiles = refs[10:]
     else:
-        slots, own, other, own_tiles, other_tiles = refs[:5]
-        outs = refs[5:9]
-        stage, acc = refs[9:]
+        slots, own, other, weights, own_tiles, other_tiles = refs[:6]
+        outs, acc = refs[6:10], refs[10]
     lane = lax.broadcasted_iota(jnp.int32, (8, TS), 1)
-    stage[:, :, 0:8, :] = jnp.zeros((2 * UNROLL, 2, 8, TS), F32)
-    stage[:, :, 8 + TS :, :] = jnp.zeros((2 * UNROLL, 2, 8, TS), F32)
     for k in range(16):
         for side in (1, 2):
             acc[4 * k + side, PAD : PAD + PATCH, :] = jnp.zeros((PATCH, TS), F32)
@@ -188,32 +182,40 @@
 
         @pl.loop(0, TILES, step=8)
         def _(first):
-            for side, table, tiles in ((0, own, own_tiles), (1, other, other_tiles)):
+            for side, table, raw, tiles in ((0, own, own_raw, own_tiles), (1, other, other_raw, other_tiles)):
                 for route in range(2):
                     for t in [first + u for u in range(8)]:
                         what = table[route, t].astype(jnp.int32)
                         at = jnp.where((what >> 8) == core, table[10 + route, t].astype(jnp.int32) + 1, 127)
                         slots[side, at] = (what << 8) + (2 * t + route)
-                sums = jnp.concatenate([jnp.sum(tiles[first + u], axis=0, keepdims=True) for u in range(8)], 0)
-                sums = jnp.sum(sums, axis=1, keepdims=True)
+                sums = []
+                for t in [first + u for u in range(8)]:
+                    tile = raw[t]
+                    at = pl.multiple_of(t * PITCH, 8)
+                    tiles[pl.ds(at, 8), :] = jnp.zeros((8, TS), F32)
+                    tiles[pl.ds(at + 8, TS), :] = tile
+                    sums.append(jnp.sum(tile, axis=0, keepdims=True))
+                sums = jnp.sum(jnp.concatenate(sums, 0), axis=1, keepdims=True)
                 at = pl.multiple_of(side * TILES + first, 8)
                 weights[pl.ds(at, 8), :] = jnp.broadcast_to(float(TS * TS) / sums, (8, TS))
 
         for side, table in ((0, own), (1, other)):
             n = table[12, core].astype(jnp.int32)
             slots[side, 0] = n
-            for u in range(3 * UNROLL):
+            for u in range(UNROLL):
                 slots[side, 1 + n + u] = EMPTY
-
-    def place(entry, u, side, table, tiles):
+        for tiles in (own_tiles, other_tiles):
+            tiles[TILES * PITCH :, :] = jnp.zeros((8, TS), F32)
+
+    def place(entry, side, table, tiles):
         item, k, slot = entry & 255, (entry >> 8) & 15, (entry >> 12) & 3
         t, route = item >> 1, item & 1
         row, col = table[2 + 2 * route, t].astype(jnp.int32), table[3 + 2 * route, t].astype(jnp.int32)
         frac_row, frac_col = table[6 + 2 * route, t], table[7 + 2 * route, t]
         real = jnp.where(entry >= EMPTY, 0.0, 1.0)
-        near, far = jnp.full((8, TS), (1.0 - frac_col) * real), jnp.full((8, TS), frac_col * real)
+        weight = jnp.broadcast_to(weights[pl.ds(side * TILES + t, 1), :], (8, TS))
+        scale = weight * real
         if with_meta:
-            weight = jnp.broadcast_to(weights[pl.ds(side * TILES + t, 1), :], (8, TS))
             field = lax.broadcasted_iota(jnp.int32, (8, TS), 0)
             value = jnp.where(field == 1, row.astype(F32), weight)
             value = jnp.where(field == 2, col.astype(F32), value)
@@ -221,42 +223,29 @@
             value = jnp.where(field == 4, frac_col, value)
             value = jnp.where((field < 5) & (lane == 2 * chip + side), value * real, 0.0)
             meta[k * CAP + slot] += value
-            near, far = near * (weight * weight), far * (weight * weight)
-        turn = (col + TS) & (TS - 1)
+            scale = scale * weight
+        near, far = scale * (1.0 - frac_col), scale * frac_col
+        turn, down = (col + TS) & (TS - 1), (row + PAD) & 7
         here = jnp.where(lane >= turn, near, 0.0)
         here_next = jnp.where(lane >= turn + 1, far, 0.0)
         over, over_next = near - here, far - here_next
-        tile = tiles[t]
-        r0 = pltpu.roll(tile, turn, 1).reshape(TS // 8, 8, TS)
-        r1 = pltpu.roll(tile, (turn + 1) & (TS - 1), 1).reshape(TS // 8, 8, TS)
-        stage[u, 0, 8 : 8 + TS, :] = (r0 * here + r1 * here_next).reshape(TS, TS)
-        stage[u, 1, 8 : 8 + TS, :] = (r0 * over + r1 * over_next).reshape(TS, TS)
-        return 4 * k + ((col + TS) >> 7), row + PAD, frac_row
-
-    def add_rows(u, first, row, frac_row):
-        down = row & 7
-        base = pl.multiple_of((row >> 3) * 8, 8)
-        for side in range(2):
-            upper = stage[u, side, pl.ds(8 - down, TS + 8), :]
-            lower = stage[u, side, pl.ds(7 - down, TS + 8), :]
-            acc[first + side, pl.ds(base, TS + 8), :] += upper * (1.0 - frac_row) + lower * frac_row
+        start = t * PITCH + 8 - down
+        upper, lower = tiles[pl.ds(start, PITCH), :], tiles[pl.ds(start - 1, PITCH), :]
+        rows = upper * (1.0 - frac_row) + lower * frac_row
+        r0 = pltpu.roll(rows, turn, 1).reshape(PITCH // 8, 8, TS)
+        r1 = pltpu.roll(rows, (turn + 1) & (TS - 1), 1).reshape(PITCH // 8, 8, TS)
+        left = (r0 * here + r1 * here_next).reshape(PITCH, TS)
+        right = (r0 * over + r1 * over_next).reshape(PITCH, TS)
+        return left, right, 4 * k + ((col + TS) >> 7), pl.multiple_of(((row + PAD) >> 3) * 8, 8)
 
     for side, table, tiles in ((0, own, own_tiles), (1, other, other_tiles)):
-        start = [place(slots[side, 1 + u], u, side, table, tiles) for u in range(UNROLL)]
-
-        def body(m, placed, side=side, table=table, tiles=tiles):
-            for half in range(2):
-                group = 2 * m + half + 1
-                then = [
-                    place(slots[side, 1 + group * UNROLL + u], UNROLL * (1 - half) + u, side, table, tiles)
-                    for u in range(UNROLL)
-                ]
-                for u in range(UNROLL):
-                    add_rows(UNROLL * half + u, *placed[u])
-                placed = then
-            return placed
-
-        lax.fori_loop(0, (slots[side, 0] + 2 * UNROLL - 1) // (2 * UNROLL), body, start)
+
+        @pl.loop(0, (slots[side, 0] + UNROLL - 1) // UNROLL)
+        def _(m, side=side, table=table, tiles=tiles):
+            for u in range(UNROLL):
+                left, right, first, base = place(slots[side, 1 + m * UNROLL + u], side, table, tiles)
+                acc[first, pl.ds(base, PITCH), :] += left
+                acc[first + 1, pl.ds(base, PITCH), :] += right
 
     for k in range(16):
         a, b, c, d = k >> 3, (k >> 2) & 1, (k >> 1) & 1, k & 1
@@ -274,20 +263,16 @@
     left = jax.ShapeDtypeStruct((8, PATCH + META if with_meta else PATCH, TS), F32)
     right = jax.ShapeDtypeStruct((8, PATCH, TS), F32)
     outs, specs = [left, left, right, right], [vmem] * 4
-    scratch = [
-        pltpu.VMEM((2 * UNROLL, 2, TS + 16, TS), F32),
-        pltpu.VMEM((64, 384, TS), F32),
-    ]
+    scratch = [pltpu.VMEM((64, 384, TS), F32)]
     if with_meta:
-        outs, specs = outs + [jax.ShapeDtypeStruct((2, 128), jnp.int32)], specs + [smem]
-        scratch += [
-            pltpu.VMEM((16 * CAP, 8, TS), F32),
-            pltpu.VMEM((2 * TILES, TS), F32),
-        ]
+        outs += [jax.ShapeDtypeStruct((2, 128), jnp.int32), jax.ShapeDtypeStruct((2 * TILES, TS), F32)]
+        specs += [smem, vmem]
+        scratch += [pltpu.VMEM((16 * CAP, 8, TS), F32)] + [pltpu.VMEM((TILES * PITCH + 8, TS), F32)] * 2
+    scalars = 2 if with_meta else 3
     return pl.pallas_call(
         functools.partial(warp_kernel, with_meta),
         out_shape=outs,
-        in_specs=[smem] * (len(args) - 2) + [vmem] * 2,
+        in_specs=[smem] * scalars + [vmem] * (len(args) - scalars),
         out_specs=specs,
         scratch_shapes=scratch,
         compiler_params=pltpu.CompilerParams(vmem_limit_bytes=40 << 20),
@@ -389,9 +374,9 @@
     return left_over[-1][0], left_over
 
 
-def double(x):
-    x = x + lax.ppermute(x, ("visit", "patch"), over_visit(0))
-    return x, lax.ppermute(x, ("visit", "patch"), over_visit(1))
+def double(x, first):
+    x = x + lax.ppermute(x, ("visit", "patch"), over_visit(first))
+    return x, lax.ppermute(x, ("visit", "patch"), over_visit(1 - first))
 
 
 def shards(image, variance, intersections, boxes, shifts, basis_ids, coefs, taps):
@@ -399,14 +384,14 @@
     other_variance = lax.ppermute(variance, "patch", swap)
     table = pack(intersections, boxes, shifts)
     other_table = lax.ppermute(table, "patch", swap)
-    matched = match(basis_ids, coefs, taps, image, variance)
+    matched = match(basis_ids, coefs, taps, image)
     matched, other_table = lax.optimization_barrier((matched, other_table))
     other_matched = lax.ppermute(matched, "patch", swap)
-    *var, slots = warp(True, table, other_table, variance, other_variance)
-    num = warp(False, slots, table, other_table, matched, other_matched)
+    *var, slots, weights = warp(True, table, other_table, variance, other_variance)
+    num = warp(False, slots, table, other_table, weights, matched, other_matched)
     var, ahead = halve(*var, 0)
     num, _ = halve(*num, 1, ahead)
-    var, num = double(var), double(num)
+    var, num = double(var, 0), double(num, 1)
     coadd_var, safe = finish(cover_kernel, "cover", 2, *var)
     (coadd,) = finish(divide_kernel, "divide", 1, *num, safe)
     return coadd, coadd_var

time: 102 us -> 95.2 us (0.933)
  the two profiles are of different devices: /device:TPU:24 before, /device:TPU:0 now
where the time goes in v7:
time: 95.2 us; the launch traced here: 95.3 us
  waiting for transfers between devices  44.8 us (47%)
  starting transfers between devices  27.2 us (29%)
  Pallas kernels  21.4 us (22%)
  other arithmetic  1.09 us (1%)
    pallas_call x2, Pallas kernels, warp(): pl.pallas_call(functools.partial(warp_kernel, with_meta), out_shape=outs,...  11.1 us
    ppermute x2, waiting for transfers between devices, halve(): lax.ppermute(right_send, 'patch', over_patch(0, 1))  9.23 us
    ppermute x2, waiting for transfers between devices, halve(): got, = after(2, lax.ppermute(send, 'patch', over_patch(1, last)))  7.02 us
    pallas_call x1, Pallas kernels, match(): pl.pallas_call(match_kernel, out_shape=jax.ShapeDtypeStruct((TILES * PITC...  6.49 us
    ppermute x2, waiting for transfers between devices, halve(): lax.ppermute(left_send, 'patch', over_patch(0, 1))  6.49 us
    ppermute x2, starting transfers between devices, halve(): got, = after(2, lax.ppermute(send, 'patch', over_patch(1, last)))  5.9 us
    ppermute x2, waiting for transfers between devices, halve(): lax.ppermute(left_send, 'patch', over_patch(0, 0))  5.72 us
    ppermute x2, starting transfers between devices, halve(): lax.ppermute(left_send, 'patch', over_patch(0, 1))  5.3 us
  transfers between devices with their start and end apart: 19, of which 12 were waited for; matrix products, arithmetic and copies ran while one was open for 1% of the time, Pallas kernels for 20%

profile of v7, /device:TPU:0, one launch (start us, length us, event | category | flops | bytes accessed | tf_op | source)
XLA Modules:
  0.0 95.3 jit_solution(3756027007171582239)
XLA Ops:
  2.6 6.5 %match.1.refs_4_ = f32[4360,128]{1,0:T(8,128)S(1)} custom-call(s32[3,32]{1,0:T(4,128)} %bitcast.12, f32[3,32]{1,0:T(4,128)} %bitcast.13, f32[8,2,41]{2,1,0:T(2,128)} %taps_hbm.1, f32[32,128,128]{2,1,0:T(8,128)} %image_hbm.1), custom_call_target="tpu_custom_call" | custom-call | flops 99999997952 | bytes 6291456 | tf_op jit(solution)/shard_map/match/pallas_call | solution.py:146
  9.2 6.4 %warp_meta.1 = (f32[8,280,128]{2,1,0:T(8,128)S(1)}, f32[8,280,128]{2,1,0:T(8,128)S(1)}, f32[8,256,128]{2,1,0:T(8,128)S(1)}, f32[8,256,128]{2,1,0:T(8,128)S(1)}, ...) custom-call(f32[16,128]{1,0:T(8,128)S(1)} %copy-done, f32[16,128]{1,0:T(8,128)S(1)} %collective-permute-done.refs_1_.refs_2_, ...), custom_call_target="tpu_custom_call" | custom-call | flops 10000000000 | bytes 8388608 | tf_op jit(solution)/shard_map/warp_meta/pallas_call | solution.py:272
  15.6 2.1 %collective-permute-start.5 = (f32[8,280,128]{2,1,0:T(8,128)S(1)}, f32[8,280,128]{2,1,0:T(8,128)S(1)}, u32[]{:S(2)}, u32[]{:S(2)}) collective-permute-start(f32[8,280,128]{2,1,0:T(8,128)S(1)} %get-tuple-element.30), channel_id=1, source_target_pairs={{0,8},{1,3},{2,10},{9,11},{4,12},{17,19},{6,14},{25,27},{8,0},{3,1... | collective-permute-start | bytes 3440648 | tf_op jit(solution)/shard_map/ppermute | solution.py:356
  17.7 2.5 %collective-permute-start.6 = (f32[8,256,128]{2,1,0:T(8,128)S(1)}, f32[8,256,128]{2,1,0:T(8,128)S(1)}, u32[]{:S(2)}, u32[]{:S(2)}) collective-permute-start(f32[8,256,128]{2,1,0:T(8,128)S(1)} %get-tuple-element.32), channel_id=1, source_target_pairs={{8,16},{3,5},{10,18},{11,13},{12,20},{19,21},{14,22},{27,29},{16,8... | collective-permute-start | bytes 3145736 | tf_op jit(solution)/shard_map/ppermute | solution.py:356
  20.2 4.7 %warp.1 = (f32[8,256,128]{2,1,0:T(8,128)S(1)}, f32[8,256,128]{2,1,0:T(8,128)S(1)}, f32[8,256,128]{2,1,0:T(8,128)S(1)}, f32[8,256,128]{2,1,0:T(8,128)S(1)}) custom-call(s32[2,128]{1,0:T(2,128)S(1)} %get-tuple-element.23.refs_0_, f32[16,128]{1,0:T(8,128)S(1)} %copy-done, f32[16,128]{1,0:T(8,128)S(1)} %collective-permute-done.refs_1_.refs_2_, ...), custom_call_target="tpu_custom_call" | custom-call | flops 10000000000 | bytes 8388608 | tf_op jit(solution)/shard_map/warp/pallas_call | solution.py:272
  26.6 7.1 %collective-permute-done.6 = f32[8,256,128]{2,1,0:T(8,128)S(1)} collective-permute-done((f32[8,256,128]{2,1,0:T(8,128)S(1)}, f32[8,256,128]{2,1,0:T(8,128)S(1)}, u32[]{:S(2)}, u32[]{:S(2)}) %collective-permute-start.6) | collective-permute-done | bytes 1048608 | tf_op jit(solution)/shard_map/ppermute | solution.py:356
  34.4 2.7 %collective-permute-start.9 = (f32[4,280,128]{2,1,0:T(8,128)S(1)}, f32[4,280,128]{2,1,0:T(8,128)S(1)}, u32[]{:S(2)}, u32[]{:S(2)}) collective-permute-start(f32[4,280,128]{2,1,0:T(8,128)S(1)} %get-tuple-element.43), channel_id=1, source_target_pairs={{8,16},{3,5},{10,18},{11,13},{12,20},{19,21},{14,22},{27,29},{16,8... | collective-permute-start | bytes 1720328 | tf_op jit(solution)/shard_map/ppermute | solution.py:362
  37.1 5.7 %collective-permute-done.3 = f32[8,256,128]{2,1,0:T(8,128)S(1)} collective-permute-done((f32[8,256,128]{2,1,0:T(8,128)S(1)}, f32[8,256,128]{2,1,0:T(8,128)S(1)}, u32[]{:S(2)}, u32[]{:S(2)}) %collective-permute-start.3) | collective-permute-done | bytes 1048608 | tf_op jit(solution)/shard_map/ppermute | solution.py:356
  42.8 2.2 %collective-permute-done.4 = f32[8,256,128]{2,1,0:T(8,128)S(1)} collective-permute-done((f32[8,256,128]{2,1,0:T(8,128)S(1)}, f32[8,256,128]{2,1,0:T(8,128)S(1)}, u32[]{:S(2)}, u32[]{:S(2)}) %collective-permute-start.4) | collective-permute-done | bytes 1048608 | tf_op jit(solution)/shard_map/ppermute | solution.py:356
  45.1 2.6 %collective-permute-start.7 = (f32[4,256,128]{2,1,0:T(8,128)S(1)}, f32[4,256,128]{2,1,0:T(8,128)S(1)}, u32[]{:S(2)}, u32[]{:S(2)}) collective-permute-start(f32[4,256,128]{2,1,0:T(8,128)S(1)} %get-tuple-element.45), channel_id=1, source_target_pairs={{8,16},{3,5},{10,18},{11,13},{12,20},{19,21},{14,22},{27,29},{16,8... | collective-permute-start | bytes 1572872 | tf_op jit(solution)/shard_map/ppermute | solution.py:362
  48.5 2.6 %collective-permute-done.9 = f32[4,280,128]{2,1,0:T(8,128)S(1)} collective-permute-done((f32[4,280,128]{2,1,0:T(8,128)S(1)}, f32[4,280,128]{2,1,0:T(8,128)S(1)}, u32[]{:S(2)}, u32[]{:S(2)}) %collective-permute-start.9) | collective-permute-done | bytes 573472 | tf_op jit(solution)/shard_map/ppermute | solution.py:362
  51.2 1.6 %collective-permute-start.12 = (f32[2,536,128]{2,1,0:T(8,128)S(1)}, f32[2,536,128]{2,1,0:T(8,128)S(1)}, u32[]{:S(2)}, u32[]{:S(2)}) collective-permute-start(f32[2,536,128]{2,1,0:T(8,128)S(1)} %pad_maximum_fusion), channel_id=1, source_target_pairs={{0,2},{1,9},{8,10},{3,11},{16,18},{5,13},{24,26},{7,15},{2,0},{9,1... | collective-permute-start | bytes 1646600 | tf_op jit(solution)/shard_map/ppermute | solution.py:369
  52.8 3.9 %collective-permute-done.7 = f32[4,256,128]{2,1,0:T(8,128)S(1)} collective-permute-done((f32[4,256,128]{2,1,0:T(8,128)S(1)}, f32[4,256,128]{2,1,0:T(8,128)S(1)}, u32[]{:S(2)}, u32[]{:S(2)}) %collective-permute-start.7) | collective-permute-done | bytes 524320 | tf_op jit(solution)/shard_map/ppermute | solution.py:362
  56.7 4.6 %collective-permute-done.8 = f32[4,256,128]{2,1,0:T(8,128)S(1)} collective-permute-done((f32[4,256,128]{2,1,0:T(8,128)S(1)}, f32[4,256,128]{2,1,0:T(8,128)S(1)}, u32[]{:S(2)}, u32[]{:S(2)}) %collective-permute-start.8) | collective-permute-done | bytes 524320 | tf_op jit(solution)/shard_map/ppermute | solution.py:362
  61.4 4.3 %collective-permute-start.11 = (f32[2,512,128]{2,1,0:T(8,128)S(1)}, f32[2,512,128]{2,1,0:T(8,128)S(1)}, u32[]{:S(2)}, u32[]{:S(2)}) collective-permute-start(f32[2,512,128]{2,1,0:T(8,128)S(1)} %pad_maximum_fusion.1), channel_id=1, source_target_pairs={{2,4},{9,17},{10,12},{11,19},{18,20},{13,21},{26,28},{15,23},{4,2}... | collective-permute-start | bytes 1572872 | tf_op jit(solution)/shard_map/ppermute | solution.py:369
  65.8 7.0 %collective-permute-done.11 = f32[2,512,128]{2,1,0:T(8,128)S(1)} collective-permute-done((f32[2,512,128]{2,1,0:T(8,128)S(1)}, f32[2,512,128]{2,1,0:T(8,128)S(1)}, u32[]{:S(2)}, u32[]{:S(2)}) %collective-permute-start.11) | collective-permute-done | bytes 524320 | tf_op jit(solution)/shard_map/ppermute | solution.py:369
  74.1 1.7 %collective-permute-done.14 = f32[1,536,128]{2,1,0:T(8,128)S(1)} collective-permute-done((f32[1,536,128]{2,1,0:T(8,128)S(1)}, f32[1,536,128]{2,1,0:T(8,128)S(1)}, u32[]{:S(2)}, u32[]{:S(2)}) %collective-permute-start.14) | collective-permute-done | bytes 274464 | tf_op jit(solution)/shard_map/ppermute | solution.py:372
  75.8 1.5 %collective-permute-start.17 = (f32[536,128]{1,0:T(8,128)S(1)}, f32[536,128]{1,0:T(8,128)S(1)}, u32[]{:S(2)}, u32[]{:S(2)}) collective-permute-start(f32[536,128]{1,0:T(8,128)S(1)} %fusion.3), channel_id=1, source_target_pairs={{0,32},{2,34},{4,36},{6,38},{8,40},{10,42},{12,44},{14,46},{16,48}... | collective-permute-start | bytes 823304 | tf_op jit(solution)/shard_map/ppermute | solution.py:378
  77.4 2.0 %collective-permute-done.13 = f32[1,512,128]{2,1,0:T(8,128)S(1)} collective-permute-done((f32[1,512,128]{2,1,0:T(8,128)S(1)}, f32[1,512,128]{2,1,0:T(8,128)S(1)}, u32[]{:S(2)}, u32[]{:S(2)}) %collective-permute-start.13) | collective-permute-done | bytes 262176 | tf_op jit(solution)/shard_map/ppermute | solution.py:372
  79.4 2.9 %collective-permute-start.15 = (f32[512,128]{1,0:T(8,128)S(1)}, f32[512,128]{1,0:T(8,128)S(1)}, u32[]{:S(2)}, u32[]{:S(2)}) collective-permute-start(f32[512,128]{1,0:T(8,128)S(1)} %fusion.7), channel_id=1, source_target_pairs={{32,64},{34,66},{36,68},{38,70},{40,72},{42,74},{44,76},{46,78},{4... | collective-permute-start | bytes 786440 | tf_op jit(solution)/shard_map/ppermute | solution.py:378
  82.2 2.8 %collective-permute-done.17 = f32[536,128]{1,0:T(8,128)S(1)} collective-permute-done((f32[536,128]{1,0:T(8,128)S(1)}, f32[536,128]{1,0:T(8,128)S(1)}, u32[]{:S(2)}, u32[]{:S(2)}) %collective-permute-start.17) | collective-permute-done | bytes 274464 | tf_op jit(solution)/shard_map/ppermute | solution.py:378
  85.1 2.9 %collective-permute-start.18 = (f32[536,128]{1,0:T(8,128)S(1)}, f32[536,128]{1,0:T(8,128)S(1)}, u32[]{:S(2)}, u32[]{:S(2)}) collective-permute-start(f32[536,128]{1,0:T(8,128)S(1)} %add.103.var), channel_id=1, source_target_pairs={{32,64},{34,66},{36,68},{38,70},{40,72},{42,74},{44,76},{46,78},{4... | collective-permute-start | bytes 823304 | tf_op jit(solution)/shard_map/ppermute | solution.py:379
  88.1 4.8 %collective-permute-done.18.got = f32[536,128]{1,0:T(8,128)S(1)} collective-permute-done((f32[536,128]{1,0:T(8,128)S(1)}, f32[536,128]{1,0:T(8,128)S(1)}, u32[]{:S(2)}, u32[]{:S(2)}) %collective-permute-start.18) | collective-permute-done | bytes 274464 | tf_op jit(solution)/shard_map/ppermute | solution.py:379
  92.9 1.7 %cover.1 = (f32[256,256]{1,0:T(8,128)}, f32[256,256]{1,0:T(8,128)S(1)}) custom-call(f32[536,128]{1,0:T(8,128)S(1)} %add.103.var, f32[536,128]{1,0:T(8,128)S(1)} %collective-permute-done.18.got), custom_call_target="tpu_custom_call" | custom-call | flops 1000000000 | bytes 1048576 | tf_op jit(solution)/shard_map/cover/pallas_call | solution.py:318
  (39 shorter events, 8.0 us)
Async XLA Ops:
  2.1 7.0 %collective-permute-start = (f32[16,128]{1,0:T(8,128)}, f32[16,128]{1,0:T(8,128)S(1)}, u32[]{:S(2)}, u32[]{:S(2)}) collective-permute-start(f32[16,128]{1,0:T(8,128)} %pack.1.refs_0_.refs_1_), channel_id=1, source_target_pairs={{0,1},{1,0},{2,3},{3,2},{4,5},{5,4},{6,7},{7,6},{8,9},{9,8},{10,11... | collective-permute-start | bytes 24584 | tf_op jit(solution)/shard_map/ppermute | solution.py:386
  2.1 7.1 %collective-permute-start.1 = (f32[32,128,128]{2,1,0:T(8,128)}, f32[32,128,128]{2,1,0:T(8,128)S(1)}, u32[]{:S(2)}, u32[]{:S(2)}) collective-permute-start(f32[32,128,128]{2,1,0:T(8,128)} %refs_2_.1), channel_id=1, source_target_pairs={{0,1},{1,0},{2,3},{3,2},{4,5},{5,4},{6,7},{7,6},{8,9},{9,8},{10,11... | collective-permute-start | bytes 6291464 | tf_op jit(solution)/shard_map/ppermute | solution.py:384
  2.6 6.6 %copy-start = (f32[16,128]{1,0:T(8,128)S(1)}, f32[16,128]{1,0:T(8,128)}, u32[]{:S(2)}) copy-start(f32[16,128]{1,0:T(8,128)} %pack.1.refs_0_.refs_1_) | copy-start | bytes 24580
  2.6 6.6 %copy-start.1 = (f32[32,128,128]{2,1,0:T(8,128)S(1)}, f32[32,128,128]{2,1,0:T(8,128)}, u32[]{:S(2)}) copy-start(f32[32,128,128]{2,1,0:T(8,128)} %refs_2_.1) | copy-start | bytes 6291460
  9.1 11.1 %collective-permute-start.2 = (f32[4360,128]{1,0:T(8,128)S(1)}, f32[4360,128]{1,0:T(8,128)S(1)}, u32[]{:S(2)}, u32[]{:S(2)}) collective-permute-start(f32[4360,128]{1,0:T(8,128)S(1)} %match.1.refs_4_), channel_id=1, source_target_pairs={{0,1},{1,0},{2,3},{3,2},{4,5},{5,4},{6,7},{7,6},{8,9},{9,8},{10,11... | collective-permute-start | bytes 6696968 | tf_op jit(solution)/shard_map/ppermute | solution.py:389
  15.6 18.6 %collective-permute-start.5 = (f32[8,280,128]{2,1,0:T(8,128)S(1)}, f32[8,280,128]{2,1,0:T(8,128)S(1)}, u32[]{:S(2)}, u32[]{:S(2)}) collective-permute-start(f32[8,280,128]{2,1,0:T(8,128)S(1)} %get-tuple-element.30), channel_id=1, source_target_pairs={{0,8},{1,3},{2,10},{9,11},{4,12},{17,19},{6,14},{25,27},{8,0},{3,1... | collective-permute-start | bytes 3440648 | tf_op jit(solution)/shard_map/ppermute | solution.py:356
  17.7 16.0 %collective-permute-start.6 = (f32[8,256,128]{2,1,0:T(8,128)S(1)}, f32[8,256,128]{2,1,0:T(8,128)S(1)}, u32[]{:S(2)}, u32[]{:S(2)}) collective-permute-start(f32[8,256,128]{2,1,0:T(8,128)S(1)} %get-tuple-element.32), channel_id=1, source_target_pairs={{8,16},{3,5},{10,18},{11,13},{12,20},{19,21},{14,22},{27,29},{16,8... | collective-permute-start | bytes 3145736 | tf_op jit(solution)/shard_map/ppermute | solution.py:356
  24.9 17.8 %collective-permute-start.3 = (f32[8,256,128]{2,1,0:T(8,128)S(1)}, f32[8,256,128]{2,1,0:T(8,128)S(1)}, u32[]{:S(2)}, u32[]{:S(2)}) collective-permute-start(f32[8,256,128]{2,1,0:T(8,128)S(1)} %get-tuple-element.27), channel_id=1, source_target_pairs={{0,8},{1,3},{2,10},{9,11},{4,12},{17,19},{6,14},{25,27},{8,0},{3,1... | collective-permute-start | bytes 3145736 | tf_op jit(solution)/shard_map/ppermute | solution.py:356
  26.0 18.9 %collective-permute-start.4 = (f32[8,256,128]{2,1,0:T(8,128)S(1)}, f32[8,256,128]{2,1,0:T(8,128)S(1)}, u32[]{:S(2)}, u32[]{:S(2)}) collective-permute-start(f32[8,256,128]{2,1,0:T(8,128)S(1)} %get-tuple-element.28), channel_id=1, source_target_pairs={{8,16},{3,5},{10,18},{11,13},{12,20},{19,21},{14,22},{27,29},{16,8... | collective-permute-start | bytes 3145736 | tf_op jit(solution)/shard_map/ppermute | solution.py:356
  33.9 14.5 %collective-permute-start.10 = (f32[4,256,128]{2,1,0:T(8,128)S(1)}, f32[4,256,128]{2,1,0:T(8,128)S(1)}, u32[]{:S(2)}, u32[]{:S(2)}) collective-permute-start(f32[4,256,128]{2,1,0:T(8,128)S(1)} %get-tuple-element.47), channel_id=1, source_target_pairs={{0,8},{1,3},{2,10},{9,11},{4,12},{17,19},{6,14},{25,27},{8,0},{3,1... | collective-permute-start | bytes 1572872 | tf_op jit(solution)/shard_map/ppermute | solution.py:362
  34.4 16.7 %collective-permute-start.9 = (f32[4,280,128]{2,1,0:T(8,128)S(1)}, f32[4,280,128]{2,1,0:T(8,128)S(1)}, u32[]{:S(2)}, u32[]{:S(2)}) collective-permute-start(f32[4,280,128]{2,1,0:T(8,128)S(1)} %get-tuple-element.43), channel_id=1, source_target_pairs={{8,16},{3,5},{10,18},{11,13},{12,20},{19,21},{14,22},{27,29},{16,8... | collective-permute-start | bytes 1720328 | tf_op jit(solution)/shard_map/ppermute | solution.py:362
  45.1 11.6 %collective-permute-start.7 = (f32[4,256,128]{2,1,0:T(8,128)S(1)}, f32[4,256,128]{2,1,0:T(8,128)S(1)}, u32[]{:S(2)}, u32[]{:S(2)}) collective-permute-start(f32[4,256,128]{2,1,0:T(8,128)S(1)} %get-tuple-element.45), channel_id=1, source_target_pairs={{8,16},{3,5},{10,18},{11,13},{12,20},{19,21},{14,22},{27,29},{16,8... | collective-permute-start | bytes 1572872 | tf_op jit(solution)/shard_map/ppermute | solution.py:362
  47.8 13.4 %collective-permute-start.8 = (f32[4,256,128]{2,1,0:T(8,128)S(1)}, f32[4,256,128]{2,1,0:T(8,128)S(1)}, u32[]{:S(2)}, u32[]{:S(2)}) collective-permute-start(f32[4,256,128]{2,1,0:T(8,128)S(1)} %get-tuple-element.48), channel_id=1, source_target_pairs={{0,8},{1,3},{2,10},{9,11},{4,12},{17,19},{6,14},{25,27},{8,0},{3,1... | collective-permute-start | bytes 1572872 | tf_op jit(solution)/shard_map/ppermute | solution.py:362
  51.2 14.5 %collective-permute-start.12 = (f32[2,536,128]{2,1,0:T(8,128)S(1)}, f32[2,536,128]{2,1,0:T(8,128)S(1)}, u32[]{:S(2)}, u32[]{:S(2)}) collective-permute-start(f32[2,536,128]{2,1,0:T(8,128)S(1)} %pad_maximum_fusion), channel_id=1, source_target_pairs={{0,2},{1,9},{8,10},{3,11},{16,18},{5,13},{24,26},{7,15},{2,0},{9,1... | collective-permute-start | bytes 1646600 | tf_op jit(solution)/shard_map/ppermute | solution.py:369
  61.4 11.4 %collective-permute-start.11 = (f32[2,512,128]{2,1,0:T(8,128)S(1)}, f32[2,512,128]{2,1,0:T(8,128)S(1)}, u32[]{:S(2)}, u32[]{:S(2)}) collective-permute-start(f32[2,512,128]{2,1,0:T(8,128)S(1)} %pad_maximum_fusion.1), channel_id=1, source_target_pairs={{2,4},{9,17},{10,12},{11,19},{18,20},{13,21},{26,28},{15,23},{4,2}... | collective-permute-start | bytes 1572872 | tf_op jit(solution)/shard_map/ppermute | solution.py:369
  65.7 10.1 %collective-permute-start.14 = (f32[1,536,128]{2,1,0:T(8,128)S(1)}, f32[1,536,128]{2,1,0:T(8,128)S(1)}, u32[]{:S(2)}, u32[]{:S(2)}) collective-permute-start(f32[1,536,128]{2,1,0:T(8,128)S(1)} %fusion.1), channel_id=1, source_target_pairs={{2,4},{9,17},{10,12},{11,19},{18,20},{13,21},{26,28},{15,23},{4,2}... | collective-permute-start | bytes 823304 | tf_op jit(solution)/shard_map/ppermute | solution.py:372
  72.9 6.5 %collective-permute-start.13 = (f32[1,512,128]{2,1,0:T(8,128)S(1)}, f32[1,512,128]{2,1,0:T(8,128)S(1)}, u32[]{:S(2)}, u32[]{:S(2)}) collective-permute-start(f32[1,512,128]{2,1,0:T(8,128)S(1)} %fusion.8), channel_id=1, source_target_pairs={{0,2},{1,9},{8,10},{3,11},{16,18},{5,13},{24,26},{7,15},{2,0},{9,1... | collective-permute-start | bytes 786440 | tf_op jit(solution)/shard_map/ppermute | solution.py:372
  75.8 9.2 %collective-permute-start.17 = (f32[536,128]{1,0:T(8,128)S(1)}, f32[536,128]{1,0:T(8,128)S(1)}, u32[]{:S(2)}, u32[]{:S(2)}) collective-permute-start(f32[536,128]{1,0:T(8,128)S(1)} %fusion.3), channel_id=1, source_target_pairs={{0,32},{2,34},{4,36},{6,38},{8,40},{10,42},{12,44},{14,46},{16,48}... | collective-permute-start | bytes 823304 | tf_op jit(solution)/shard_map/ppermute | solution.py:378
  79.4 8.6 %collective-permute-start.15 = (f32[512,128]{1,0:T(8,128)S(1)}, f32[512,128]{1,0:T(8,128)S(1)}, u32[]{:S(2)}, u32[]{:S(2)}) collective-permute-start(f32[512,128]{1,0:T(8,128)S(1)} %fusion.7), channel_id=1, source_target_pairs={{32,64},{34,66},{36,68},{38,70},{40,72},{42,74},{44,76},{46,78},{4... | collective-permute-start | bytes 786440 | tf_op jit(solution)/shard_map/ppermute | solution.py:378
  85.1 7.8 %collective-permute-start.18 = (f32[536,128]{1,0:T(8,128)S(1)}, f32[536,128]{1,0:T(8,128)S(1)}, u32[]{:S(2)}, u32[]{:S(2)}) collective-permute-start(f32[536,128]{1,0:T(8,128)S(1)} %add.103.var), channel_id=1, source_target_pairs={{32,64},{34,66},{36,68},{38,70},{40,72},{42,74},{44,76},{46,78},{4... | collective-permute-start | bytes 823304 | tf_op jit(solution)/shard_map/ppermute | solution.py:379
  88.0 6.6 %collective-permute-start.16 = (f32[512,128]{1,0:T(8,128)S(1)}, f32[512,128]{1,0:T(8,128)S(1)}, u32[]{:S(2)}, u32[]{:S(2)}) collective-permute-start(f32[512,128]{1,0:T(8,128)S(1)} %add.102.num), channel_id=1, source_target_pairs={{0,32},{2,34},{4,36},{6,38},{8,40},{10,42},{12,44},{14,46},{16,48}... | collective-permute-start | bytes 786440 | tf_op jit(solution)/shard_map/ppermute | solution.py:379

commit v8 on v7

--- a/solution.py
+++ b/solution.py
@@ -88,23 +88,26 @@
 
 
 def match_kernel(
-    basis_ids, coefs, taps_hbm, image_hbm, out, taps, line, row_mats, col_mats, image, sems, taps_sem
+    ids_hbm, coefs_hbm, taps_hbm, image_hbm, out, basis_ids, coefs, taps, line, row_mats, col_mats, image, sems, small_sems
 ):
     size = TILES // CHUNKS
     copies = [
         pltpu.make_async_copy(image_hbm.at[pl.ds(c * size, size)], image.at[pl.ds(c * size, size)], sems.at[c])
         for c in range(CHUNKS)
     ]
-    fetch = pltpu.make_async_copy(taps_hbm, taps, taps_sem)
-    fetch.start()
-    for copy in copies:
+    small = [
+        pltpu.make_async_copy(source, target, small_sems.at[i])
+        for i, (source, target) in enumerate(((taps_hbm, taps), (ids_hbm, basis_ids), (coefs_hbm, coefs)))
+    ]
+    for copy in small + copies:
         copy.start()
     i = lax.broadcasted_iota(jnp.int32, (TS, TS), 0)
     k = lax.broadcasted_iota(jnp.int32, (TS, TS), 1)
     near = jnp.abs(i - k) <= HALF
     none = jnp.zeros((TS, TS), BF16)
     line[...] = jnp.zeros_like(line)
-    fetch.wait()
+    for copy in small:
+        copy.wait()
     for b in range(NBASIS):
         line[2 * b : 2 * b + 2, 0 : 2 * HALF + 1] = taps[b]
     line[...] = pltpu.roll(line[...], TS - HALF, 1)
@@ -129,13 +132,13 @@
         def _(first):
             for t in [first + u for u in range(MATCH_UNROLL)]:
                 pixels = square(*split(image[t]))
-                total = None
-                for j in range(NB):
-                    basis = basis_ids[j, t]
-                    p = jnp.dot(row_mats[basis], pixels, preferred_element_type=F32)
-                    part = (p[:, :TS] + p[:, TS:]) * coefs[j, t]
-                    p = jnp.dot(jnp.concatenate(split(part), 1), col_mats[basis], preferred_element_type=F32)
-                    total = p if total is None else total + p
+                bases = [basis_ids[j, t] for j in range(NB)]
+                bands = jnp.concatenate([row_mats[basis] for basis in bases], 0)
+                p = jnp.dot(bands, pixels, preferred_element_type=F32)
+                p = p[:, :TS] + p[:, TS:]
+                parts = [jnp.concatenate(split(p[TS * j : TS * (j + 1)] * coefs[j, t]), 1) for j in range(NB)]
+                bands = jnp.concatenate([col_mats[basis] for basis in bases], 0)
+                total = jnp.dot(jnp.concatenate(parts, 1), bands, preferred_element_type=F32)
                 at = pl.multiple_of(t * PITCH, 8)
                 out[pl.ds(at, 8), :] = jnp.zeros((8, TS), F32)
                 out[pl.ds(at + 8, TS), :] = total[:, :TS] + total[:, TS:]
@@ -146,16 +149,18 @@
     return pl.pallas_call(
         match_kernel,
         out_shape=jax.ShapeDtypeStruct((TILES * PITCH + 8, TS), F32),
-        in_specs=[pl.BlockSpec(memory_space=pltpu.SMEM)] * 2 + [hbm] * 2,
+        in_specs=[hbm] * 4,
         out_specs=vmem,
         scratch_shapes=[
+            pltpu.SMEM((NB, TILES), jnp.int32),
+            pltpu.SMEM((NB, TILES), F32),
             pltpu.VMEM((NBASIS, 2, 2 * HALF + 1), F32),
             pltpu.VMEM((2 * NBASIS, TS), F32),
             pltpu.VMEM((NBASIS, TS, 2 * TS), BF16),
             pltpu.VMEM((NBASIS, 2 * TS, 2 * TS), BF16),
             pltpu.VMEM((TILES, TS, TS), F32),
             pltpu.SemaphoreType.DMA((CHUNKS,)),
-            pltpu.SemaphoreType.DMA,
+            pltpu.SemaphoreType.DMA((3,)),
         ],
         compiler_params=pltpu.CompilerParams(vmem_limit_bytes=40 << 20),
         cost_estimate=pl.CostEstimate(flops=MATCH_COST, bytes_accessed=6 << 20, transcendentals=0),
@@ -289,15 +294,18 @@
         lower = jnp.where((u >= 0.0) & (u <= TS - 1.0), 1.0 - shift, 0.0)
         return lower + jnp.where((u >= 1.0) & (u <= float(TS)), shift, 0.0)
 
-    den = jnp.zeros((PATCH, PATCH), F32)
+    downs, acrosses = [], []
     for slot in range(CAP):
         at = PATCH + 8 * slot
         fields = var[at : at + 8, :] + got[at : at + 8, :]
         weight, row, col, frac_row, frac_col = (fields[f : f + 1, :] for f in range(5))
-        down, across = cover(row, frac_row) * weight, cover(col, frac_col)
-        den += lax.dot_general(
-            down, across, (((1,), (1,)), ((), ())), precision=lax.Precision.HIGHEST, preferred_element_type=F32
-        )
+        down, down_low = split(cover(row, frac_row) * weight)
+        across, across_low = split(cover(col, frac_col))
+        downs += [down, down_low, down]
+        acrosses += [across, across, across_low]
+    den = lax.dot_general(
+        jnp.concatenate(downs, 1), jnp.concatenate(acrosses, 1), (((1,), (1,)), ((), ())), preferred_element_type=F32
+    )
     safe = jnp.maximum(den, 1.0)
     safe_ref[...] = safe
     for half in range(2):

time: 95.2 us -> 94.7 us (level)
  Pallas kernels: 21.4 us -> 19.9 us
    pallas_call x1, Pallas kernels: 6.49 us -> 5.34 us  [match(): pl.pallas_call(match_kernel, out_shape=jax.ShapeDtypeStruct((TILES * PITC...]
  transfers between devices with their start and end apart: 19 -> 19, of which waited for: 12 -> 14; matrix products, arithmetic and copies ran while one was open for 1% -> 1% of each run, Pallas kernels for 20% -> 19%
where the time goes in v8:
time: 94.7 us; the launch traced here: 94.3 us
  waiting for transfers between devices  45.5 us (48%)
  starting transfers between devices  27.1 us (29%)
  Pallas kernels  19.9 us (21%)
  other arithmetic  1.09 us (1%)
    pallas_call x2, Pallas kernels, warp(): pl.pallas_call(functools.partial(warp_kernel, with_meta), out_shape=outs,...  11.1 us
    ppermute x2, waiting for transfers between devices, halve(): lax.ppermute(right_send, 'patch', over_patch(0, 1))  9.19 us
    ppermute x2, waiting for transfers between devices, halve(): got, = after(2, lax.ppermute(send, 'patch', over_patch(1, last)))  7.02 us
    ppermute x2, starting transfers between devices, halve(): got, = after(2, lax.ppermute(send, 'patch', over_patch(1, last)))  6.3 us
    ppermute x2, waiting for transfers between devices, halve(): lax.ppermute(left_send, 'patch', over_patch(0, 1))  6.08 us
    ppermute x2, waiting for transfers between devices, halve(): lax.ppermute(left_send, 'patch', over_patch(0, 0))  5.71 us
    pallas_call x1, Pallas kernels, match(): pl.pallas_call(match_kernel, out_shape=jax.ShapeDtypeStruct((TILES * PITC...  5.34 us
    ppermute x2, starting transfers between devices, halve(): lax.ppermute(left_send, 'patch', over_patch(0, 1))  5.3 us
  transfers between devices with their start and end apart: 19, of which 14 were waited for; matrix products, arithmetic and copies ran while one was open for 1% of the time, Pallas kernels for 19%

profile of v8, /device:TPU:0, one launch (start us, length us, event | category | flops | bytes accessed | tf_op | source)
XLA Modules:
  0.0 94.3 jit_solution(13976595979654617191)
XLA Ops:
  0.6 1.4 %pack.1.refs_0_.refs_1_ = f32[16,128]{1,0:T(8,128)} custom-call(s32[2,32]{1,0:T(2,128)} %bitcast.11, s32[2,2,32]{2,1,0:T(2,128)} %bitcast.9, f32[2,2,32]{2,1,0:T(2,128)} %bitcast.10), custom_call_target="tpu_custom_call" | custom-call | tf_op jit(solution)/shard_map/pack/pallas_call | solution.py:81
  2.6 5.3 %match.1.refs_4_ = f32[4360,128]{1,0:T(8,128)S(1)} custom-call(s32[3,32]{1,0:T(4,128)} %bitcast.12, f32[3,32]{1,0:T(4,128)} %bitcast.13, f32[8,2,41]{2,1,0:T(2,128)} %taps_hbm.1, f32[32,128,128]{2,1,0:T(8,128)} %image_hbm.1), custom_call_target="tpu_custom_call" | custom-call | flops 99999997952 | bytes 6291456 | tf_op jit(solution)/shard_map/match/pallas_call | solution.py:149
  8.1 6.4 %warp_meta.1 = (f32[8,280,128]{2,1,0:T(8,128)S(1)}, f32[8,280,128]{2,1,0:T(8,128)S(1)}, f32[8,256,128]{2,1,0:T(8,128)S(1)}, f32[8,256,128]{2,1,0:T(8,128)S(1)}, ...) custom-call(f32[16,128]{1,0:T(8,128)S(1)} %copy-done, f32[16,128]{1,0:T(8,128)S(1)} %collective-permute-done.refs_1_.refs_2_, ...), custom_call_target="tpu_custom_call" | custom-call | flops 10000000000 | bytes 8388608 | tf_op jit(solution)/shard_map/warp_meta/pallas_call | solution.py:277
  14.5 2.1 %collective-permute-start.5 = (f32[8,280,128]{2,1,0:T(8,128)S(1)}, f32[8,280,128]{2,1,0:T(8,128)S(1)}, u32[]{:S(2)}, u32[]{:S(2)}) collective-permute-start(f32[8,280,128]{2,1,0:T(8,128)S(1)} %get-tuple-element.30), channel_id=1, source_target_pairs={{0,8},{1,3},{2,10},{9,11},{4,12},{17,19},{6,14},{25,27},{8,0},{3,1... | collective-permute-start | bytes 3440648 | tf_op jit(solution)/shard_map/ppermute | solution.py:364
  16.5 2.5 %collective-permute-start.6 = (f32[8,256,128]{2,1,0:T(8,128)S(1)}, f32[8,256,128]{2,1,0:T(8,128)S(1)}, u32[]{:S(2)}, u32[]{:S(2)}) collective-permute-start(f32[8,256,128]{2,1,0:T(8,128)S(1)} %get-tuple-element.32), channel_id=1, source_target_pairs={{8,16},{3,5},{10,18},{11,13},{12,20},{19,21},{14,22},{27,29},{16,8... | collective-permute-start | bytes 3145736 | tf_op jit(solution)/shard_map/ppermute | solution.py:364
  19.1 4.7 %warp.1 = (f32[8,256,128]{2,1,0:T(8,128)S(1)}, f32[8,256,128]{2,1,0:T(8,128)S(1)}, f32[8,256,128]{2,1,0:T(8,128)S(1)}, f32[8,256,128]{2,1,0:T(8,128)S(1)}) custom-call(s32[2,128]{1,0:T(2,128)S(1)} %get-tuple-element.23.refs_0_, f32[16,128]{1,0:T(8,128)S(1)} %copy-done, f32[16,128]{1,0:T(8,128)S(1)} %collective-permute-done.refs_1_.refs_2_, ...), custom_call_target="tpu_custom_call" | custom-call | flops 10000000000 | bytes 8388608 | tf_op jit(solution)/shard_map/warp/pallas_call | solution.py:277
  25.5 7.0 %collective-permute-done.6 = f32[8,256,128]{2,1,0:T(8,128)S(1)} collective-permute-done((f32[8,256,128]{2,1,0:T(8,128)S(1)}, f32[8,256,128]{2,1,0:T(8,128)S(1)}, u32[]{:S(2)}, u32[]{:S(2)}) %collective-permute-start.6) | collective-permute-done | bytes 1048608 | tf_op jit(solution)/shard_map/ppermute | solution.py:364
  33.2 2.7 %collective-permute-start.9 = (f32[4,280,128]{2,1,0:T(8,128)S(1)}, f32[4,280,128]{2,1,0:T(8,128)S(1)}, u32[]{:S(2)}, u32[]{:S(2)}) collective-permute-start(f32[4,280,128]{2,1,0:T(8,128)S(1)} %get-tuple-element.43), channel_id=1, source_target_pairs={{8,16},{3,5},{10,18},{11,13},{12,20},{19,21},{14,22},{27,29},{16,8... | collective-permute-start | bytes 1720328 | tf_op jit(solution)/shard_map/ppermute | solution.py:370
  35.9 5.7 %collective-permute-done.3 = f32[8,256,128]{2,1,0:T(8,128)S(1)} collective-permute-done((f32[8,256,128]{2,1,0:T(8,128)S(1)}, f32[8,256,128]{2,1,0:T(8,128)S(1)}, u32[]{:S(2)}, u32[]{:S(2)}) %collective-permute-start.3) | collective-permute-done | bytes 1048608 | tf_op jit(solution)/shard_map/ppermute | solution.py:364
  41.6 2.2 %collective-permute-done.4 = f32[8,256,128]{2,1,0:T(8,128)S(1)} collective-permute-done((f32[8,256,128]{2,1,0:T(8,128)S(1)}, f32[8,256,128]{2,1,0:T(8,128)S(1)}, u32[]{:S(2)}, u32[]{:S(2)}) %collective-permute-start.4) | collective-permute-done | bytes 1048608 | tf_op jit(solution)/shard_map/ppermute | solution.py:364
  43.9 2.6 %collective-permute-start.7 = (f32[4,256,128]{2,1,0:T(8,128)S(1)}, f32[4,256,128]{2,1,0:T(8,128)S(1)}, u32[]{:S(2)}, u32[]{:S(2)}) collective-permute-start(f32[4,256,128]{2,1,0:T(8,128)S(1)} %get-tuple-element.45), channel_id=1, source_target_pairs={{8,16},{3,5},{10,18},{11,13},{12,20},{19,21},{14,22},{27,29},{16,8... | collective-permute-start | bytes 1572872 | tf_op jit(solution)/shard_map/ppermute | solution.py:370
  47.3 2.6 %collective-permute-done.9 = f32[4,280,128]{2,1,0:T(8,128)S(1)} collective-permute-done((f32[4,280,128]{2,1,0:T(8,128)S(1)}, f32[4,280,128]{2,1,0:T(8,128)S(1)}, u32[]{:S(2)}, u32[]{:S(2)}) %collective-permute-start.9) | collective-permute-done | bytes 573472 | tf_op jit(solution)/shard_map/ppermute | solution.py:370
  50.0 2.1 %collective-permute-start.12 = (f32[2,536,128]{2,1,0:T(8,128)S(1)}, f32[2,536,128]{2,1,0:T(8,128)S(1)}, u32[]{:S(2)}, u32[]{:S(2)}) collective-permute-start(f32[2,536,128]{2,1,0:T(8,128)S(1)} %pad_maximum_fusion), channel_id=1, source_target_pairs={{0,2},{1,9},{8,10},{3,11},{16,18},{5,13},{24,26},{7,15},{2,0},{9,1... | collective-permute-start | bytes 1646600 | tf_op jit(solution)/shard_map/ppermute | solution.py:377
  52.1 3.5 %collective-permute-done.7 = f32[4,256,128]{2,1,0:T(8,128)S(1)} collective-permute-done((f32[4,256,128]{2,1,0:T(8,128)S(1)}, f32[4,256,128]{2,1,0:T(8,128)S(1)}, u32[]{:S(2)}, u32[]{:S(2)}) %collective-permute-start.7) | collective-permute-done | bytes 524320 | tf_op jit(solution)/shard_map/ppermute | solution.py:370
  55.5 4.6 %collective-permute-done.8 = f32[4,256,128]{2,1,0:T(8,128)S(1)} collective-permute-done((f32[4,256,128]{2,1,0:T(8,128)S(1)}, f32[4,256,128]{2,1,0:T(8,128)S(1)}, u32[]{:S(2)}, u32[]{:S(2)}) %collective-permute-start.8) | collective-permute-done | bytes 524320 | tf_op jit(solution)/shard_map/ppermute | solution.py:370
  60.3 4.2 %collective-permute-start.11 = (f32[2,512,128]{2,1,0:T(8,128)S(1)}, f32[2,512,128]{2,1,0:T(8,128)S(1)}, u32[]{:S(2)}, u32[]{:S(2)}) collective-permute-start(f32[2,512,128]{2,1,0:T(8,128)S(1)} %pad_maximum_fusion.1), channel_id=1, source_target_pairs={{2,4},{9,17},{10,12},{11,19},{18,20},{13,21},{26,28},{15,23},{4,2}... | collective-permute-start | bytes 1572872 | tf_op jit(solution)/shard_map/ppermute | solution.py:377
  64.7 7.0 %collective-permute-done.11 = f32[2,512,128]{2,1,0:T(8,128)S(1)} collective-permute-done((f32[2,512,128]{2,1,0:T(8,128)S(1)}, f32[2,512,128]{2,1,0:T(8,128)S(1)}, u32[]{:S(2)}, u32[]{:S(2)}) %collective-permute-start.11) | collective-permute-done | bytes 524320 | tf_op jit(solution)/shard_map/ppermute | solution.py:377
  72.6 2.0 %collective-permute-done.14 = f32[1,536,128]{2,1,0:T(8,128)S(1)} collective-permute-done((f32[1,536,128]{2,1,0:T(8,128)S(1)}, f32[1,536,128]{2,1,0:T(8,128)S(1)}, u32[]{:S(2)}, u32[]{:S(2)}) %collective-permute-start.14) | collective-permute-done | bytes 274464 | tf_op jit(solution)/shard_map/ppermute | solution.py:380
  74.7 1.6 %collective-permute-start.17 = (f32[536,128]{1,0:T(8,128)S(1)}, f32[536,128]{1,0:T(8,128)S(1)}, u32[]{:S(2)}, u32[]{:S(2)}) collective-permute-start(f32[536,128]{1,0:T(8,128)S(1)} %fusion.3), channel_id=1, source_target_pairs={{0,32},{2,34},{4,36},{6,38},{8,40},{10,42},{12,44},{14,46},{16,48}... | collective-permute-start | bytes 823304 | tf_op jit(solution)/shard_map/ppermute | solution.py:386
  76.2 1.9 %collective-permute-done.13 = f32[1,512,128]{2,1,0:T(8,128)S(1)} collective-permute-done((f32[1,512,128]{2,1,0:T(8,128)S(1)}, f32[1,512,128]{2,1,0:T(8,128)S(1)}, u32[]{:S(2)}, u32[]{:S(2)}) %collective-permute-start.13) | collective-permute-done | bytes 262176 | tf_op jit(solution)/shard_map/ppermute | solution.py:380
  78.2 2.8 %collective-permute-start.15 = (f32[512,128]{1,0:T(8,128)S(1)}, f32[512,128]{1,0:T(8,128)S(1)}, u32[]{:S(2)}, u32[]{:S(2)}) collective-permute-start(f32[512,128]{1,0:T(8,128)S(1)} %fusion.7), channel_id=1, source_target_pairs={{32,64},{34,66},{36,68},{38,70},{40,72},{42,74},{44,76},{46,78},{4... | collective-permute-start | bytes 786440 | tf_op jit(solution)/shard_map/ppermute | solution.py:386
  81.0 3.0 %collective-permute-done.17 = f32[536,128]{1,0:T(8,128)S(1)} collective-permute-done((f32[536,128]{1,0:T(8,128)S(1)}, f32[536,128]{1,0:T(8,128)S(1)}, u32[]{:S(2)}, u32[]{:S(2)}) %collective-permute-start.17) | collective-permute-done | bytes 274464 | tf_op jit(solution)/shard_map/ppermute | solution.py:386
  84.0 2.6 %collective-permute-start.18 = (f32[536,128]{1,0:T(8,128)S(1)}, f32[536,128]{1,0:T(8,128)S(1)}, u32[]{:S(2)}, u32[]{:S(2)}) collective-permute-start(f32[536,128]{1,0:T(8,128)S(1)} %add.103.var), channel_id=1, source_target_pairs={{32,64},{34,66},{36,68},{38,70},{40,72},{42,74},{44,76},{46,78},{4... | collective-permute-start | bytes 823304 | tf_op jit(solution)/shard_map/ppermute | solution.py:387
  87.3 4.6 %collective-permute-done.18.got = f32[536,128]{1,0:T(8,128)S(1)} collective-permute-done((f32[536,128]{1,0:T(8,128)S(1)}, f32[536,128]{1,0:T(8,128)S(1)}, u32[]{:S(2)}, u32[]{:S(2)}) %collective-permute-start.18) | collective-permute-done | bytes 274464 | tf_op jit(solution)/shard_map/ppermute | solution.py:387
  (39 shorter events, 8.4 us)
Async XLA Ops:
  2.1 5.9 %collective-permute-start = (f32[16,128]{1,0:T(8,128)}, f32[16,128]{1,0:T(8,128)S(1)}, u32[]{:S(2)}, u32[]{:S(2)}) collective-permute-start(f32[16,128]{1,0:T(8,128)} %pack.1.refs_0_.refs_1_), channel_id=1, source_target_pairs={{0,1},{1,0},{2,3},{3,2},{4,5},{5,4},{6,7},{7,6},{8,9},{9,8},{10,11... | collective-permute-start | bytes 24584 | tf_op jit(solution)/shard_map/ppermute | solution.py:394
  2.1 6.0 %collective-permute-start.1 = (f32[32,128,128]{2,1,0:T(8,128)}, f32[32,128,128]{2,1,0:T(8,128)S(1)}, u32[]{:S(2)}, u32[]{:S(2)}) collective-permute-start(f32[32,128,128]{2,1,0:T(8,128)} %refs_2_.1), channel_id=1, source_target_pairs={{0,1},{1,0},{2,3},{3,2},{4,5},{5,4},{6,7},{7,6},{8,9},{9,8},{10,11... | collective-permute-start | bytes 6291464 | tf_op jit(solution)/shard_map/ppermute | solution.py:392
  2.6 5.5 %copy-start = (f32[16,128]{1,0:T(8,128)S(1)}, f32[16,128]{1,0:T(8,128)}, u32[]{:S(2)}) copy-start(f32[16,128]{1,0:T(8,128)} %pack.1.refs_0_.refs_1_) | copy-start | bytes 24580
  2.6 5.5 %copy-start.1 = (f32[32,128,128]{2,1,0:T(8,128)S(1)}, f32[32,128,128]{2,1,0:T(8,128)}, u32[]{:S(2)}) copy-start(f32[32,128,128]{2,1,0:T(8,128)} %refs_2_.1) | copy-start | bytes 6291460
  7.9 11.1 %collective-permute-start.2 = (f32[4360,128]{1,0:T(8,128)S(1)}, f32[4360,128]{1,0:T(8,128)S(1)}, u32[]{:S(2)}, u32[]{:S(2)}) collective-permute-start(f32[4360,128]{1,0:T(8,128)S(1)} %match.1.refs_4_), channel_id=1, source_target_pairs={{0,1},{1,0},{2,3},{3,2},{4,5},{5,4},{6,7},{7,6},{8,9},{9,8},{10,11... | collective-permute-start | bytes 6696968 | tf_op jit(solution)/shard_map/ppermute | solution.py:397
  14.5 18.6 %collective-permute-start.5 = (f32[8,280,128]{2,1,0:T(8,128)S(1)}, f32[8,280,128]{2,1,0:T(8,128)S(1)}, u32[]{:S(2)}, u32[]{:S(2)}) collective-permute-start(f32[8,280,128]{2,1,0:T(8,128)S(1)} %get-tuple-element.30), channel_id=1, source_target_pairs={{0,8},{1,3},{2,10},{9,11},{4,12},{17,19},{6,14},{25,27},{8,0},{3,1... | collective-permute-start | bytes 3440648 | tf_op jit(solution)/shard_map/ppermute | solution.py:364
  16.5 16.0 %collective-permute-start.6 = (f32[8,256,128]{2,1,0:T(8,128)S(1)}, f32[8,256,128]{2,1,0:T(8,128)S(1)}, u32[]{:S(2)}, u32[]{:S(2)}) collective-permute-start(f32[8,256,128]{2,1,0:T(8,128)S(1)} %get-tuple-element.32), channel_id=1, source_target_pairs={{8,16},{3,5},{10,18},{11,13},{12,20},{19,21},{14,22},{27,29},{16,8... | collective-permute-start | bytes 3145736 | tf_op jit(solution)/shard_map/ppermute | solution.py:364
  23.8 17.8 %collective-permute-start.3 = (f32[8,256,128]{2,1,0:T(8,128)S(1)}, f32[8,256,128]{2,1,0:T(8,128)S(1)}, u32[]{:S(2)}, u32[]{:S(2)}) collective-permute-start(f32[8,256,128]{2,1,0:T(8,128)S(1)} %get-tuple-element.27), channel_id=1, source_target_pairs={{0,8},{1,3},{2,10},{9,11},{4,12},{17,19},{6,14},{25,27},{8,0},{3,1... | collective-permute-start | bytes 3145736 | tf_op jit(solution)/shard_map/ppermute | solution.py:364
  24.9 18.9 %collective-permute-start.4 = (f32[8,256,128]{2,1,0:T(8,128)S(1)}, f32[8,256,128]{2,1,0:T(8,128)S(1)}, u32[]{:S(2)}, u32[]{:S(2)}) collective-permute-start(f32[8,256,128]{2,1,0:T(8,128)S(1)} %get-tuple-element.28), channel_id=1, source_target_pairs={{8,16},{3,5},{10,18},{11,13},{12,20},{19,21},{14,22},{27,29},{16,8... | collective-permute-start | bytes 3145736 | tf_op jit(solution)/shard_map/ppermute | solution.py:364
  32.7 14.5 %collective-permute-start.10 = (f32[4,256,128]{2,1,0:T(8,128)S(1)}, f32[4,256,128]{2,1,0:T(8,128)S(1)}, u32[]{:S(2)}, u32[]{:S(2)}) collective-permute-start(f32[4,256,128]{2,1,0:T(8,128)S(1)} %get-tuple-element.47), channel_id=1, source_target_pairs={{0,8},{1,3},{2,10},{9,11},{4,12},{17,19},{6,14},{25,27},{8,0},{3,1... | collective-permute-start | bytes 1572872 | tf_op jit(solution)/shard_map/ppermute | solution.py:370
  33.2 16.7 %collective-permute-start.9 = (f32[4,280,128]{2,1,0:T(8,128)S(1)}, f32[4,280,128]{2,1,0:T(8,128)S(1)}, u32[]{:S(2)}, u32[]{:S(2)}) collective-permute-start(f32[4,280,128]{2,1,0:T(8,128)S(1)} %get-tuple-element.43), channel_id=1, source_target_pairs={{8,16},{3,5},{10,18},{11,13},{12,20},{19,21},{14,22},{27,29},{16,8... | collective-permute-start | bytes 1720328 | tf_op jit(solution)/shard_map/ppermute | solution.py:370
  43.9 11.6 %collective-permute-start.7 = (f32[4,256,128]{2,1,0:T(8,128)S(1)}, f32[4,256,128]{2,1,0:T(8,128)S(1)}, u32[]{:S(2)}, u32[]{:S(2)}) collective-permute-start(f32[4,256,128]{2,1,0:T(8,128)S(1)} %get-tuple-element.45), channel_id=1, source_target_pairs={{8,16},{3,5},{10,18},{11,13},{12,20},{19,21},{14,22},{27,29},{16,8... | collective-permute-start | bytes 1572872 | tf_op jit(solution)/shard_map/ppermute | solution.py:370
  46.7 13.4 %collective-permute-start.8 = (f32[4,256,128]{2,1,0:T(8,128)S(1)}, f32[4,256,128]{2,1,0:T(8,128)S(1)}, u32[]{:S(2)}, u32[]{:S(2)}) collective-permute-start(f32[4,256,128]{2,1,0:T(8,128)S(1)} %get-tuple-element.48), channel_id=1, source_target_pairs={{0,8},{1,3},{2,10},{9,11},{4,12},{17,19},{6,14},{25,27},{8,0},{3,1... | collective-permute-start | bytes 1572872 | tf_op jit(solution)/shard_map/ppermute | solution.py:370
  50.0 14.5 %collective-permute-start.12 = (f32[2,536,128]{2,1,0:T(8,128)S(1)}, f32[2,536,128]{2,1,0:T(8,128)S(1)}, u32[]{:S(2)}, u32[]{:S(2)}) collective-permute-start(f32[2,536,128]{2,1,0:T(8,128)S(1)} %pad_maximum_fusion), channel_id=1, source_target_pairs={{0,2},{1,9},{8,10},{3,11},{16,18},{5,13},{24,26},{7,15},{2,0},{9,1... | collective-permute-start | bytes 1646600 | tf_op jit(solution)/shard_map/ppermute | solution.py:377
  60.3 11.4 %collective-permute-start.11 = (f32[2,512,128]{2,1,0:T(8,128)S(1)}, f32[2,512,128]{2,1,0:T(8,128)S(1)}, u32[]{:S(2)}, u32[]{:S(2)}) collective-permute-start(f32[2,512,128]{2,1,0:T(8,128)S(1)} %pad_maximum_fusion.1), channel_id=1, source_target_pairs={{2,4},{9,17},{10,12},{11,19},{18,20},{13,21},{26,28},{15,23},{4,2}... | collective-permute-start | bytes 1572872 | tf_op jit(solution)/shard_map/ppermute | solution.py:377
  64.6 10.1 %collective-permute-start.14 = (f32[1,536,128]{2,1,0:T(8,128)S(1)}, f32[1,536,128]{2,1,0:T(8,128)S(1)}, u32[]{:S(2)}, u32[]{:S(2)}) collective-permute-start(f32[1,536,128]{2,1,0:T(8,128)S(1)} %fusion.1), channel_id=1, source_target_pairs={{2,4},{9,17},{10,12},{11,19},{18,20},{13,21},{26,28},{15,23},{4,2}... | collective-permute-start | bytes 823304 | tf_op jit(solution)/shard_map/ppermute | solution.py:380
  71.7 6.5 %collective-permute-start.13 = (f32[1,512,128]{2,1,0:T(8,128)S(1)}, f32[1,512,128]{2,1,0:T(8,128)S(1)}, u32[]{:S(2)}, u32[]{:S(2)}) collective-permute-start(f32[1,512,128]{2,1,0:T(8,128)S(1)} %fusion.8), channel_id=1, source_target_pairs={{0,2},{1,9},{8,10},{3,11},{16,18},{5,13},{24,26},{7,15},{2,0},{9,1... | collective-permute-start | bytes 786440 | tf_op jit(solution)/shard_map/ppermute | solution.py:380
  74.7 9.3 %collective-permute-start.17 = (f32[536,128]{1,0:T(8,128)S(1)}, f32[536,128]{1,0:T(8,128)S(1)}, u32[]{:S(2)}, u32[]{:S(2)}) collective-permute-start(f32[536,128]{1,0:T(8,128)S(1)} %fusion.3), channel_id=1, source_target_pairs={{0,32},{2,34},{4,36},{6,38},{8,40},{10,42},{12,44},{14,46},{16,48}... | collective-permute-start | bytes 823304 | tf_op jit(solution)/shard_map/ppermute | solution.py:386
  78.2 8.9 %collective-permute-start.15 = (f32[512,128]{1,0:T(8,128)S(1)}, f32[512,128]{1,0:T(8,128)S(1)}, u32[]{:S(2)}, u32[]{:S(2)}) collective-permute-start(f32[512,128]{1,0:T(8,128)S(1)} %fusion.7), channel_id=1, source_target_pairs={{32,64},{34,66},{36,68},{38,70},{40,72},{42,74},{44,76},{46,78},{4... | collective-permute-start | bytes 786440 | tf_op jit(solution)/shard_map/ppermute | solution.py:386
  84.0 7.8 %collective-permute-start.18 = (f32[536,128]{1,0:T(8,128)S(1)}, f32[536,128]{1,0:T(8,128)S(1)}, u32[]{:S(2)}, u32[]{:S(2)}) collective-permute-start(f32[536,128]{1,0:T(8,128)S(1)} %add.103.var), channel_id=1, source_target_pairs={{32,64},{34,66},{36,68},{38,70},{40,72},{42,74},{44,76},{46,78},{4... | collective-permute-start | bytes 823304 | tf_op jit(solution)/shard_map/ppermute | solution.py:387
  87.1 6.5 %collective-permute-start.16 = (f32[512,128]{1,0:T(8,128)S(1)}, f32[512,128]{1,0:T(8,128)S(1)}, u32[]{:S(2)}, u32[]{:S(2)}) collective-permute-start(f32[512,128]{1,0:T(8,128)S(1)} %add.102.num), channel_id=1, source_target_pairs={{0,32},{2,34},{4,36},{6,38},{8,40},{10,42},{12,44},{14,46},{16,48}... | collective-permute-start | bytes 786440 | tf_op jit(solution)/shard_map/ppermute | solution.py:387
